TPU v7x, 32 devices: a whole 2x2x4 slice. The times are simulated.
32 devices in a mesh: row: 8 (over y, x, core), col: 4 (over z).
Axes of the slice: x: 2, y: 2, z: 4, core: 2. Of those that a mesh axis runs over, the one named last changes fastest.
Arguments:
- factor: bfloat16 [64, 16, 128, 128], P('row', 'col'), may hold values from -0.1796875 to 0.1796875
- inverse_pivot: float32 [64, 128], P('row'), may hold values from 0.5 to 2
- lower_rhs: float32 [16, 64, 128], P(None, 'col'), may hold values from -6 to 6
- upper_rhs: float32 [16, 64, 128], P(None, 'col'), may hold values from -6 to 6
- snode_of_block: int32 [64], replicated, may hold values from 0 to 15, as said below
- level_of_snode: int32 [16], replicated, may hold values from 0 to 5, as said below
- slot_columns: int32 [64, 16], P('row', 'col'), may hold values from 0 to 64, as said below
Outputs:
- lower_solution: float32 [16, 64, 128], P(None, 'row')
- upper_solution: float32 [16, 64, 128], P(None, 'row')
Inputs may be any that keep to these rules, and one draw needn't show every extreme that they name: `snode_of_block`: never falling along the blocks, starting at 0 and rising by at most one; every supernode covers an even number of blocks. `level_of_snode`: never falling along the supernodes, starting at 0 and rising by at most one; every level holds one or more supernodes, the top level exactly one, the last. `slot_columns`: the slots of process column c name distinct blocks J with J % 4 == c, or 64; every block row names its own block; a named J lies in the row's supernode or in one that is an ancestor or descendant of it in the elimination tree, in which every supernode below the top level has its parent one level up; some block row fills all 4 slots of some process column.
All inputs are finite; a program needn't handle non-finite values.
Results may differ from a plain program's by a relative error of at most 0.0059.
Values may be sent and summed in bfloat16 or wider, within the bound.
No kernel may reach another device: no remote copies, remote signals or barrier semaphores. Data moves between devices by JAX's collectives and lax.ppermute only.
A program may use at most 128 MiB of HBM per device.

v0:
```python
import jax
import jax.numpy as jnp
from jax import lax
from jax.sharding import PartitionSpec as P


def select_columns(lower_piece, upper_piece):
    row_count = lax.axis_size("row")
    col_count = lax.axis_size("col")
    group_count = row_count // col_count
    column = lax.axis_index("col")
    rows_here = lower_piece.shape[1]
    gathered = (
        lax.all_gather(lower_piece, "row", axis=1, tiled=True),
        lax.all_gather(upper_piece, "row", axis=1, tiled=True),
    )

    def select(values):
        reshaped = values.reshape(
            values.shape[0], group_count, col_count, rows_here, values.shape[2]
        )
        own_part = lax.dynamic_index_in_dim(reshaped, column, 2, keepdims=False)
        return jnp.transpose(own_part, (0, 2, 1, 3))

    lower_all = select(gathered[0])
    upper_all = select(gathered[1])
    rhs_count = lower_all.shape[0]
    block_width = lower_all.shape[3]
    return (
        lower_all.reshape(rhs_count, rows_here * group_count, block_width),
        upper_all.reshape(rhs_count, rows_here * group_count, block_width),
    )


def shards(
    factor, inverse_pivot, lower_rhs, upper_rhs, snode_of_block, level_of_snode, slot_columns
):
    row_count = lax.axis_size("row")
    col_count = lax.axis_size("col")
    row_index = lax.axis_index("row")
    col_index = lax.axis_index("col")
    rows_here = factor.shape[0]
    slots_here = factor.shape[1]
    block_size = factor.shape[2]
    cols_here = lower_rhs.shape[1]
    total_blocks = snode_of_block.shape[0]
    snode_count = level_of_snode.shape[0]
    levels_total = min(6, snode_count // 2)
    group_count = row_count // col_count
    onehot = snode_of_block[:, None] == jnp.arange(snode_count, dtype=jnp.int32)[None, :]
    levels = jnp.sum(jnp.where(onehot, level_of_snode[None, :], 0), axis=1)
    row_ids = jnp.arange(rows_here, dtype=jnp.int32) * row_count + row_index
    col_ids = jnp.arange(cols_here, dtype=jnp.int32) * col_count + col_index
    row_snode = jnp.take(snode_of_block, row_ids)
    row_level = jnp.take(levels, row_ids)
    col_level = jnp.take(levels, col_ids)
    valid = slot_columns < total_blocks
    safe = jnp.minimum(slot_columns, total_blocks - 1)
    slot_snode = jnp.take(snode_of_block, safe)
    slot_level = jnp.take(levels, safe)
    same_snode = row_snode[:, None] == slot_snode
    lower_mask = valid & jnp.where(
        same_snode, safe < row_ids[:, None], row_level[:, None] > slot_level
    )
    upper_mask = valid & jnp.where(
        same_snode, safe > row_ids[:, None], row_level[:, None] < slot_level
    )
    diagonal = valid & (safe == row_ids[:, None])
    local_cols = (safe // col_count).reshape(-1)
    inner_ids = jnp.arange(block_size, dtype=jnp.int32)
    strict_lower = inner_ids[None, :] < inner_ids[:, None]
    strict_upper = inner_ids[None, :] > inner_ids[:, None]
    lower_keep = jnp.where(
        diagonal[:, :, None, None], strict_lower[None, None], lower_mask[:, :, None, None]
    )
    upper_keep = jnp.where(
        diagonal[:, :, None, None], strict_upper[None, None], upper_mask[:, :, None, None]
    )
    zero_value = jnp.zeros((), factor.dtype)
    lower_op = jnp.where(lower_keep, factor, zero_value)
    upper_op = jnp.where(upper_keep, factor, zero_value)
    diag_weight = (row_index % col_count == col_index).astype(jnp.float32)
    diag_slot = row_index // col_count

    def diagonal_part(values):
        reshaped = values.reshape(values.shape[0], rows_here, group_count, block_size)
        return lax.dynamic_index_in_dim(reshaped, diag_slot, 2, keepdims=False).astype(jnp.float32)

    def picked(values):
        taken = jnp.take(values, local_cols, axis=1)
        return taken.reshape(values.shape[0], rows_here, slots_here, block_size)

    def products(lower_in, upper_in):
        lower_part = jnp.einsum(
            "kisb,isab->kia", picked(lower_in), lower_op, preferred_element_type=jnp.float32
        )
        upper_part = jnp.einsum(
            "kisb,isab->kia", picked(upper_in), upper_op, preferred_element_type=jnp.float32
        )
        lower_part = lower_part + diag_weight * diagonal_part(lower_in)
        upper_part = upper_part + diag_weight * inverse_pivot[None, :, :] * diagonal_part(upper_in)
        return lax.psum((lower_part, upper_part), "col")

    def spread(lower_piece, upper_piece):
        return select_columns(lower_piece, upper_piece)

    lower_res = lower_rhs
    upper_res = upper_rhs
    lower_sol = jnp.zeros((lower_rhs.shape[0], rows_here, block_size), jnp.float32)
    upper_sol = jnp.zeros((upper_rhs.shape[0], rows_here, block_size), jnp.float32)
    for level_step in range(levels_total):
        upper_level = levels_total - 1 - level_step
        lower_in = jnp.where((col_level == level_step)[None, :, None], lower_res, 0.0).astype(
            jnp.bfloat16
        )
        upper_in = jnp.where((col_level == upper_level)[None, :, None], upper_res, 0.0).astype(
            jnp.bfloat16
        )
        lower_sum, upper_sum = products(lower_in, upper_in)
        lower_new = jnp.where((row_level == level_step)[None, :, None], lower_sum, 0.0)
        upper_new = jnp.where((row_level == upper_level)[None, :, None], upper_sum, 0.0)
        lower_sol = lower_sol + lower_new
        upper_sol = upper_sol + upper_new
        if level_step + 1 < levels_total:
            lower_cols, upper_cols = spread(
                lower_new.astype(jnp.bfloat16), upper_new.astype(jnp.bfloat16)
            )
            lower_upd, upper_upd = products(lower_cols, upper_cols)
            lower_back = jnp.where((row_level > level_step)[None, :, None], lower_upd, 0.0).astype(
                jnp.bfloat16
            )
            upper_back = jnp.where((row_level < upper_level)[None, :, None], upper_upd, 0.0).astype(
                jnp.bfloat16
            )
            lower_moved, upper_moved = spread(lower_back, upper_back)
            lower_res = lower_res - lower_moved.astype(jnp.float32)
            upper_res = upper_res - upper_moved.astype(jnp.float32)
    return (lower_sol, upper_sol)


def solution(mesh):
    in_specs = (
        P("row", "col", None, None),
        P("row", None),
        P(None, "col", None),
        P(None, "col", None),
        P(),
        P(),
        P("row", "col"),
    )
    out_specs = (P(None, "row", None), P(None, "row", None))
    return jax.shard_map(shards, mesh=mesh, in_specs=in_specs, out_specs=out_specs, check_vma=False)
```

profile of v0, /device:TPU:0, one launch (start us, length us, event | category | flops | bytes accessed | tf_op | source)
XLA Modules:
  0.0 543.8 jit_solution(16155989096270582812)
XLA Ops:
  7.3 0.6 copy-done.14
  8.1 0.6 copy-done
  8.9 0.6 gather_fusion.2
  9.5 0.6 gather_fusion.1
  10.3 0.7 gather_fusion.4
  11.0 0.7 gather_fusion.3
  11.8 0.7 gather_fusion
  12.8 0.6 copy-done.2
  15.0 1.1 fusion.21
  16.1 1.1 fusion.10
  17.3 37.5 %all-reduce.33.cloned.1.call-done = (f32[16,8,128]{2,0,1:T(8,128)}, f32[16,8,128]{2,0,1:T(8,128)}) async-done(((f32[16,8,128]{2,0,1:T(8,128)}, f32[16,8,128]{2,0,1:T(8,128)}), (f32[16,8,128]{2,0,1:T(8,128)}, f32[16,8,128]{2,0,1:T(8,128)})) %all-reduce.33.cloned.1.call-update) | async-done | bytes 131088 | tf_op jit(solution)/shard_map/psum | solution.py:102
  54.8 0.9 select_convert_fusion.24
  55.7 9.2 %all_gather.70 = bf16[16,64,128]{2,0,1:T(8,128)(2,1)S(1)} all-gather(bf16[16,8,128]{2,0,1:T(8,128)(2,1)S(1)} %select_convert_fusion.24), channel_id=1, replica_groups=mesh['row'=8,'col'=4] {'row'}, dimensions={1}, use_global_device_ids=true | all-gather | bytes 294912 | tf_op jit(solution)/shard_map/all_gather | solution.py:15
  65.9 9.3 %all_gather.60 = bf16[16,64,128]{2,0,1:T(8,128)(2,1)S(1)} all-gather(bf16[16,8,128]{2,0,1:T(8,128)(2,1)S(1)} %select_convert_fusion.29), channel_id=1, replica_groups=mesh['row'=8,'col'=4] {'row'}, dimensions={1}, use_global_device_ids=true | all-gather | bytes 294912 | tf_op jit(solution)/shard_map/all_gather | solution.py:14
  76.8 20.2 %all-reduce.34 = (bf16[16,8,128]{2,0,1:T(8,128)(2,1)S(1)}, bf16[16,8,128]{2,0,1:T(8,128)(2,1)S(1)}) all-reduce(f32[16,8,128]{2,0,1:T(8,128)S(1)} %fusion.20, f32[16,8,128]{2,0,1:T(8,128)S(1)} %fusion.9), channel_id=1, replica_groups=mesh['row'=8,'col'=4] {'col'}, use_global_device_ids=true, to_apply=%region_2.6 | all-reduce | flops 32768 | bytes 196608 | tf_op jit(solution)/shard_map/psum | solution.py:102
  97.1 8.4 %all_gather.71 = bf16[16,64,128]{2,0,1:T(8,128)(2,1)S(1)} all-gather(bf16[16,8,128]{2,0,1:T(8,128)(2,1)S(1)} %select_convert_fusion.14), channel_id=1, replica_groups=mesh['row'=8,'col'=4] {'row'}, dimensions={1}, use_global_device_ids=true | all-gather | bytes 294912 | tf_op jit(solution)/shard_map/all_gather | solution.py:15
  106.2 9.3 %all_gather.61 = bf16[16,64,128]{2,0,1:T(8,128)(2,1)S(1)} all-gather(bf16[16,8,128]{2,0,1:T(8,128)(2,1)S(1)} %select_convert_fusion.19), channel_id=1, replica_groups=mesh['row'=8,'col'=4] {'row'}, dimensions={1}, use_global_device_ids=true | all-gather | bytes 294912 | tf_op jit(solution)/shard_map/all_gather | solution.py:14
  116.3 1.1 fusion.8
  117.4 1.1 fusion.19
  118.5 32.2 %all-reduce.31.cloned.1.call-done = (f32[16,8,128]{2,0,1:T(8,128)}, f32[16,8,128]{2,0,1:T(8,128)}) async-done(((f32[16,8,128]{2,0,1:T(8,128)}, f32[16,8,128]{2,0,1:T(8,128)}), (f32[16,8,128]{2,0,1:T(8,128)}, f32[16,8,128]{2,0,1:T(8,128)})) %all-reduce.31.cloned.1.call-update) | async-done | bytes 131088 | tf_op jit(solution)/shard_map/psum | solution.py:102
  150.8 0.9 select_convert_fusion.23
  151.7 9.2 %all_gather.72 = bf16[16,64,128]{2,0,1:T(8,128)(2,1)S(1)} all-gather(bf16[16,8,128]{2,0,1:T(8,128)(2,1)S(1)} %select_convert_fusion.23), channel_id=1, replica_groups=mesh['row'=8,'col'=4] {'row'}, dimensions={1}, use_global_device_ids=true | all-gather | bytes 294912 | tf_op jit(solution)/shard_map/all_gather | solution.py:15
  161.9 9.3 %all_gather.62 = bf16[16,64,128]{2,0,1:T(8,128)(2,1)S(1)} all-gather(bf16[16,8,128]{2,0,1:T(8,128)(2,1)S(1)} %select_convert_fusion.28), channel_id=1, replica_groups=mesh['row'=8,'col'=4] {'row'}, dimensions={1}, use_global_device_ids=true | all-gather | bytes 294912 | tf_op jit(solution)/shard_map/all_gather | solution.py:14
  172.8 20.2 %all-reduce.35 = (bf16[16,8,128]{2,0,1:T(8,128)(2,1)S(1)}, bf16[16,8,128]{2,0,1:T(8,128)(2,1)S(1)}) all-reduce(f32[16,8,128]{2,0,1:T(8,128)S(1)} %fusion.18, f32[16,8,128]{2,0,1:T(8,128)S(1)} %fusion.7), channel_id=1, replica_groups=mesh['row'=8,'col'=4] {'col'}, use_global_device_ids=true, to_apply=%region_4.8 | all-reduce | flops 32768 | bytes 196608 | tf_op jit(solution)/shard_map/psum | solution.py:102
  193.0 8.4 %all_gather.73 = bf16[16,64,128]{2,0,1:T(8,128)(2,1)S(1)} all-gather(bf16[16,8,128]{2,0,1:T(8,128)(2,1)S(1)} %select_convert_fusion.13), channel_id=1, replica_groups=mesh['row'=8,'col'=4] {'row'}, dimensions={1}, use_global_device_ids=true | all-gather | bytes 294912 | tf_op jit(solution)/shard_map/all_gather | solution.py:15
  202.2 9.4 %all_gather.63 = bf16[16,64,128]{2,0,1:T(8,128)(2,1)S(1)} all-gather(bf16[16,8,128]{2,0,1:T(8,128)(2,1)S(1)} %select_convert_fusion.18), channel_id=1, replica_groups=mesh['row'=8,'col'=4] {'row'}, dimensions={1}, use_global_device_ids=true | all-gather | bytes 294912 | tf_op jit(solution)/shard_map/all_gather | solution.py:14
  212.4 1.1 fusion.6
  213.5 1.1 fusion.17
  214.7 32.2 %all-reduce.29.cloned.1.call-done = (f32[16,8,128]{2,0,1:T(8,128)}, f32[16,8,128]{2,0,1:T(8,128)}) async-done(((f32[16,8,128]{2,0,1:T(8,128)}, f32[16,8,128]{2,0,1:T(8,128)}), (f32[16,8,128]{2,0,1:T(8,128)}, f32[16,8,128]{2,0,1:T(8,128)})) %all-reduce.29.cloned.1.call-update) | async-done | bytes 131088 | tf_op jit(solution)/shard_map/psum | solution.py:102
  246.9 0.9 select_convert_fusion.22
  247.9 9.2 %all_gather.74 = bf16[16,64,128]{2,0,1:T(8,128)(2,1)S(1)} all-gather(bf16[16,8,128]{2,0,1:T(8,128)(2,1)S(1)} %select_convert_fusion.22), channel_id=1, replica_groups=mesh['row'=8,'col'=4] {'row'}, dimensions={1}, use_global_device_ids=true | all-gather | bytes 294912 | tf_op jit(solution)/shard_map/all_gather | solution.py:15
  258.0 9.3 %all_gather.64 = bf16[16,64,128]{2,0,1:T(8,128)(2,1)S(1)} all-gather(bf16[16,8,128]{2,0,1:T(8,128)(2,1)S(1)} %select_convert_fusion.27), channel_id=1, replica_groups=mesh['row'=8,'col'=4] {'row'}, dimensions={1}, use_global_device_ids=true | all-gather | bytes 294912 | tf_op jit(solution)/shard_map/all_gather | solution.py:14
  268.9 20.2 %all-reduce.36 = (bf16[16,8,128]{2,0,1:T(8,128)(2,1)S(1)}, bf16[16,8,128]{2,0,1:T(8,128)(2,1)S(1)}) all-reduce(f32[16,8,128]{2,0,1:T(8,128)S(1)} %fusion.16, f32[16,8,128]{2,0,1:T(8,128)S(1)} %fusion.5), channel_id=1, replica_groups=mesh['row'=8,'col'=4] {'col'}, use_global_device_ids=true, to_apply=%region_6.10 | all-reduce | flops 32768 | bytes 196608 | tf_op jit(solution)/shard_map/psum | solution.py:102
  289.2 8.4 %all_gather.75 = bf16[16,64,128]{2,0,1:T(8,128)(2,1)S(1)} all-gather(bf16[16,8,128]{2,0,1:T(8,128)(2,1)S(1)} %select_convert_fusion.12), channel_id=1, replica_groups=mesh['row'=8,'col'=4] {'row'}, dimensions={1}, use_global_device_ids=true | all-gather | bytes 294912 | tf_op jit(solution)/shard_map/all_gather | solution.py:15
  298.4 9.3 %all_gather.65 = bf16[16,64,128]{2,0,1:T(8,128)(2,1)S(1)} all-gather(bf16[16,8,128]{2,0,1:T(8,128)(2,1)S(1)} %select_convert_fusion.17), channel_id=1, replica_groups=mesh['row'=8,'col'=4] {'row'}, dimensions={1}, use_global_device_ids=true | all-gather | bytes 294912 | tf_op jit(solution)/shard_map/all_gather | solution.py:14
  308.4 1.1 fusion.4
  309.5 1.1 fusion.15
  310.7 32.2 %all-reduce.27.cloned.1.call-done = (f32[16,8,128]{2,0,1:T(8,128)}, f32[16,8,128]{2,0,1:T(8,128)}) async-done(((f32[16,8,128]{2,0,1:T(8,128)}, f32[16,8,128]{2,0,1:T(8,128)}), (f32[16,8,128]{2,0,1:T(8,128)}, f32[16,8,128]{2,0,1:T(8,128)})) %all-reduce.27.cloned.1.call-update) | async-done | bytes 131088 | tf_op jit(solution)/shard_map/psum | solution.py:102
  342.9 0.9 select_convert_fusion.26
  344.0 9.2 %all_gather.76 = bf16[16,64,128]{2,0,1:T(8,128)(2,1)S(1)} all-gather(bf16[16,8,128]{2,0,1:T(8,128)(2,1)S(1)} %select_convert_fusion.21), channel_id=1, replica_groups=mesh['row'=8,'col'=4] {'row'}, dimensions={1}, use_global_device_ids=true | all-gather | bytes 294912 | tf_op jit(solution)/shard_map/all_gather | solution.py:15
  353.2 0.6 gather_fusion.23
  353.8 9.3 %all_gather.66 = bf16[16,64,128]{2,0,1:T(8,128)(2,1)S(1)} all-gather(bf16[16,8,128]{2,0,1:T(8,128)(2,1)S(1)} %select_convert_fusion.26), channel_id=1, replica_groups=mesh['row'=8,'col'=4] {'row'}, dimensions={1}, use_global_device_ids=true | all-gather | bytes 294912 | tf_op jit(solution)/shard_map/all_gather | solution.py:14
  363.1 0.6 gather_fusion.12
  364.7 20.2 %all-reduce.37 = (bf16[16,8,128]{2,0,1:T(8,128)(2,1)S(1)}, bf16[16,8,128]{2,0,1:T(8,128)(2,1)S(1)}) all-reduce(f32[16,8,128]{2,0,1:T(8,128)S(1)} %fusion.14, f32[16,8,128]{2,0,1:T(8,128)S(1)} %fusion.3), channel_id=1, replica_groups=mesh['row'=8,'col'=4] {'col'}, use_global_device_ids=true, to_apply=%region_8.12 | all-reduce | flops 32768 | bytes 196608 | tf_op jit(solution)/shard_map/psum | solution.py:102
  385.0 8.3 %all_gather.77 = bf16[16,64,128]{2,0,1:T(8,128)(2,1)S(1)} all-gather(bf16[16,8,128]{2,0,1:T(8,128)(2,1)S(1)} %select_convert_fusion.11), channel_id=1, replica_groups=mesh['row'=8,'col'=4] {'row'}, dimensions={1}, use_global_device_ids=true | all-gather | bytes 294912 | tf_op jit(solution)/shard_map/all_gather | solution.py:15
  393.5 0.6 gather_fusion.24
  394.2 9.3 %all_gather.67 = bf16[16,64,128]{2,0,1:T(8,128)(2,1)S(1)} all-gather(bf16[16,8,128]{2,0,1:T(8,128)(2,1)S(1)} %select_convert_fusion.16), channel_id=1, replica_groups=mesh['row'=8,'col'=4] {'row'}, dimensions={1}, use_global_device_ids=true | all-gather | bytes 294912 | tf_op jit(solution)/shard_map/all_gather | solution.py:14
  404.2 1.1 fusion.2
  405.3 1.1 fusion.13
  406.5 32.2 %all-reduce.25.cloned.1.call-done = (f32[16,8,128]{2,0,1:T(8,128)}, f32[16,8,128]{2,0,1:T(8,128)}) async-done(((f32[16,8,128]{2,0,1:T(8,128)}, f32[16,8,128]{2,0,1:T(8,128)}), (f32[16,8,128]{2,0,1:T(8,128)}, f32[16,8,128]{2,0,1:T(8,128)})) %all-reduce.25.cloned.1.call-update) | async-done | bytes 131088 | tf_op jit(solution)/shard_map/psum | solution.py:102
  438.7 0.9 select_convert_fusion.25
  439.8 9.5 %all_gather.78 = bf16[16,64,128]{2,0,1:T(8,128)(2,1)S(1)} all-gather(bf16[16,8,128]{2,0,1:T(8,128)(2,1)S(1)} %select_convert_fusion.20), channel_id=1, replica_groups=mesh['row'=8,'col'=4] {'row'}, dimensions={1}, use_global_device_ids=true | all-gather | bytes 294912 | tf_op jit(solution)/shard_map/all_gather | solution.py:15
  449.3 0.6 gather_fusion.25
  449.9 9.3 %all_gather.68 = bf16[16,64,128]{2,0,1:T(8,128)(2,1)S(1)} all-gather(bf16[16,8,128]{2,0,1:T(8,128)(2,1)S(1)} %select_convert_fusion.25), channel_id=1, replica_groups=mesh['row'=8,'col'=4] {'row'}, dimensions={1}, use_global_device_ids=true | all-gather | bytes 294912 | tf_op jit(solution)/shard_map/all_gather | solution.py:14
  459.1 0.6 gather_fusion.14
  460.8 20.2 %all-reduce.38 = (bf16[16,8,128]{2,0,1:T(8,128)(2,1)S(1)}, bf16[16,8,128]{2,0,1:T(8,128)(2,1)S(1)}) all-reduce(f32[16,8,128]{2,0,1:T(8,128)S(1)} %fusion.12, f32[16,8,128]{2,0,1:T(8,128)S(1)} %fusion.1), channel_id=1, replica_groups=mesh['row'=8,'col'=4] {'col'}, use_global_device_ids=true, to_apply=%region_10.14 | all-reduce | flops 32768 | bytes 196608 | tf_op jit(solution)/shard_map/psum | solution.py:102
  481.0 8.4 %all_gather.79 = bf16[16,64,128]{2,0,1:T(8,128)(2,1)S(1)} all-gather(bf16[16,8,128]{2,0,1:T(8,128)(2,1)S(1)} %select_convert_fusion.10), channel_id=1, replica_groups=mesh['row'=8,'col'=4] {'row'}, dimensions={1}, use_global_device_ids=true | all-gather | bytes 294912 | tf_op jit(solution)/shard_map/all_gather | solution.py:15
  489.5 9.3 %all_gather.69 = bf16[16,64,128]{2,0,1:T(8,128)(2,1)S(1)} all-gather(bf16[16,8,128]{2,0,1:T(8,128)(2,1)S(1)} %select_convert_fusion.15), channel_id=1, replica_groups=mesh['row'=8,'col'=4] {'row'}, dimensions={1}, use_global_device_ids=true | all-gather | bytes 294912 | tf_op jit(solution)/shard_map/all_gather | solution.py:14
  500.2 1.1 fusion
  501.3 1.1 fusion.11
  502.4 32.2 %all-reduce.23.cloned.1.call-done = (f32[16,8,128]{2,0,1:T(8,128)}, f32[16,8,128]{2,0,1:T(8,128)}) async-done(((f32[16,8,128]{2,0,1:T(8,128)}, f32[16,8,128]{2,0,1:T(8,128)}), (f32[16,8,128]{2,0,1:T(8,128)}, f32[16,8,128]{2,0,1:T(8,128)})) %all-reduce.23.cloned.1.call-update) | async-done | bytes 131088 | tf_op jit(solution)/shard_map/psum | solution.py:102
  534.6 1.0 select_add_fusion
  535.7 0.7 copy.214
  536.3 0.7 copy.213
  (162 shorter events, 20.1 us)
Async XLA Ops:
  7.2 47.6 %all-reduce.33.cloned.1.call-start = ((), (), s32[]{:S(2)}) async-start(), calls=%async_computation.5 | async-start | bytes 262144 | tf_op jit(solution)/shard_map/psum | solution.py:102
  7.2 0.7 copy-start.14
  8.1 0.7 copy-start
  8.1 0.7 copy-start.16
  11.0 4.0 copy-start.15
  11.8 0.9 copy-start.1
  12.5 0.9 copy-start.2
  14.1 0.7 copy-start.13
  17.2 133.6 %all-reduce.31.cloned.1.call-start = ((), (), s32[]{:S(2)}) async-start(), calls=%async_computation.4 | async-start | bytes 262144 | tf_op jit(solution)/shard_map/psum | solution.py:102
  65.0 0.8 copy-start.3
  118.5 128.4 %all-reduce.29.cloned.1.call-start = ((), (), s32[]{:S(2)}) async-start(), calls=%async_computation.3 | async-start | bytes 262144 | tf_op jit(solution)/shard_map/psum | solution.py:102
  160.9 0.8 copy-start.5
  214.7 128.3 %all-reduce.27.cloned.1.call-start = ((), (), s32[]{:S(2)}) async-start(), calls=%async_computation.2 | async-start | bytes 262144 | tf_op jit(solution)/shard_map/psum | solution.py:102
  257.1 0.8 copy-start.7
  310.7 128.1 %all-reduce.25.cloned.1.call-start = ((), (), s32[]{:S(2)}) async-start(), calls=%async_computation.1 | async-start | bytes 262144 | tf_op jit(solution)/shard_map/psum | solution.py:102
  342.9 1.0 copy-start.10
  406.5 128.2 %all-reduce.23.cloned.1.call-start = ((), (), s32[]{:S(2)}) async-start(), calls=%async_computation | async-start | bytes 262144 | tf_op jit(solution)/shard_map/psum | solution.py:102
  438.7 1.0 copy-start.12
  501.3 33.3 %copy-start.8 = (f32[16,8,128]{2,0,1:T(8,128)S(1)}, f32[16,8,128]{2,0,1:T(8,128)}, u32[]{:S(2)}) copy-start(f32[16,8,128]{2,0,1:T(8,128)} %get-tuple-element.32) | copy-start | bytes 196612
  501.3 33.3 %copy-start.9 = (f32[16,8,128]{2,0,1:T(8,128)S(1)}, f32[16,8,128]{2,0,1:T(8,128)}, u32[]{:S(2)}) copy-start(f32[16,8,128]{2,0,1:T(8,128)} %get-tuple-element.29) | copy-start | bytes 196612
  501.3 33.3 %copy-start.11 = (f32[16,8,128]{2,0,1:T(8,128)S(1)}, f32[16,8,128]{2,0,1:T(8,128)}, u32[]{:S(2)}) copy-start(f32[16,8,128]{2,0,1:T(8,128)} %get-tuple-element.27) | copy-start | bytes 196612
  502.4 32.2 %copy-start.4 = (f32[16,8,128]{2,0,1:T(8,128)S(1)}, f32[16,8,128]{2,0,1:T(8,128)}, u32[]{:S(2)}) copy-start(f32[16,8,128]{2,0,1:T(8,128)} %get-tuple-element.36) | copy-start | bytes 196612
  502.4 32.3 %copy-start.6 = (f32[16,8,128]{2,0,1:T(8,128)S(1)}, f32[16,8,128]{2,0,1:T(8,128)}, u32[]{:S(2)}) copy-start(f32[16,8,128]{2,0,1:T(8,128)} %get-tuple-element.34) | copy-start | bytes 196612
Sparse Core Ops, SparseCore 0:
  17.3 37.4 all-reduce.32
  118.6 32.0 all-reduce.30
  214.8 32.0 all-reduce.28
  310.8 32.0 all-reduce.26
  406.6 32.0 all-reduce.24
  502.5 32.0 all-reduce.22
where the time goes:
time: 545 us; the launch traced here: 544 us
  blocking collectives  282 us (52%)
  waiting for transfers between devices  199 us (37%)
  local copies, waits for them, and re-layouts  20.9 us (4%)
  matrix products  17.8 us (3%)
  between operations  14.8 us (3%)
  other arithmetic  9.37 us (2%)
    psum x6, waiting for transfers between devices, products(): return lax.psum((lower_part, upper_part), 'col')  199 us
    psum x5, blocking collectives, products(): return lax.psum((lower_part, upper_part), 'col')  101 us
    all_gather x10, blocking collectives, select_columns(): lax.all_gather(lower_piece, 'row', axis=1, tiled=True)  92.8 us
    all_gather x10, blocking collectives, select_columns(): lax.all_gather(upper_piece, 'row', axis=1, tiled=True)  88.2 us
    gather x22, local copies, waits for them, and re-layouts, picked(): taken = jnp.take(values, local_cols, axis=1)  13 us
  transfers between devices with their start and end apart: 6, of which 6 were waited for; matrix products, arithmetic and copies ran while one was open for 0% of the time, Pallas kernels for 0%

commit v1 on v0

v1 whole, which is shorter than its diff:
```python
import functools

import jax
import jax.numpy as jnp
from jax import lax
from jax.experimental import pallas as pl
from jax.experimental.pallas import tpu as pltpu
from jax.sharding import PartitionSpec as P


def xor_permute(value, axis, distance):
    size = lax.axis_size(axis)
    return lax.ppermute(value, axis, [(i, i ^ distance) for i in range(size)])


def bits_of(size):
    return [1 << b for b in range(size.bit_length() - 1)]


def gather_rows(factor):
    size = lax.axis_size("row")
    half = factor.shape[0] // 2
    pieces = {0: (factor[:half], factor[half:])}
    for k in range(2, size, 2):
        high = 1 << (k.bit_length() - 1)
        low = k & -k
        pieces[k] = (
            xor_permute(pieces[k ^ high][0], "row", high),
            xor_permute(pieces[k ^ low][1], "row", low),
        )
    for k in range(0, size, 2):
        pieces[k ^ 1] = tuple(xor_permute(part, "row", 1) for part in pieces[k])
    return [part for k in range(size) for part in pieces[k]]


def prepare_diagonal(scalars, dims, parts):
    rows, cols, groups, per_row, slots, block = dims
    half = per_row // 2

    def body(*refs):
        sc, slot_of = refs[0], refs[1]
        part_refs = refs[2:2 + 2 * rows]
        out = refs[2 + 2 * rows]
        here = sc[0]
        row_high = sc[1]
        op = sc[2]
        row_i = lax.broadcasted_iota(jnp.int32, (block, block), 0)
        col_i = lax.broadcasted_iota(jnp.int32, (block, block), 1)
        ahead = jnp.where(op == 0, row_i - col_i, col_i - row_i) > 0
        for k in range(rows):
            @pl.when(here == k % cols)
            def _(k=k):
                m = row_high ^ (k // cols)
                for i in range(per_row):
                    source = part_refs[2 * k + i // half]
                    s = slot_of[m * per_row + i]
                    value = source[i % half, s].astype(jnp.float32)
                    out[m, i] = jnp.where(ahead, value, 0.0).astype(out.dtype)

    vmem = pl.BlockSpec(memory_space=pltpu.VMEM)
    smem = pl.BlockSpec(memory_space=pltpu.SMEM)
    return pl.pallas_call(
        body,
        out_shape=jax.ShapeDtypeStruct((groups, per_row, block, block), parts[0].dtype),
        in_specs=[smem, smem] + [vmem] * len(parts),
        out_specs=vmem,
        name="prepare_diagonal",
    )(scalars[0], scalars[1], *parts)


def step_kernel(kind, step, dims, scalars, table, parts, diag, level, pivot, state, received):
    rows, cols, groups, per_row, slots, block, kept = dims
    half = per_row // 2
    lanes = groups * kept
    locals_here = per_row * groups
    flat = (per_row * lanes, block)
    tile = (per_row, lanes, block)

    def body(*refs):
        refs = list(refs)
        sc = refs.pop(0)
        idx = refs.pop(0)
        part_refs = [refs.pop(0) for _ in parts]
        diag_ref = refs.pop(0)
        level_ref = refs.pop(0)
        pivot_ref = refs.pop(0)
        res_ref = refs.pop(0)
        sol_ref = refs.pop(0)
        got = [refs.pop(0) for _ in received]
        if kind == "last":
            out_sol = refs.pop(0)
        else:
            sends = [refs.pop(0) for _ in range(cols)]
            out_state = refs.pop(0)
            xs, acc = refs
        lv = level_ref[...]
        res = res_ref[...]
        if got:
            total = got[0][...]
            for ref in got[1:]:
                total = total + ref[...].astype(jnp.float32)
        if kind in ("solved", "last"):
            rounded = res.astype(jnp.bfloat16).astype(jnp.float32)
            y = jnp.where(lv == step, total + pivot_ref[...] * rounded, 0.0)
            sol = sol_ref[...] + y
            if kind == "last":
                out_sol[...] = sol
                return
            out_state[...] = sol
            source = y
        elif kind == "updated":
            back = total.astype(jnp.bfloat16).astype(jnp.float32)
            res = jnp.where(lv > step, res - back, res)
            out_state[...] = res
            source = jnp.where(lv == step + 1, res, 0.0)
        else:
            out_state[...] = res
            source = jnp.where(lv == 0, res, 0.0)
        source = source.reshape(tile)
        lane_group = lax.broadcasted_iota(jnp.int32, (1, lanes, block), 1) // kept
        for shift in range(groups):
            moved = source
            if shift:
                moved = jnp.concatenate([source[:, lanes - shift * kept:], source[:, :lanes - shift * kept]], axis=1)
            for m in range(groups):
                mine = (m + groups - shift) % groups
                put = jnp.where(lane_group == m, moved, 0.0)
                for i in range(per_row):
                    xs[m, i * groups + mine] = put[i]
        for m in range(groups):
            xs[m, locals_here] = jnp.zeros((lanes, block), jnp.float32)
        acc[...] = jnp.zeros(acc.shape, jnp.float32)
        here = sc[0]
        row_high = sc[1]
        which = 3 + 4 * (step + (1 if kind == "updated" else 0)) + (2 if kind == "solved" else 0)
        low = sc[which]
        high = sc[which + 1]

        def contract(x, w):
            return lax.dot_general(
                x.astype(jnp.bfloat16), w, (((1,), (1,)), ((), ())), preferred_element_type=jnp.float32
            )

        def group(i, part):
            for kk in range(cols):
                value = None
                for mm in range(groups):
                    k = kk + cols * mm
                    m = row_high ^ mm
                    for s in range(slots):
                        j = idx[(k * per_row + i) * slots + s]
                        term = contract(xs[m, j], part_refs[2 * k + part][i - part * half, s])
                        value = term if value is None else value + term
                acc[here ^ kk, i] = value
            own = acc[0, i]
            for m in range(groups):
                own = own + contract(xs[m, i * groups + m], diag_ref[m, i])
            acc[0, i] = own

        for part in range(2):
            begin = jnp.maximum(low, part * half)
            end = jnp.minimum(high, (part + 1) * half)

            def loop(i, carry, part=part):
                group(i, part)
                return carry

            lax.fori_loop(begin, end, loop, 0)
        sends[0][...] = acc[0].reshape(flat)
        for d in range(1, cols):
            sends[d][...] = acc[d].reshape(flat).astype(sends[d].dtype)

    vmem = pl.BlockSpec(memory_space=pltpu.VMEM)
    smem = pl.BlockSpec(memory_space=pltpu.SMEM)
    args = [scalars, table, *parts, diag, level, pivot, *state, *received]
    if kind == "last":
        out_shape = jax.ShapeDtypeStruct(flat, jnp.float32)
        out_specs = vmem
        scratch = []
    else:
        out_shape = (
            [jax.ShapeDtypeStruct(flat, jnp.float32)]
            + [jax.ShapeDtypeStruct(flat, jnp.bfloat16)] * (cols - 1)
            + [jax.ShapeDtypeStruct(flat, jnp.float32)]
        )
        out_specs = [vmem] * (cols + 1)
        scratch = [
            pltpu.VMEM((groups, locals_here + 1, lanes, block), jnp.float32),
            pltpu.VMEM((cols, per_row, lanes, block), jnp.float32),
        ]
    return pl.pallas_call(
        body,
        out_shape=out_shape,
        in_specs=[smem, smem] + [vmem] * (len(args) - 2),
        out_specs=out_specs,
        scratch_shapes=scratch,
        name="step_" + kind,
    )(*args)


def shards(
    factor, inverse_pivot, lower_rhs, upper_rhs, snode_of_block, level_of_snode, slot_columns
):
    rows = lax.axis_size("row")
    cols = lax.axis_size("col")
    r = lax.axis_index("row")
    c = lax.axis_index("col")
    per_row, slots, block = factor.shape[:3]
    total = snode_of_block.shape[0]
    snodes = level_of_snode.shape[0]
    rhs_count = lower_rhs.shape[0]
    steps = min(6, snodes // 2)
    groups = rows // cols
    kept = 2 * rhs_count // rows
    locals_here = per_row * groups
    lanes = groups * kept
    op = r % 2
    dims = (rows, cols, groups, per_row, slots, block)

    small = jnp.concatenate(
        [inverse_pivot, jnp.pad(slot_columns.astype(jnp.float32), ((0, 0), (0, block - slots)))], axis=1
    )[None]
    for bit in bits_of(rows):
        small = jnp.concatenate([small, xor_permute(small, "row", bit)], axis=0)
    parts = gather_rows(factor)

    blocks = jnp.arange(total, dtype=jnp.int32)
    onehot = snode_of_block[:, None] == jnp.arange(snodes, dtype=jnp.int32)[None, :]
    levels = jnp.sum(jnp.where(onehot, level_of_snode[None, :], 0), axis=1)
    levels = jnp.where(op == 0, levels, steps - 1 - levels)

    def look_up(values, index):
        return jnp.sum(jnp.where(index[..., None] == blocks, values, 0), axis=-1)

    slot_ids = small[:, :, block:block + slots].astype(jnp.int32)
    row_class = jnp.arange(rows, dtype=jnp.int32) ^ r
    row_ids = jnp.arange(per_row, dtype=jnp.int32)[None, :] * rows + row_class[:, None]
    valid = slot_ids < total
    slot_snode = look_up(snode_of_block, slot_ids)
    slot_level = look_up(levels, slot_ids)
    row_snode = look_up(snode_of_block, row_ids)[..., None]
    row_level = look_up(levels, row_ids)[..., None]
    before = jnp.where(op == 0, row_ids[..., None] - slot_ids, slot_ids - row_ids[..., None]) > 0
    active = valid & jnp.where(slot_snode == row_snode, before, row_level > slot_level)
    table = jnp.where(active, slot_ids // cols, locals_here).reshape(-1)

    own_k = (c + cols * jnp.arange(groups, dtype=jnp.int32)) ^ r
    own_small = jnp.take(small, own_k, axis=0)
    own_ids = jnp.arange(per_row, dtype=jnp.int32)[None, :] * rows + c + cols * jnp.arange(groups)[:, None]
    own_slots = own_small[:, :, block:block + slots].astype(jnp.int32)
    slot_of = jnp.sum(
        jnp.where(own_slots == own_ids[..., None], jnp.arange(slots, dtype=jnp.int32), 0), axis=-1
    ).reshape(-1)

    def lay(values):
        shape = (per_row, groups, kept, block)
        return jnp.broadcast_to(values.transpose(1, 0, 2)[:, :, None], shape).reshape(-1, block)

    pivot = lay(jnp.where(op == 0, 1.0, own_small[:, :, :block]))
    level = lay(jnp.broadcast_to(look_up(levels, own_ids)[..., None], (groups, per_row, block)))

    step_ids = jnp.arange(steps, dtype=jnp.int32)
    at = jnp.sum((levels[None, :] == step_ids[:, None]).astype(jnp.int32), axis=1)
    upto = jnp.sum((levels[None, :] <= step_ids[:, None]).astype(jnp.int32), axis=1)
    solve_low = jnp.where(op == 0, upto - at, total - upto)
    solve_high = solve_low + at
    update_low = jnp.where(op == 0, upto, 0)
    update_high = jnp.where(op == 0, total, total - upto)
    bounds = jnp.stack(
        [
            solve_low // rows,
            (solve_high + rows - 1) // rows,
            update_low // rows,
            (update_high + rows - 1) // rows,
        ],
        axis=1,
    ).reshape(-1)
    scalars = jnp.concatenate([jnp.stack([(r % cols) ^ c, r // cols, op]), bounds]).astype(jnp.int32)

    chosen = jnp.where(op == 0, lower_rhs, upper_rhs)
    chosen = lax.dynamic_slice_in_dim(chosen, (r // 2) * kept, kept, 0)
    chosen = chosen.reshape(kept, per_row, groups, block).transpose(1, 2, 0, 3).reshape(-1, block)

    diag = prepare_diagonal((scalars, slot_of), dims, parts)
    run = functools.partial(
        step_kernel,
        dims=dims + (kept,),
        scalars=scalars,
        table=table,
        parts=parts,
        diag=diag,
        level=level,
        pivot=pivot,
    )

    def exchange(sends):
        return [sends[0]] + [xor_permute(sends[d], "col", d) for d in range(1, cols)]

    res = chosen
    sol = jnp.zeros(chosen.shape, jnp.float32)
    *sends, res = run("first", 0, state=(res, sol), received=[])
    for step in range(steps - 1):
        *sends, sol = run("solved", step, state=(res, sol), received=exchange(sends))
        *sends, res = run("updated", step, state=(res, sol), received=exchange(sends))
    sol = run("last", steps - 1, state=(res, sol), received=exchange(sends))

    whole = jnp.stack([sol] + [xor_permute(sol, "col", d) for d in range(1, cols)])
    for bit in bits_of(cols):
        paired = whole.reshape(cols // (2 * bit), 2, bit, *sol.shape)
        whole = jnp.where((c & bit) != 0, paired[:, ::-1], paired).reshape(cols, *sol.shape)
    whole = whole.reshape(cols, per_row, groups, kept, block).transpose(2, 0, 1, 3, 4)
    whole = whole.reshape(rows, per_row * kept, block)
    got = lax.all_to_all(whole, "row", 0, 0).reshape(rows // 2, 2, per_row, kept, block)
    got = got.transpose(1, 0, 3, 2, 4).reshape(2, rhs_count, per_row, block)
    return got[0], got[1]


def solution(mesh):
    in_specs = (
        P("row", "col", None, None),
        P("row", None),
        P(None, "col", None),
        P(None, "col", None),
        P(),
        P(),
        P("row", "col"),
    )
    out_specs = (P(None, "row", None), P(None, "row", None))
    return jax.shard_map(shards, mesh=mesh, in_specs=in_specs, out_specs=out_specs, check_vma=False)
```

time: 545 us -> 248 us (0.46)
  blocking collectives: 282 us -> 8.08 us
  waiting for transfers between devices: 199 us -> 75.1 us
  Pallas kernels: 0 us -> 79.9 us
  starting transfers between devices: 0.25 us -> 67.3 us
  matrix products: 17.8 us -> 0 us
  between operations: 14.8 us -> 1.1 us
  local copies, waits for them, and re-layouts: 20.9 us -> 14.9 us
    psum x6 -> x0, waiting for transfers between devices: 199 us -> none  [products(): return lax.psum((lower_part, upper_part), 'col')]
    all_gather x20 -> x0, blocking collectives: 181 us -> none  [the longest x10 92.8 us: select_columns(): lax.all_gather(lower_piece, 'row', axis=1, tiled=True)]
    psum x5 -> x0, blocking collectives: 101 us -> none  [products(): return lax.psum((lower_part, upper_part), 'col')]
    pallas_call x0 -> x13, Pallas kernels: none -> 79.9 us  [the longest x12 75.5 us: step_kernel(): pl.pallas_call(body, out_shape=out_shape, in_specs=[smem, smem] + [vmem]...]
    ppermute x0 -> x53, waiting for transfers between devices: none -> 75.1 us  [xor_permute(): return lax.ppermute(value, axis, [(i, i ^ distance) for i in range(size)])]
    ppermute x0 -> x53, starting transfers between devices: none -> 67.3 us  [xor_permute(): return lax.ppermute(value, axis, [(i, i ^ distance) for i in range(size)])]
    dot_general x22 -> x0, matrix products: 17.8 us -> none  [the longest x11 8.93 us: products(): jnp.einsum('kisb,isab->kia', picked(lower_in), lower_op, preferred_elemen...]
    gather x29 -> x1, local copies, waits for them, and re-layouts: 16.5 us -> 0.55 us  [shards(): own_small = jnp.take(small, own_k, axis=0)]
  transfers between devices with their start and end apart: 6 -> 53, of which waited for: 6 -> 28; matrix products, arithmetic and copies ran while one was open for 0% -> 3% of each run, Pallas kernels for 0% -> 0%
where the time goes in v1:
time: 248 us; the launch traced here: 251 us
  Pallas kernels  79.9 us (32%)
  waiting for transfers between devices  75.1 us (30%)
  starting transfers between devices  67.3 us (27%)
  local copies, waits for them, and re-layouts  14.9 us (6%)
  blocking collectives  8.08 us (3%)
  other arithmetic  4.88 us (2%)
    pallas_call x12, Pallas kernels, step_kernel(): pl.pallas_call(body, out_shape=out_shape, in_specs=[smem, smem] + [vmem]...  75.5 us
    ppermute x53, waiting for transfers between devices, xor_permute(): return lax.ppermute(value, axis, [(i, i ^ distance) for i in range(size)])  75.1 us
    ppermute x53, starting transfers between devices, xor_permute(): return lax.ppermute(value, axis, [(i, i ^ distance) for i in range(size)])  67.3 us
    all_to_all x1, blocking collectives, shards(): lax.all_to_all(whole, 'row', 0, 0)  8.08 us
    unnamed x88, local copies, waits for them, and re-layouts  7.57 us
  transfers between devices with their start and end apart: 53, of which 28 were waited for; matrix products, arithmetic and copies ran while one was open for 3% of the time, Pallas kernels for 0%

profile of v1, /device:TPU:0, one launch (start us, length us, event | category | flops | bytes accessed | tf_op | source)
XLA Modules:
  0.0 251.2 jit_solution(7875208660945069684)
XLA Ops:
  0.6 1.3 fusion.11
  1.9 3.0 %collective-permute-start.5 = (bf16[4,4,128,128]{3,2,1,0:T(8,128)(2,1)S(1)}, bf16[4,4,128,128]{3,2,1,0:T(8,128)(2,1)S(1)}, u32[]{:S(2)}, u32[]{:S(2)}) collective-permute-start(bf16[4,4,128,128]{3,2,1,0:T(8,128)(2,1)S(1)} %get-tuple-element.119.refs_2_), channel_id=1, source_target_pairs={{0,8},{4,12},{8,0},{12,4},{16,24},{20,28},{24,16},{28,20},{1,9},{5... | collective-permute-start | bytes 1572872 | tf_op jit(solution)/shard_map/ppermute | solution.py:13
  5.0 1.5 collective-permute-start.9
  9.2 0.8 dynamic-slice_select_fusion
  10.0 2.0 collective-permute-start.1
  12.0 16.4 %collective-permute-done.1 = f32[2,8,256]{2,1,0:T(8,128)S(1)} collective-permute-done((f32[2,8,256]{2,1,0:T(8,128)S(1)}, f32[2,8,256]{2,1,0:T(8,128)S(1)}, u32[]{:S(2)}, u32[]{:S(2)}) %collective-permute-start.1) | collective-permute-done | bytes 16416 | tf_op jit(solution)/shard_map/ppermute | solution.py:13
  28.5 1.8 collective-permute-start.2
  31.1 1.3 collective-permute-done.2
  32.9 1.7 collective-permute-start.14
  34.7 1.6 collective-permute-start.13
  39.0 10.1 %collective-permute-done.13.refs_14_ = bf16[4,4,128,128]{3,2,1,0:T(8,128)(2,1)} collective-permute-done((bf16[4,4,128,128]{3,2,1,0:T(8,128)(2,1)S(1)}, bf16[4,4,128,128]{3,2,1,0:T(8,128)(2,1)}, u32[]{:S(2)}, u32[]{:S(2)}) %collective-permute-start.13) | collective-permute-done | bytes 524320 | tf_op jit(solution)/shard_map/ppermute | solution.py:13
  49.7 1.3 select_reduce_fusion.1
  52.7 4.3 %prepare_diagonal.1.refs_18_ = bf16[2,8,128,128]{3,2,1,0:T(8,128)(2,1)} custom-call(s32[27]{0:T(128)} %pad_add_fusion.1.refs_0_, s32[16]{0:T(128)} %reshape.377.refs_1_, bf16[4,4,128,128]{3,2,1,0:T(8,128)(2,1)} %copy-done.1, bf16[4,4,128,128]{3,2,1,0:T(8,128)(2,1)} %copy-done, bf16[4,4,128,128]{3,2,1,0:T(8,128)(2,1)} %collective-permute-done.3.refs_4_, ...), custom_call_target="tpu_custom_call" | custom-call | tf_op jit(solution)/shard_map/prepare_diagonal/pallas_call | solution.py:62
  58.9 5.6 %step_first.1 = (f32[64,128]{1,0:T(8,128)}, bf16[64,128]{1,0:T(8,128)(2,1)}, bf16[64,128]{1,0:T(8,128)(2,1)}, bf16[64,128]{1,0:T(8,128)(2,1)}, f32[64,128]{1,0:T(8,128)}) custom-call(s32[27]{0:T(128)} %pad_add_fusion.1.refs_0_, s32[256]{0:T(256)} %reshape.376.refs_1_, bf16[4,4,128,128]{3,2,1,0:T(8,128)(2,1)} %copy-done.1, bf16[4,4,128,128]{3,2,1,0:T(8,128)(2,1)} %copy-done, ...), custom_call_target="tpu_custom_call" | custom-call | tf_op jit(solution)/shard_map/step_first/pallas_call | solution.py:191
  64.5 1.6 collective-permute-start.17
  66.2 2.6 %collective-permute-start.18 = (bf16[64,128]{1,0:T(8,128)(2,1)}, bf16[64,128]{1,0:T(8,128)(2,1)S(1)}, u32[]{:S(2)}, u32[]{:S(2)}) collective-permute-start(bf16[64,128]{1,0:T(8,128)(2,1)} %get-tuple-element.60), channel_id=1, source_target_pairs={{0,2},{1,3},{2,0},{3,1},{4,6},{5,7},{6,4},{7,5},{8,10},{9,11},{10,... | collective-permute-start | bytes 49160 | tf_op jit(solution)/shard_map/ppermute | solution.py:13
  69.0 2.1 collective-permute-done.18.refs_25_
  71.1 3.4 %collective-permute-done.19.refs_26_ = bf16[64,128]{1,0:T(8,128)(2,1)S(1)} collective-permute-done((bf16[64,128]{1,0:T(8,128)(2,1)}, bf16[64,128]{1,0:T(8,128)(2,1)S(1)}, u32[]{:S(2)}, u32[]{:S(2)}) %collective-permute-start.19) | collective-permute-done | bytes 16416 | tf_op jit(solution)/shard_map/ppermute | solution.py:13
  75.1 9.1 %step_solved.5 = (f32[64,128]{1,0:T(8,128)}, bf16[64,128]{1,0:T(8,128)(2,1)}, bf16[64,128]{1,0:T(8,128)(2,1)}, bf16[64,128]{1,0:T(8,128)(2,1)}, f32[64,128]{1,0:T(8,128)}) custom-call(s32[27]{0:T(128)} %pad_add_fusion.1.refs_0_, s32[256]{0:T(256)} %reshape.376.refs_1_, bf16[4,4,128,128]{3,2,1,0:T(8,128)(2,1)} %copy-done.1, bf16[4,4,128,128]{3,2,1,0:T(8,128)(2,1)} %copy-done, ...), custom_call_target="tpu_custom_call" | custom-call | tf_op jit(solution)/shard_map/step_solved/pallas_call | solution.py:191
  84.3 0.8 collective-permute-start.21
  85.1 3.6 %collective-permute-start.22 = (bf16[64,128]{1,0:T(8,128)(2,1)}, bf16[64,128]{1,0:T(8,128)(2,1)S(1)}, u32[]{:S(2)}, u32[]{:S(2)}) collective-permute-start(bf16[64,128]{1,0:T(8,128)(2,1)} %get-tuple-element.66), channel_id=1, source_target_pairs={{0,3},{1,2},{2,1},{3,0},{4,7},{5,6},{6,5},{7,4},{8,11},{9,10},{10,... | collective-permute-start | bytes 49160 | tf_op jit(solution)/shard_map/ppermute | solution.py:13
  89.2 1.6 collective-permute-done.22.refs_26_
  91.4 5.6 %step_updated.5 = (f32[64,128]{1,0:T(8,128)}, bf16[64,128]{1,0:T(8,128)(2,1)}, bf16[64,128]{1,0:T(8,128)(2,1)}, bf16[64,128]{1,0:T(8,128)(2,1)}, f32[64,128]{1,0:T(8,128)}) custom-call(s32[27]{0:T(128)} %pad_add_fusion.1.refs_0_, s32[256]{0:T(256)} %reshape.376.refs_1_, bf16[4,4,128,128]{3,2,1,0:T(8,128)(2,1)} %copy-done.1, ...), custom_call_target="tpu_custom_call" | custom-call | tf_op jit(solution)/shard_map/step_updated/pallas_call | solution.py:191
  97.5 3.8 %collective-permute-start.24 = (bf16[64,128]{1,0:T(8,128)(2,1)}, bf16[64,128]{1,0:T(8,128)(2,1)S(1)}, u32[]{:S(2)}, u32[]{:S(2)}) collective-permute-start(bf16[64,128]{1,0:T(8,128)(2,1)} %get-tuple-element.70), channel_id=1, source_target_pairs={{0,2},{1,3},{2,0},{3,1},{4,6},{5,7},{6,4},{7,5},{8,10},{9,11},{10,... | collective-permute-start | bytes 49160 | tf_op jit(solution)/shard_map/ppermute | solution.py:13
  101.6 1.7 collective-permute-done.24.refs_25_
  103.2 3.8 %collective-permute-done.25.refs_26_ = bf16[64,128]{1,0:T(8,128)(2,1)S(1)} collective-permute-done((bf16[64,128]{1,0:T(8,128)(2,1)}, bf16[64,128]{1,0:T(8,128)(2,1)S(1)}, u32[]{:S(2)}, u32[]{:S(2)}) %collective-permute-start.25) | collective-permute-done | bytes 16416 | tf_op jit(solution)/shard_map/ppermute | solution.py:13
  107.7 8.4 %step_solved.6 = (f32[64,128]{1,0:T(8,128)}, bf16[64,128]{1,0:T(8,128)(2,1)}, bf16[64,128]{1,0:T(8,128)(2,1)}, bf16[64,128]{1,0:T(8,128)(2,1)}, f32[64,128]{1,0:T(8,128)}) custom-call(s32[27]{0:T(128)} %pad_add_fusion.1.refs_0_, s32[256]{0:T(256)} %reshape.376.refs_1_, bf16[4,4,128,128]{3,2,1,0:T(8,128)(2,1)} %copy-done.1, bf16[4,4,128,128]{3,2,1,0:T(8,128)(2,1)} %copy-done, ...), custom_call_target="tpu_custom_call" | custom-call | tf_op jit(solution)/shard_map/step_solved/pallas_call | solution.py:191
  116.2 0.8 collective-permute-start.27
  117.0 3.6 %collective-permute-start.28 = (bf16[64,128]{1,0:T(8,128)(2,1)}, bf16[64,128]{1,0:T(8,128)(2,1)S(1)}, u32[]{:S(2)}, u32[]{:S(2)}) collective-permute-start(bf16[64,128]{1,0:T(8,128)(2,1)} %get-tuple-element.76), channel_id=1, source_target_pairs={{0,3},{1,2},{2,1},{3,0},{4,7},{5,6},{6,5},{7,4},{8,11},{9,10},{10,... | collective-permute-start | bytes 49160 | tf_op jit(solution)/shard_map/ppermute | solution.py:13
  121.1 1.6 collective-permute-done.28.refs_26_
  123.3 5.7 %step_updated.6 = (f32[64,128]{1,0:T(8,128)}, bf16[64,128]{1,0:T(8,128)(2,1)}, bf16[64,128]{1,0:T(8,128)(2,1)}, bf16[64,128]{1,0:T(8,128)(2,1)}, f32[64,128]{1,0:T(8,128)}) custom-call(s32[27]{0:T(128)} %pad_add_fusion.1.refs_0_, s32[256]{0:T(256)} %reshape.376.refs_1_, bf16[4,4,128,128]{3,2,1,0:T(8,128)(2,1)} %copy-done.1, ...), custom_call_target="tpu_custom_call" | custom-call | tf_op jit(solution)/shard_map/step_updated/pallas_call | solution.py:191
  129.4 3.8 %collective-permute-start.30 = (bf16[64,128]{1,0:T(8,128)(2,1)}, bf16[64,128]{1,0:T(8,128)(2,1)S(1)}, u32[]{:S(2)}, u32[]{:S(2)}) collective-permute-start(bf16[64,128]{1,0:T(8,128)(2,1)} %get-tuple-element.80), channel_id=1, source_target_pairs={{0,2},{1,3},{2,0},{3,1},{4,6},{5,7},{6,4},{7,5},{8,10},{9,11},{10,... | collective-permute-start | bytes 49160 | tf_op jit(solution)/shard_map/ppermute | solution.py:13
  133.5 1.7 collective-permute-done.30.refs_25_
  135.2 3.8 %collective-permute-done.31.refs_26_ = bf16[64,128]{1,0:T(8,128)(2,1)S(1)} collective-permute-done((bf16[64,128]{1,0:T(8,128)(2,1)}, bf16[64,128]{1,0:T(8,128)(2,1)S(1)}, u32[]{:S(2)}, u32[]{:S(2)}) %collective-permute-start.31) | collective-permute-done | bytes 16416 | tf_op jit(solution)/shard_map/ppermute | solution.py:13
  139.6 7.7 %step_solved.7 = (f32[64,128]{1,0:T(8,128)}, bf16[64,128]{1,0:T(8,128)(2,1)}, bf16[64,128]{1,0:T(8,128)(2,1)}, bf16[64,128]{1,0:T(8,128)(2,1)}, f32[64,128]{1,0:T(8,128)}) custom-call(s32[27]{0:T(128)} %pad_add_fusion.1.refs_0_, s32[256]{0:T(256)} %reshape.376.refs_1_, bf16[4,4,128,128]{3,2,1,0:T(8,128)(2,1)} %copy-done.1, bf16[4,4,128,128]{3,2,1,0:T(8,128)(2,1)} %copy-done, ...), custom_call_target="tpu_custom_call" | custom-call | tf_op jit(solution)/shard_map/step_solved/pallas_call | solution.py:191
  147.4 0.8 collective-permute-start.33
  148.2 3.6 %collective-permute-start.34 = (bf16[64,128]{1,0:T(8,128)(2,1)}, bf16[64,128]{1,0:T(8,128)(2,1)S(1)}, u32[]{:S(2)}, u32[]{:S(2)}) collective-permute-start(bf16[64,128]{1,0:T(8,128)(2,1)} %get-tuple-element.86), channel_id=1, source_target_pairs={{0,3},{1,2},{2,1},{3,0},{4,7},{5,6},{6,5},{7,4},{8,11},{9,10},{10,... | collective-permute-start | bytes 49160 | tf_op jit(solution)/shard_map/ppermute | solution.py:13
  152.3 1.6 collective-permute-done.34.refs_26_
  154.6 6.4 %step_updated.7 = (f32[64,128]{1,0:T(8,128)}, bf16[64,128]{1,0:T(8,128)(2,1)}, bf16[64,128]{1,0:T(8,128)(2,1)}, bf16[64,128]{1,0:T(8,128)(2,1)}, f32[64,128]{1,0:T(8,128)}) custom-call(s32[27]{0:T(128)} %pad_add_fusion.1.refs_0_, s32[256]{0:T(256)} %reshape.376.refs_1_, bf16[4,4,128,128]{3,2,1,0:T(8,128)(2,1)} %copy-done.1, ...), custom_call_target="tpu_custom_call" | custom-call | tf_op jit(solution)/shard_map/step_updated/pallas_call | solution.py:191
  161.3 3.9 %collective-permute-start.36 = (bf16[64,128]{1,0:T(8,128)(2,1)}, bf16[64,128]{1,0:T(8,128)(2,1)S(1)}, u32[]{:S(2)}, u32[]{:S(2)}) collective-permute-start(bf16[64,128]{1,0:T(8,128)(2,1)} %get-tuple-element.90), channel_id=1, source_target_pairs={{0,2},{1,3},{2,0},{3,1},{4,6},{5,7},{6,4},{7,5},{8,10},{9,11},{10,... | collective-permute-start | bytes 49160 | tf_op jit(solution)/shard_map/ppermute | solution.py:13
  165.4 1.8 collective-permute-done.36.refs_25_
  167.2 3.8 %collective-permute-done.37.refs_26_ = bf16[64,128]{1,0:T(8,128)(2,1)S(1)} collective-permute-done((bf16[64,128]{1,0:T(8,128)(2,1)}, bf16[64,128]{1,0:T(8,128)(2,1)S(1)}, u32[]{:S(2)}, u32[]{:S(2)}) %collective-permute-start.37) | collective-permute-done | bytes 16416 | tf_op jit(solution)/shard_map/ppermute | solution.py:13
  171.6 6.4 %step_solved.8 = (f32[64,128]{1,0:T(8,128)}, bf16[64,128]{1,0:T(8,128)(2,1)}, bf16[64,128]{1,0:T(8,128)(2,1)}, bf16[64,128]{1,0:T(8,128)(2,1)}, f32[64,128]{1,0:T(8,128)}) custom-call(s32[27]{0:T(128)} %pad_add_fusion.1.refs_0_, s32[256]{0:T(256)} %reshape.376.refs_1_, bf16[4,4,128,128]{3,2,1,0:T(8,128)(2,1)} %copy-done.1, bf16[4,4,128,128]{3,2,1,0:T(8,128)(2,1)} %copy-done, ...), custom_call_target="tpu_custom_call" | custom-call | tf_op jit(solution)/shard_map/step_solved/pallas_call | solution.py:191
  178.1 0.8 collective-permute-start.39
  178.9 3.6 %collective-permute-start.40 = (bf16[64,128]{1,0:T(8,128)(2,1)}, bf16[64,128]{1,0:T(8,128)(2,1)S(1)}, u32[]{:S(2)}, u32[]{:S(2)}) collective-permute-start(bf16[64,128]{1,0:T(8,128)(2,1)} %get-tuple-element.96), channel_id=1, source_target_pairs={{0,3},{1,2},{2,1},{3,0},{4,7},{5,6},{6,5},{7,4},{8,11},{9,10},{10,... | collective-permute-start | bytes 49160 | tf_op jit(solution)/shard_map/ppermute | solution.py:13
  183.0 1.6 collective-permute-done.40.refs_26_
  185.3 6.3 %step_updated.8 = (f32[64,128]{1,0:T(8,128)}, bf16[64,128]{1,0:T(8,128)(2,1)}, bf16[64,128]{1,0:T(8,128)(2,1)}, bf16[64,128]{1,0:T(8,128)(2,1)}, f32[64,128]{1,0:T(8,128)}) custom-call(s32[27]{0:T(128)} %pad_add_fusion.1.refs_0_, s32[256]{0:T(256)} %reshape.376.refs_1_, bf16[4,4,128,128]{3,2,1,0:T(8,128)(2,1)} %copy-done.1, ...), custom_call_target="tpu_custom_call" | custom-call | tf_op jit(solution)/shard_map/step_updated/pallas_call | solution.py:191
  192.0 3.8 %collective-permute-start.42 = (bf16[64,128]{1,0:T(8,128)(2,1)}, bf16[64,128]{1,0:T(8,128)(2,1)S(1)}, u32[]{:S(2)}, u32[]{:S(2)}) collective-permute-start(bf16[64,128]{1,0:T(8,128)(2,1)} %get-tuple-element.100), channel_id=1, source_target_pairs={{0,2},{1,3},{2,0},{3,1},{4,6},{5,7},{6,4},{7,5},{8,10},{9,11},{10,... | collective-permute-start | bytes 49160 | tf_op jit(solution)/shard_map/ppermute | solution.py:13
  196.1 1.7 collective-permute-done.42.refs_25_
  197.7 3.8 %collective-permute-done.43.refs_26_ = bf16[64,128]{1,0:T(8,128)(2,1)S(1)} collective-permute-done((bf16[64,128]{1,0:T(8,128)(2,1)}, bf16[64,128]{1,0:T(8,128)(2,1)S(1)}, u32[]{:S(2)}, u32[]{:S(2)}) %collective-permute-start.43) | collective-permute-done | bytes 16416 | tf_op jit(solution)/shard_map/ppermute | solution.py:13
  202.2 5.0 %step_solved.9 = (f32[64,128]{1,0:T(8,128)}, bf16[64,128]{1,0:T(8,128)(2,1)}, bf16[64,128]{1,0:T(8,128)(2,1)}, bf16[64,128]{1,0:T(8,128)(2,1)}, f32[64,128]{1,0:T(8,128)}) custom-call(s32[27]{0:T(128)} %pad_add_fusion.1.refs_0_, s32[256]{0:T(256)} %reshape.376.refs_1_, bf16[4,4,128,128]{3,2,1,0:T(8,128)(2,1)} %copy-done.1, bf16[4,4,128,128]{3,2,1,0:T(8,128)(2,1)} %copy-done, ...), custom_call_target="tpu_custom_call" | custom-call | tf_op jit(solution)/shard_map/step_solved/pallas_call | solution.py:191
  207.2 0.8 collective-permute-start.45
  208.0 3.6 %collective-permute-start.46 = (bf16[64,128]{1,0:T(8,128)(2,1)}, bf16[64,128]{1,0:T(8,128)(2,1)S(1)}, u32[]{:S(2)}, u32[]{:S(2)}) collective-permute-start(bf16[64,128]{1,0:T(8,128)(2,1)} %get-tuple-element.106), channel_id=1, source_target_pairs={{0,3},{1,2},{2,1},{3,0},{4,7},{5,6},{6,5},{7,4},{8,11},{9,10},{10,... | collective-permute-start | bytes 49160 | tf_op jit(solution)/shard_map/ppermute | solution.py:13
  212.1 1.6 collective-permute-done.46.refs_26_
  214.4 5.0 %step_updated.9 = (f32[64,128]{1,0:T(8,128)}, bf16[64,128]{1,0:T(8,128)(2,1)}, bf16[64,128]{1,0:T(8,128)(2,1)}, bf16[64,128]{1,0:T(8,128)(2,1)}, f32[64,128]{1,0:T(8,128)}) custom-call(s32[27]{0:T(128)} %pad_add_fusion.1.refs_0_, s32[256]{0:T(256)} %reshape.376.refs_1_, bf16[4,4,128,128]{3,2,1,0:T(8,128)(2,1)} %copy-done.1, ...), custom_call_target="tpu_custom_call" | custom-call | tf_op jit(solution)/shard_map/step_updated/pallas_call | solution.py:191
  219.7 3.8 %collective-permute-start.48 = (bf16[64,128]{1,0:T(8,128)(2,1)}, bf16[64,128]{1,0:T(8,128)(2,1)S(1)}, u32[]{:S(2)}, u32[]{:S(2)}) collective-permute-start(bf16[64,128]{1,0:T(8,128)(2,1)} %get-tuple-element.110), channel_id=1, source_target_pairs={{0,2},{1,3},{2,0},{3,1},{4,6},{5,7},{6,4},{7,5},{8,10},{9,11},{10,... | collective-permute-start | bytes 49160 | tf_op jit(solution)/shard_map/ppermute | solution.py:13
  223.8 1.7 collective-permute-done.48.refs_25_
  225.5 3.8 %collective-permute-done.49.refs_26_ = bf16[64,128]{1,0:T(8,128)(2,1)S(1)} collective-permute-done((bf16[64,128]{1,0:T(8,128)(2,1)}, bf16[64,128]{1,0:T(8,128)(2,1)S(1)}, u32[]{:S(2)}, u32[]{:S(2)}) %collective-permute-start.49) | collective-permute-done | bytes 16416 | tf_op jit(solution)/shard_map/ppermute | solution.py:13
  229.9 4.2 %step_last.1 = f32[64,128]{1,0:T(8,128)} custom-call(s32[27]{0:T(128)} %pad_add_fusion.1.refs_0_, s32[256]{0:T(256)} %reshape.376.refs_1_, bf16[4,4,128,128]{3,2,1,0:T(8,128)(2,1)} %copy-done.1, bf16[4,4,128,128]{3,2,1,0:T(8,128)(2,1)} %copy-done, bf16[4,4,128,128]{3,2,1,0:T(8,128)(2,1)} %collective-permute-done.3.refs_4_, ...), custom_call_target="tpu_custom_call" | custom-call | tf_op jit(solution)/shard_map/step_last/pallas_call | solution.py:191
  234.2 0.8 collective-permute-start.51
  235.0 3.6 %collective-permute-start.52 = (f32[64,128]{1,0:T(8,128)}, f32[64,128]{1,0:T(8,128)S(1)}, u32[]{:S(2)}, u32[]{:S(2)}) collective-permute-start(f32[64,128]{1,0:T(8,128)} %step_last.1), channel_id=1, source_target_pairs={{0,3},{1,2},{2,1},{3,0},{4,7},{5,6},{6,5},{7,4},{8,11},{9,10},{10,... | collective-permute-start | bytes 98312 | tf_op jit(solution)/shard_map/ppermute | solution.py:13
  239.3 1.7 collective-permute-done.52
  241.0 0.8 pad_maximum_fusion
  241.8 8.1 %all_to_all.5 = f32[8,32,128]{2,1,0:T(8,128)S(1)} all-to-all(f32[8,32,128]{2,1,0:T(8,128)S(1)} %bitcast.89), channel_id=1, replica_groups=mesh['row'=8,'col'=4] {'row'}, dimensions={0} | all-to-all | bytes 262144 | tf_op jit(solution)/shard_map/all_to_all | solution.py:313
  (194 shorter events, 25.9 us)
Async XLA Ops:
  1.9 49.9 %copy-start = (bf16[4,4,128,128]{3,2,1,0:T(8,128)(2,1)}, bf16[4,4,128,128]{3,2,1,0:T(8,128)(2,1)S(1)}, u32[]{:S(2)}) copy-start(bf16[4,4,128,128]{3,2,1,0:T(8,128)(2,1)S(1)} %get-tuple-element.118.refs_3_) | copy-start | bytes 1572868
  1.9 49.9 %copy-start.1 = (bf16[4,4,128,128]{3,2,1,0:T(8,128)(2,1)}, bf16[4,4,128,128]{3,2,1,0:T(8,128)(2,1)S(1)}, u32[]{:S(2)}) copy-start(bf16[4,4,128,128]{3,2,1,0:T(8,128)(2,1)S(1)} %get-tuple-element.119.refs_2_) | copy-start | bytes 1572868
  1.9 30.5 %collective-permute-start.5 = (bf16[4,4,128,128]{3,2,1,0:T(8,128)(2,1)S(1)}, bf16[4,4,128,128]{3,2,1,0:T(8,128)(2,1)S(1)}, u32[]{:S(2)}, u32[]{:S(2)}) collective-permute-start(bf16[4,4,128,128]{3,2,1,0:T(8,128)(2,1)S(1)} %get-tuple-element.119.refs_2_), channel_id=1, source_target_pairs={{0,8},{4,12},{8,0},{12,4},{16,24},{20,28},{24,16},{28,20},{1,9},{5... | collective-permute-start | bytes 1572872 | tf_op jit(solution)/shard_map/ppermute | solution.py:13
  5.0 29.7 %collective-permute-start.9 = (bf16[4,4,128,128]{3,2,1,0:T(8,128)(2,1)S(1)}, bf16[4,4,128,128]{3,2,1,0:T(8,128)(2,1)S(1)}, u32[]{:S(2)}, u32[]{:S(2)}) collective-permute-start(bf16[4,4,128,128]{3,2,1,0:T(8,128)(2,1)S(1)} %get-tuple-element.119.refs_2_), channel_id=1, source_target_pairs={{0,16},{4,20},{8,24},{12,28},{16,0},{20,4},{24,8},{28,12},{1,17},{... | collective-permute-start | bytes 1572872 | tf_op jit(solution)/shard_map/ppermute | solution.py:13
  6.5 26.4 %collective-permute-start.10 = (bf16[4,4,128,128]{3,2,1,0:T(8,128)(2,1)S(1)}, bf16[4,4,128,128]{3,2,1,0:T(8,128)(2,1)S(1)}, u32[]{:S(2)}, u32[]{:S(2)}) collective-permute-start(bf16[4,4,128,128]{3,2,1,0:T(8,128)(2,1)S(1)} %get-tuple-element.118.refs_3_), channel_id=1, source_target_pairs={{0,16},{4,20},{8,24},{12,28},{16,0},{20,4},{24,8},{28,12},{1,17},{... | collective-permute-start | bytes 1572872 | tf_op jit(solution)/shard_map/ppermute | solution.py:13
  7.0 27.7 %collective-permute-start.6 = (bf16[4,4,128,128]{3,2,1,0:T(8,128)(2,1)S(1)}, bf16[4,4,128,128]{3,2,1,0:T(8,128)(2,1)S(1)}, u32[]{:S(2)}, u32[]{:S(2)}) collective-permute-start(bf16[4,4,128,128]{3,2,1,0:T(8,128)(2,1)S(1)} %get-tuple-element.118.refs_3_), channel_id=1, source_target_pairs={{0,8},{4,12},{8,0},{12,4},{16,24},{20,28},{24,16},{28,20},{1,9},{5... | collective-permute-start | bytes 1572872 | tf_op jit(solution)/shard_map/ppermute | solution.py:13
  7.2 2.8 %collective-permute-start = (f32[1,8,256]{2,1,0:T(8,128)S(1)}, f32[1,8,256]{2,1,0:T(8,128)S(1)}, u32[]{:S(2)}, u32[]{:S(2)}) collective-permute-start(f32[1,8,256]{2,1,0:T(8,128)S(1)} %fusion.7), channel_id=1, source_target_pairs={{0,4},{4,0},{8,12},{12,8},{16,20},{20,16},{24,28},{28,24},{1,5},{5... | collective-permute-start | bytes 24584 | tf_op jit(solution)/shard_map/ppermute | solution.py:13
  10.0 18.5 %collective-permute-start.1 = (f32[2,8,256]{2,1,0:T(8,128)S(1)}, f32[2,8,256]{2,1,0:T(8,128)S(1)}, u32[]{:S(2)}, u32[]{:S(2)}) collective-permute-start(f32[2,8,256]{2,1,0:T(8,128)S(1)} %pad_maximum_fusion.3), channel_id=1, source_target_pairs={{0,8},{4,12},{8,0},{12,4},{16,24},{20,28},{24,16},{28,20},{1,9},{5... | collective-permute-start | bytes 49160 | tf_op jit(solution)/shard_map/ppermute | solution.py:13
  28.5 3.9 %collective-permute-start.2 = (f32[4,8,256]{2,1,0:T(8,128)S(1)}, f32[4,8,256]{2,1,0:T(8,128)S(1)}, u32[]{:S(2)}, u32[]{:S(2)}) collective-permute-start(f32[4,8,256]{2,1,0:T(8,128)S(1)} %pad_maximum_fusion.2), channel_id=1, source_target_pairs={{0,16},{4,20},{8,24},{12,28},{16,0},{20,4},{24,8},{28,12},{1,17},{... | collective-permute-start | bytes 98312 | tf_op jit(solution)/shard_map/ppermute | solution.py:13
  32.4 6.1 %collective-permute-start.3 = (bf16[4,4,128,128]{3,2,1,0:T(8,128)(2,1)S(1)}, bf16[4,4,128,128]{3,2,1,0:T(8,128)(2,1)}, u32[]{:S(2)}, u32[]{:S(2)}) collective-permute-start(bf16[4,4,128,128]{3,2,1,0:T(8,128)(2,1)S(1)} %get-tuple-element.119.refs_2_), channel_id=1, source_target_pairs={{0,4},{4,0},{8,12},{12,8},{16,20},{20,16},{24,28},{28,24},{1,5},{5... | collective-permute-start | bytes 1572872 | tf_op jit(solution)/shard_map/ppermute | solution.py:13
  32.4 20.3 %copy-start.2 = (bf16[4,4,128,128]{3,2,1,0:T(8,128)(2,1)}, bf16[4,4,128,128]{3,2,1,0:T(8,128)(2,1)S(1)}, u32[]{:S(2)}) copy-start(bf16[4,4,128,128]{3,2,1,0:T(8,128)(2,1)S(1)} %collective-permute-done.5.refs_6_) | copy-start | bytes 1572868
  32.4 6.3 %collective-permute-start.4 = (bf16[4,4,128,128]{3,2,1,0:T(8,128)(2,1)S(1)}, bf16[4,4,128,128]{3,2,1,0:T(8,128)(2,1)}, u32[]{:S(2)}, u32[]{:S(2)}) collective-permute-start(bf16[4,4,128,128]{3,2,1,0:T(8,128)(2,1)S(1)} %get-tuple-element.118.refs_3_), channel_id=1, source_target_pairs={{0,4},{4,0},{8,12},{12,8},{16,20},{20,16},{24,28},{28,24},{1,5},{5... | collective-permute-start | bytes 1572872 | tf_op jit(solution)/shard_map/ppermute | solution.py:13
  32.9 19.7 %copy-start.4 = (bf16[4,4,128,128]{3,2,1,0:T(8,128)(2,1)}, bf16[4,4,128,128]{3,2,1,0:T(8,128)(2,1)S(1)}, u32[]{:S(2)}) copy-start(bf16[4,4,128,128]{3,2,1,0:T(8,128)(2,1)S(1)} %collective-permute-done.10.refs_11_) | copy-start | bytes 1572868
  32.9 16.2 %collective-permute-start.14 = (bf16[4,4,128,128]{3,2,1,0:T(8,128)(2,1)S(1)}, bf16[4,4,128,128]{3,2,1,0:T(8,128)(2,1)}, u32[]{:S(2)}, u32[]{:S(2)}) collective-permute-start(bf16[4,4,128,128]{3,2,1,0:T(8,128)(2,1)S(1)} %collective-permute-done.10.refs_11_), channel_id=1, source_target_pairs={{0,8},{4,12},{8,0},{12,4},{16,24},{20,28},{24,16},{28,20},{1,9},{5... | collective-permute-start | bytes 1572872 | tf_op jit(solution)/shard_map/ppermute | solution.py:13
  34.7 18.0 %copy-start.3 = (bf16[4,4,128,128]{3,2,1,0:T(8,128)(2,1)}, bf16[4,4,128,128]{3,2,1,0:T(8,128)(2,1)S(1)}, u32[]{:S(2)}) copy-start(bf16[4,4,128,128]{3,2,1,0:T(8,128)(2,1)S(1)} %collective-permute-done.9.refs_10_) | copy-start | bytes 1572868
  34.7 15.0 %collective-permute-start.12 = (bf16[4,4,128,128]{3,2,1,0:T(8,128)(2,1)S(1)}, bf16[4,4,128,128]{3,2,1,0:T(8,128)(2,1)}, u32[]{:S(2)}, u32[]{:S(2)}) collective-permute-start(bf16[4,4,128,128]{3,2,1,0:T(8,128)(2,1)S(1)} %collective-permute-done.10.refs_11_), channel_id=1, source_target_pairs={{0,4},{4,0},{8,12},{12,8},{16,20},{20,16},{24,28},{28,24},{1,5},{5... | collective-permute-start | bytes 1572872 | tf_op jit(solution)/shard_map/ppermute | solution.py:13
  34.7 18.0 %copy-start.5 = (bf16[4,4,128,128]{3,2,1,0:T(8,128)(2,1)}, bf16[4,4,128,128]{3,2,1,0:T(8,128)(2,1)S(1)}, u32[]{:S(2)}) copy-start(bf16[4,4,128,128]{3,2,1,0:T(8,128)(2,1)S(1)} %collective-permute-done.6.refs_7_) | copy-start | bytes 1572868
  34.7 14.4 %collective-permute-start.13 = (bf16[4,4,128,128]{3,2,1,0:T(8,128)(2,1)S(1)}, bf16[4,4,128,128]{3,2,1,0:T(8,128)(2,1)}, u32[]{:S(2)}, u32[]{:S(2)}) collective-permute-start(bf16[4,4,128,128]{3,2,1,0:T(8,128)(2,1)S(1)} %collective-permute-done.5.refs_6_), channel_id=1, source_target_pairs={{0,16},{4,20},{8,24},{12,28},{16,0},{20,4},{24,8},{28,12},{1,17},{... | collective-permute-start | bytes 1572872 | tf_op jit(solution)/shard_map/ppermute | solution.py:13
  38.5 13.4 %collective-permute-start.7 = (bf16[4,4,128,128]{3,2,1,0:T(8,128)(2,1)S(1)}, bf16[4,4,128,128]{3,2,1,0:T(8,128)(2,1)}, u32[]{:S(2)}, u32[]{:S(2)}) collective-permute-start(bf16[4,4,128,128]{3,2,1,0:T(8,128)(2,1)S(1)} %collective-permute-done.5.refs_6_), channel_id=1, source_target_pairs={{0,4},{4,0},{8,12},{12,8},{16,20},{20,16},{24,28},{28,24},{1,5},{5... | collective-permute-start | bytes 1572872 | tf_op jit(solution)/shard_map/ppermute | solution.py:13
  38.7 13.2 %collective-permute-start.11 = (bf16[4,4,128,128]{3,2,1,0:T(8,128)(2,1)S(1)}, bf16[4,4,128,128]{3,2,1,0:T(8,128)(2,1)}, u32[]{:S(2)}, u32[]{:S(2)}) collective-permute-start(bf16[4,4,128,128]{3,2,1,0:T(8,128)(2,1)S(1)} %collective-permute-done.9.refs_10_), channel_id=1, source_target_pairs={{0,4},{4,0},{8,12},{12,8},{16,20},{20,16},{24,28},{28,24},{1,5},{5... | collective-permute-start | bytes 1572872 | tf_op jit(solution)/shard_map/ppermute | solution.py:13
  49.1 2.8 %collective-permute-start.8 = (bf16[4,4,128,128]{3,2,1,0:T(8,128)(2,1)S(1)}, bf16[4,4,128,128]{3,2,1,0:T(8,128)(2,1)}, u32[]{:S(2)}, u32[]{:S(2)}) collective-permute-start(bf16[4,4,128,128]{3,2,1,0:T(8,128)(2,1)S(1)} %collective-permute-done.6.refs_7_), channel_id=1, source_target_pairs={{0,4},{4,0},{8,12},{12,8},{16,20},{20,16},{24,28},{28,24},{1,5},{5... | collective-permute-start | bytes 1572872 | tf_op jit(solution)/shard_map/ppermute | solution.py:13
  49.1 2.8 %collective-permute-start.15 = (bf16[4,4,128,128]{3,2,1,0:T(8,128)(2,1)}, bf16[4,4,128,128]{3,2,1,0:T(8,128)(2,1)}, u32[]{:S(2)}, u32[]{:S(2)}) collective-permute-start(bf16[4,4,128,128]{3,2,1,0:T(8,128)(2,1)} %collective-permute-done.13.refs_14_), channel_id=1, source_target_pairs={{0,4},{4,0},{8,12},{12,8},{16,20},{20,16},{24,28},{28,24},{1,5},{5... | collective-permute-start | bytes 1572872 | tf_op jit(solution)/shard_map/ppermute | solution.py:13
  49.6 3.0 %collective-permute-start.16 = (bf16[4,4,128,128]{3,2,1,0:T(8,128)(2,1)}, bf16[4,4,128,128]{3,2,1,0:T(8,128)(2,1)}, u32[]{:S(2)}, u32[]{:S(2)}) collective-permute-start(bf16[4,4,128,128]{3,2,1,0:T(8,128)(2,1)} %collective-permute-done.14.refs_15_), channel_id=1, source_target_pairs={{0,4},{4,0},{8,12},{12,8},{16,20},{20,16},{24,28},{28,24},{1,5},{5... | collective-permute-start | bytes 1572872 | tf_op jit(solution)/shard_map/ppermute | solution.py:13
  64.5 4.5 %collective-permute-start.17 = (bf16[64,128]{1,0:T(8,128)(2,1)}, bf16[64,128]{1,0:T(8,128)(2,1)S(1)}, u32[]{:S(2)}, u32[]{:S(2)}) collective-permute-start(bf16[64,128]{1,0:T(8,128)(2,1)} %get-tuple-element.59), channel_id=1, source_target_pairs={{0,1},{1,0},{2,3},{3,2},{4,5},{5,4},{6,7},{7,6},{8,9},{9,8},{10,11... | collective-permute-start | bytes 49160 | tf_op jit(solution)/shard_map/ppermute | solution.py:13
  66.2 4.9 %collective-permute-start.18 = (bf16[64,128]{1,0:T(8,128)(2,1)}, bf16[64,128]{1,0:T(8,128)(2,1)S(1)}, u32[]{:S(2)}, u32[]{:S(2)}) collective-permute-start(bf16[64,128]{1,0:T(8,128)(2,1)} %get-tuple-element.60), channel_id=1, source_target_pairs={{0,2},{1,3},{2,0},{3,1},{4,6},{5,7},{6,4},{7,5},{8,10},{9,11},{10,... | collective-permute-start | bytes 49160 | tf_op jit(solution)/shard_map/ppermute | solution.py:13
  68.7 5.7 %collective-permute-start.19 = (bf16[64,128]{1,0:T(8,128)(2,1)}, bf16[64,128]{1,0:T(8,128)(2,1)S(1)}, u32[]{:S(2)}, u32[]{:S(2)}) collective-permute-start(bf16[64,128]{1,0:T(8,128)(2,1)} %get-tuple-element.61), channel_id=1, source_target_pairs={{0,3},{1,2},{2,1},{3,0},{4,7},{5,6},{6,5},{7,4},{8,11},{9,10},{10,... | collective-permute-start | bytes 49160 | tf_op jit(solution)/shard_map/ppermute | solution.py:13
  69.0 5.5 %copy-start.9 = (bf16[64,128]{1,0:T(8,128)(2,1)}, bf16[64,128]{1,0:T(8,128)(2,1)S(1)}, u32[]{:S(2)}) copy-start(bf16[64,128]{1,0:T(8,128)(2,1)S(1)} %collective-permute-done.17.refs_24_) | copy-start | bytes 49156
  84.2 4.5 %collective-permute-start.20 = (bf16[64,128]{1,0:T(8,128)(2,1)}, bf16[64,128]{1,0:T(8,128)(2,1)S(1)}, u32[]{:S(2)}, u32[]{:S(2)}) collective-permute-start(bf16[64,128]{1,0:T(8,128)(2,1)} %get-tuple-element.64), channel_id=1, source_target_pairs={{0,1},{1,0},{2,3},{3,2},{4,5},{5,4},{6,7},{7,6},{8,9},{9,8},{10,11... | collective-permute-start | bytes 49160 | tf_op jit(solution)/shard_map/ppermute | solution.py:13
  84.3 4.9 %collective-permute-start.21 = (bf16[64,128]{1,0:T(8,128)(2,1)}, bf16[64,128]{1,0:T(8,128)(2,1)S(1)}, u32[]{:S(2)}, u32[]{:S(2)}) collective-permute-start(bf16[64,128]{1,0:T(8,128)(2,1)} %get-tuple-element.65), channel_id=1, source_target_pairs={{0,2},{1,3},{2,0},{3,1},{4,6},{5,7},{6,4},{7,5},{8,10},{9,11},{10,... | collective-permute-start | bytes 49160 | tf_op jit(solution)/shard_map/ppermute | solution.py:13
  85.1 5.7 %collective-permute-start.22 = (bf16[64,128]{1,0:T(8,128)(2,1)}, bf16[64,128]{1,0:T(8,128)(2,1)S(1)}, u32[]{:S(2)}, u32[]{:S(2)}) collective-permute-start(bf16[64,128]{1,0:T(8,128)(2,1)} %get-tuple-element.66), channel_id=1, source_target_pairs={{0,3},{1,2},{2,1},{3,0},{4,7},{5,6},{6,5},{7,4},{8,11},{9,10},{10,... | collective-permute-start | bytes 49160 | tf_op jit(solution)/shard_map/ppermute | solution.py:13
  97.1 4.5 %collective-permute-start.23 = (bf16[64,128]{1,0:T(8,128)(2,1)}, bf16[64,128]{1,0:T(8,128)(2,1)S(1)}, u32[]{:S(2)}, u32[]{:S(2)}) collective-permute-start(bf16[64,128]{1,0:T(8,128)(2,1)} %get-tuple-element.69), channel_id=1, source_target_pairs={{0,1},{1,0},{2,3},{3,2},{4,5},{5,4},{6,7},{7,6},{8,9},{9,8},{10,11... | collective-permute-start | bytes 49160 | tf_op jit(solution)/shard_map/ppermute | solution.py:13
  97.5 5.7 %collective-permute-start.24 = (bf16[64,128]{1,0:T(8,128)(2,1)}, bf16[64,128]{1,0:T(8,128)(2,1)S(1)}, u32[]{:S(2)}, u32[]{:S(2)}) collective-permute-start(bf16[64,128]{1,0:T(8,128)(2,1)} %get-tuple-element.70), channel_id=1, source_target_pairs={{0,2},{1,3},{2,0},{3,1},{4,6},{5,7},{6,4},{7,5},{8,10},{9,11},{10,... | collective-permute-start | bytes 49160 | tf_op jit(solution)/shard_map/ppermute | solution.py:13
  101.3 5.7 %collective-permute-start.25 = (bf16[64,128]{1,0:T(8,128)(2,1)}, bf16[64,128]{1,0:T(8,128)(2,1)S(1)}, u32[]{:S(2)}, u32[]{:S(2)}) collective-permute-start(bf16[64,128]{1,0:T(8,128)(2,1)} %get-tuple-element.71), channel_id=1, source_target_pairs={{0,3},{1,2},{2,1},{3,0},{4,7},{5,6},{6,5},{7,4},{8,11},{9,10},{10,... | collective-permute-start | bytes 49160 | tf_op jit(solution)/shard_map/ppermute | solution.py:13
  101.6 5.5 %copy-start.11 = (bf16[64,128]{1,0:T(8,128)(2,1)}, bf16[64,128]{1,0:T(8,128)(2,1)S(1)}, u32[]{:S(2)}) copy-start(bf16[64,128]{1,0:T(8,128)(2,1)S(1)} %collective-permute-done.23.refs_24_) | copy-start | bytes 49156
  116.1 4.5 %collective-permute-start.26 = (bf16[64,128]{1,0:T(8,128)(2,1)}, bf16[64,128]{1,0:T(8,128)(2,1)S(1)}, u32[]{:S(2)}, u32[]{:S(2)}) collective-permute-start(bf16[64,128]{1,0:T(8,128)(2,1)} %get-tuple-element.74), channel_id=1, source_target_pairs={{0,1},{1,0},{2,3},{3,2},{4,5},{5,4},{6,7},{7,6},{8,9},{9,8},{10,11... | collective-permute-start | bytes 49160 | tf_op jit(solution)/shard_map/ppermute | solution.py:13
  116.2 4.9 %collective-permute-start.27 = (bf16[64,128]{1,0:T(8,128)(2,1)}, bf16[64,128]{1,0:T(8,128)(2,1)S(1)}, u32[]{:S(2)}, u32[]{:S(2)}) collective-permute-start(bf16[64,128]{1,0:T(8,128)(2,1)} %get-tuple-element.75), channel_id=1, source_target_pairs={{0,2},{1,3},{2,0},{3,1},{4,6},{5,7},{6,4},{7,5},{8,10},{9,11},{10,... | collective-permute-start | bytes 49160 | tf_op jit(solution)/shard_map/ppermute | solution.py:13
  117.0 5.7 %collective-permute-start.28 = (bf16[64,128]{1,0:T(8,128)(2,1)}, bf16[64,128]{1,0:T(8,128)(2,1)S(1)}, u32[]{:S(2)}, u32[]{:S(2)}) collective-permute-start(bf16[64,128]{1,0:T(8,128)(2,1)} %get-tuple-element.76), channel_id=1, source_target_pairs={{0,3},{1,2},{2,1},{3,0},{4,7},{5,6},{6,5},{7,4},{8,11},{9,10},{10,... | collective-permute-start | bytes 49160 | tf_op jit(solution)/shard_map/ppermute | solution.py:13
  129.0 4.5 %collective-permute-start.29 = (bf16[64,128]{1,0:T(8,128)(2,1)}, bf16[64,128]{1,0:T(8,128)(2,1)S(1)}, u32[]{:S(2)}, u32[]{:S(2)}) collective-permute-start(bf16[64,128]{1,0:T(8,128)(2,1)} %get-tuple-element.79), channel_id=1, source_target_pairs={{0,1},{1,0},{2,3},{3,2},{4,5},{5,4},{6,7},{7,6},{8,9},{9,8},{10,11... | collective-permute-start | bytes 49160 | tf_op jit(solution)/shard_map/ppermute | solution.py:13
  129.4 5.7 %collective-permute-start.30 = (bf16[64,128]{1,0:T(8,128)(2,1)}, bf16[64,128]{1,0:T(8,128)(2,1)S(1)}, u32[]{:S(2)}, u32[]{:S(2)}) collective-permute-start(bf16[64,128]{1,0:T(8,128)(2,1)} %get-tuple-element.80), channel_id=1, source_target_pairs={{0,2},{1,3},{2,0},{3,1},{4,6},{5,7},{6,4},{7,5},{8,10},{9,11},{10,... | collective-permute-start | bytes 49160 | tf_op jit(solution)/shard_map/ppermute | solution.py:13
  133.2 5.7 %collective-permute-start.31 = (bf16[64,128]{1,0:T(8,128)(2,1)}, bf16[64,128]{1,0:T(8,128)(2,1)S(1)}, u32[]{:S(2)}, u32[]{:S(2)}) collective-permute-start(bf16[64,128]{1,0:T(8,128)(2,1)} %get-tuple-element.81), channel_id=1, source_target_pairs={{0,3},{1,2},{2,1},{3,0},{4,7},{5,6},{6,5},{7,4},{8,11},{9,10},{10,... | collective-permute-start | bytes 49160 | tf_op jit(solution)/shard_map/ppermute | solution.py:13
  133.5 5.5 %copy-start.13 = (bf16[64,128]{1,0:T(8,128)(2,1)}, bf16[64,128]{1,0:T(8,128)(2,1)S(1)}, u32[]{:S(2)}) copy-start(bf16[64,128]{1,0:T(8,128)(2,1)S(1)} %collective-permute-done.29.refs_24_) | copy-start | bytes 49156
  147.3 4.5 %collective-permute-start.32 = (bf16[64,128]{1,0:T(8,128)(2,1)}, bf16[64,128]{1,0:T(8,128)(2,1)S(1)}, u32[]{:S(2)}, u32[]{:S(2)}) collective-permute-start(bf16[64,128]{1,0:T(8,128)(2,1)} %get-tuple-element.84), channel_id=1, source_target_pairs={{0,1},{1,0},{2,3},{3,2},{4,5},{5,4},{6,7},{7,6},{8,9},{9,8},{10,11... | collective-permute-start | bytes 49160 | tf_op jit(solution)/shard_map/ppermute | solution.py:13
  147.4 4.9 %collective-permute-start.33 = (bf16[64,128]{1,0:T(8,128)(2,1)}, bf16[64,128]{1,0:T(8,128)(2,1)S(1)}, u32[]{:S(2)}, u32[]{:S(2)}) collective-permute-start(bf16[64,128]{1,0:T(8,128)(2,1)} %get-tuple-element.85), channel_id=1, source_target_pairs={{0,2},{1,3},{2,0},{3,1},{4,6},{5,7},{6,4},{7,5},{8,10},{9,11},{10,... | collective-permute-start | bytes 49160 | tf_op jit(solution)/shard_map/ppermute | solution.py:13
  148.2 5.7 %collective-permute-start.34 = (bf16[64,128]{1,0:T(8,128)(2,1)}, bf16[64,128]{1,0:T(8,128)(2,1)S(1)}, u32[]{:S(2)}, u32[]{:S(2)}) collective-permute-start(bf16[64,128]{1,0:T(8,128)(2,1)} %get-tuple-element.86), channel_id=1, source_target_pairs={{0,3},{1,2},{2,1},{3,0},{4,7},{5,6},{6,5},{7,4},{8,11},{9,10},{10,... | collective-permute-start | bytes 49160 | tf_op jit(solution)/shard_map/ppermute | solution.py:13
  160.9 4.5 %collective-permute-start.35 = (bf16[64,128]{1,0:T(8,128)(2,1)}, bf16[64,128]{1,0:T(8,128)(2,1)S(1)}, u32[]{:S(2)}, u32[]{:S(2)}) collective-permute-start(bf16[64,128]{1,0:T(8,128)(2,1)} %get-tuple-element.89), channel_id=1, source_target_pairs={{0,1},{1,0},{2,3},{3,2},{4,5},{5,4},{6,7},{7,6},{8,9},{9,8},{10,11... | collective-permute-start | bytes 49160 | tf_op jit(solution)/shard_map/ppermute | solution.py:13
  161.3 5.9 %collective-permute-start.36 = (bf16[64,128]{1,0:T(8,128)(2,1)}, bf16[64,128]{1,0:T(8,128)(2,1)S(1)}, u32[]{:S(2)}, u32[]{:S(2)}) collective-permute-start(bf16[64,128]{1,0:T(8,128)(2,1)} %get-tuple-element.90), channel_id=1, source_target_pairs={{0,2},{1,3},{2,0},{3,1},{4,6},{5,7},{6,4},{7,5},{8,10},{9,11},{10,... | collective-permute-start | bytes 49160 | tf_op jit(solution)/shard_map/ppermute | solution.py:13
  165.3 5.7 %collective-permute-start.37 = (bf16[64,128]{1,0:T(8,128)(2,1)}, bf16[64,128]{1,0:T(8,128)(2,1)S(1)}, u32[]{:S(2)}, u32[]{:S(2)}) collective-permute-start(bf16[64,128]{1,0:T(8,128)(2,1)} %get-tuple-element.91), channel_id=1, source_target_pairs={{0,3},{1,2},{2,1},{3,0},{4,7},{5,6},{6,5},{7,4},{8,11},{9,10},{10,... | collective-permute-start | bytes 49160 | tf_op jit(solution)/shard_map/ppermute | solution.py:13
  165.4 5.6 %copy-start.15 = (bf16[64,128]{1,0:T(8,128)(2,1)}, bf16[64,128]{1,0:T(8,128)(2,1)S(1)}, u32[]{:S(2)}) copy-start(bf16[64,128]{1,0:T(8,128)(2,1)S(1)} %collective-permute-done.35.refs_24_) | copy-start | bytes 49156
  178.0 4.5 %collective-permute-start.38 = (bf16[64,128]{1,0:T(8,128)(2,1)}, bf16[64,128]{1,0:T(8,128)(2,1)S(1)}, u32[]{:S(2)}, u32[]{:S(2)}) collective-permute-start(bf16[64,128]{1,0:T(8,128)(2,1)} %get-tuple-element.94), channel_id=1, source_target_pairs={{0,1},{1,0},{2,3},{3,2},{4,5},{5,4},{6,7},{7,6},{8,9},{9,8},{10,11... | collective-permute-start | bytes 49160 | tf_op jit(solution)/shard_map/ppermute | solution.py:13
  178.1 4.9 %collective-permute-start.39 = (bf16[64,128]{1,0:T(8,128)(2,1)}, bf16[64,128]{1,0:T(8,128)(2,1)S(1)}, u32[]{:S(2)}, u32[]{:S(2)}) collective-permute-start(bf16[64,128]{1,0:T(8,128)(2,1)} %get-tuple-element.95), channel_id=1, source_target_pairs={{0,2},{1,3},{2,0},{3,1},{4,6},{5,7},{6,4},{7,5},{8,10},{9,11},{10,... | collective-permute-start | bytes 49160 | tf_op jit(solution)/shard_map/ppermute | solution.py:13
  178.9 5.7 %collective-permute-start.40 = (bf16[64,128]{1,0:T(8,128)(2,1)}, bf16[64,128]{1,0:T(8,128)(2,1)S(1)}, u32[]{:S(2)}, u32[]{:S(2)}) collective-permute-start(bf16[64,128]{1,0:T(8,128)(2,1)} %get-tuple-element.96), channel_id=1, source_target_pairs={{0,3},{1,2},{2,1},{3,0},{4,7},{5,6},{6,5},{7,4},{8,11},{9,10},{10,... | collective-permute-start | bytes 49160 | tf_op jit(solution)/shard_map/ppermute | solution.py:13
  191.6 4.5 %collective-permute-start.41 = (bf16[64,128]{1,0:T(8,128)(2,1)}, bf16[64,128]{1,0:T(8,128)(2,1)S(1)}, u32[]{:S(2)}, u32[]{:S(2)}) collective-permute-start(bf16[64,128]{1,0:T(8,128)(2,1)} %get-tuple-element.99), channel_id=1, source_target_pairs={{0,1},{1,0},{2,3},{3,2},{4,5},{5,4},{6,7},{7,6},{8,9},{9,8},{10,11... | collective-permute-start | bytes 49160 | tf_op jit(solution)/shard_map/ppermute | solution.py:13
  192.0 5.7 %collective-permute-start.42 = (bf16[64,128]{1,0:T(8,128)(2,1)}, bf16[64,128]{1,0:T(8,128)(2,1)S(1)}, u32[]{:S(2)}, u32[]{:S(2)}) collective-permute-start(bf16[64,128]{1,0:T(8,128)(2,1)} %get-tuple-element.100), channel_id=1, source_target_pairs={{0,2},{1,3},{2,0},{3,1},{4,6},{5,7},{6,4},{7,5},{8,10},{9,11},{10,... | collective-permute-start | bytes 49160 | tf_op jit(solution)/shard_map/ppermute | solution.py:13
  195.8 5.7 %collective-permute-start.43 = (bf16[64,128]{1,0:T(8,128)(2,1)}, bf16[64,128]{1,0:T(8,128)(2,1)S(1)}, u32[]{:S(2)}, u32[]{:S(2)}) collective-permute-start(bf16[64,128]{1,0:T(8,128)(2,1)} %get-tuple-element.101), channel_id=1, source_target_pairs={{0,3},{1,2},{2,1},{3,0},{4,7},{5,6},{6,5},{7,4},{8,11},{9,10},{10,... | collective-permute-start | bytes 49160 | tf_op jit(solution)/shard_map/ppermute | solution.py:13
  196.1 5.5 %copy-start.17 = (bf16[64,128]{1,0:T(8,128)(2,1)}, bf16[64,128]{1,0:T(8,128)(2,1)S(1)}, u32[]{:S(2)}) copy-start(bf16[64,128]{1,0:T(8,128)(2,1)S(1)} %collective-permute-done.41.refs_24_) | copy-start | bytes 49156
  207.1 4.5 %collective-permute-start.44 = (bf16[64,128]{1,0:T(8,128)(2,1)}, bf16[64,128]{1,0:T(8,128)(2,1)S(1)}, u32[]{:S(2)}, u32[]{:S(2)}) collective-permute-start(bf16[64,128]{1,0:T(8,128)(2,1)} %get-tuple-element.104), channel_id=1, source_target_pairs={{0,1},{1,0},{2,3},{3,2},{4,5},{5,4},{6,7},{7,6},{8,9},{9,8},{10,11... | collective-permute-start | bytes 49160 | tf_op jit(solution)/shard_map/ppermute | solution.py:13
  207.2 4.9 %collective-permute-start.45 = (bf16[64,128]{1,0:T(8,128)(2,1)}, bf16[64,128]{1,0:T(8,128)(2,1)S(1)}, u32[]{:S(2)}, u32[]{:S(2)}) collective-permute-start(bf16[64,128]{1,0:T(8,128)(2,1)} %get-tuple-element.105), channel_id=1, source_target_pairs={{0,2},{1,3},{2,0},{3,1},{4,6},{5,7},{6,4},{7,5},{8,10},{9,11},{10,... | collective-permute-start | bytes 49160 | tf_op jit(solution)/shard_map/ppermute | solution.py:13
  208.0 5.7 %collective-permute-start.46 = (bf16[64,128]{1,0:T(8,128)(2,1)}, bf16[64,128]{1,0:T(8,128)(2,1)S(1)}, u32[]{:S(2)}, u32[]{:S(2)}) collective-permute-start(bf16[64,128]{1,0:T(8,128)(2,1)} %get-tuple-element.106), channel_id=1, source_target_pairs={{0,3},{1,2},{2,1},{3,0},{4,7},{5,6},{6,5},{7,4},{8,11},{9,10},{10,... | collective-permute-start | bytes 49160 | tf_op jit(solution)/shard_map/ppermute | solution.py:13
  219.3 4.5 %collective-permute-start.47 = (bf16[64,128]{1,0:T(8,128)(2,1)}, bf16[64,128]{1,0:T(8,128)(2,1)S(1)}, u32[]{:S(2)}, u32[]{:S(2)}) collective-permute-start(bf16[64,128]{1,0:T(8,128)(2,1)} %get-tuple-element.109), channel_id=1, source_target_pairs={{0,1},{1,0},{2,3},{3,2},{4,5},{5,4},{6,7},{7,6},{8,9},{9,8},{10,11... | collective-permute-start | bytes 49160 | tf_op jit(solution)/shard_map/ppermute | solution.py:13
  219.7 5.7 %collective-permute-start.48 = (bf16[64,128]{1,0:T(8,128)(2,1)}, bf16[64,128]{1,0:T(8,128)(2,1)S(1)}, u32[]{:S(2)}, u32[]{:S(2)}) collective-permute-start(bf16[64,128]{1,0:T(8,128)(2,1)} %get-tuple-element.110), channel_id=1, source_target_pairs={{0,2},{1,3},{2,0},{3,1},{4,6},{5,7},{6,4},{7,5},{8,10},{9,11},{10,... | collective-permute-start | bytes 49160 | tf_op jit(solution)/shard_map/ppermute | solution.py:13
  223.5 5.7 %collective-permute-start.49 = (bf16[64,128]{1,0:T(8,128)(2,1)}, bf16[64,128]{1,0:T(8,128)(2,1)S(1)}, u32[]{:S(2)}, u32[]{:S(2)}) collective-permute-start(bf16[64,128]{1,0:T(8,128)(2,1)} %get-tuple-element.111), channel_id=1, source_target_pairs={{0,3},{1,2},{2,1},{3,0},{4,7},{5,6},{6,5},{7,4},{8,11},{9,10},{10,... | collective-permute-start | bytes 49160 | tf_op jit(solution)/shard_map/ppermute | solution.py:13
  234.1 4.5 %collective-permute-start.50 = (f32[64,128]{1,0:T(8,128)}, f32[64,128]{1,0:T(8,128)S(1)}, u32[]{:S(2)}, u32[]{:S(2)}) collective-permute-start(f32[64,128]{1,0:T(8,128)} %step_last.1), channel_id=1, source_target_pairs={{0,1},{1,0},{2,3},{3,2},{4,5},{5,4},{6,7},{7,6},{8,9},{9,8},{10,11... | collective-permute-start | bytes 98312 | tf_op jit(solution)/shard_map/ppermute | solution.py:13
  234.2 5.1 %collective-permute-start.51 = (f32[64,128]{1,0:T(8,128)}, f32[64,128]{1,0:T(8,128)S(1)}, u32[]{:S(2)}, u32[]{:S(2)}) collective-permute-start(f32[64,128]{1,0:T(8,128)} %step_last.1), channel_id=1, source_target_pairs={{0,2},{1,3},{2,0},{3,1},{4,6},{5,7},{6,4},{7,5},{8,10},{9,11},{10,... | collective-permute-start | bytes 98312 | tf_op jit(solution)/shard_map/ppermute | solution.py:13
  235.0 6.0 %collective-permute-start.52 = (f32[64,128]{1,0:T(8,128)}, f32[64,128]{1,0:T(8,128)S(1)}, u32[]{:S(2)}, u32[]{:S(2)}) collective-permute-start(f32[64,128]{1,0:T(8,128)} %step_last.1), channel_id=1, source_target_pairs={{0,3},{1,2},{2,1},{3,0},{4,7},{5,6},{6,5},{7,4},{8,11},{9,10},{10,... | collective-permute-start | bytes 98312 | tf_op jit(solution)/shard_map/ppermute | solution.py:13
  (32 other events, 61.0 us)

commit v2 on v1

--- a/solution.py
+++ b/solution.py
@@ -15,6 +15,15 @@
 
 def bits_of(size):
     return [1 << b for b in range(size.bit_length() - 1)]
+
+
+def flip_order(values, position):
+    size = values.shape[0]
+    rest = values.shape[1:]
+    for bit in bits_of(size):
+        paired = values.reshape(size // (2 * bit), 2, bit, *rest)
+        values = jnp.where((position & bit) != 0, paired[:, ::-1], paired).reshape(size, *rest)
+    return values
 
 
 def gather_rows(factor):
@@ -33,44 +42,58 @@
     return [part for k in range(size) for part in pieces[k]]
 
 
-def prepare_diagonal(scalars, dims, parts):
+def vmem_budget(parts):
+    return sum(part.size * part.dtype.itemsize for part in parts) * 5 // 4 + (2 << 20)
+
+
+def load_operator(scalars, slot_of, dims, parts):
     rows, cols, groups, per_row, slots, block = dims
     half = per_row // 2
 
     def body(*refs):
-        sc, slot_of = refs[0], refs[1]
+        sc, slots_own = refs[0], refs[1]
         part_refs = refs[2:2 + 2 * rows]
-        out = refs[2 + 2 * rows]
-        here = sc[0]
-        row_high = sc[1]
+        whole, diag, sems = refs[2 + 2 * rows:]
+        row = sc[0]
+        col = sc[1]
         op = sc[2]
+        copies = []
+        for k in range(rows):
+            for h in range(2):
+                copies.append(
+                    pltpu.make_async_copy(
+                        part_refs[2 * k + h], whole.at[pl.ds(h * half, half), row ^ k], sems.at[2 * k + h]
+                    )
+                )
+                copies[-1].start()
+        for copy in copies:
+            copy.wait()
         row_i = lax.broadcasted_iota(jnp.int32, (block, block), 0)
         col_i = lax.broadcasted_iota(jnp.int32, (block, block), 1)
         ahead = jnp.where(op == 0, row_i - col_i, col_i - row_i) > 0
-        for k in range(rows):
-            @pl.when(here == k % cols)
-            def _(k=k):
-                m = row_high ^ (k // cols)
-                for i in range(per_row):
-                    source = part_refs[2 * k + i // half]
-                    s = slot_of[m * per_row + i]
-                    value = source[i % half, s].astype(jnp.float32)
-                    out[m, i] = jnp.where(ahead, value, 0.0).astype(out.dtype)
+        for m in range(groups):
+            for i in range(per_row):
+                value = whole[i, col + cols * m, slots_own[m * per_row + i]].astype(jnp.float32)
+                diag[m, i] = jnp.where(ahead, value, 0.0).astype(diag.dtype)
 
     vmem = pl.BlockSpec(memory_space=pltpu.VMEM)
     smem = pl.BlockSpec(memory_space=pltpu.SMEM)
     return pl.pallas_call(
         body,
-        out_shape=jax.ShapeDtypeStruct((groups, per_row, block, block), parts[0].dtype),
-        in_specs=[smem, smem] + [vmem] * len(parts),
-        out_specs=vmem,
-        name="prepare_diagonal",
-    )(scalars[0], scalars[1], *parts)
-
-
-def step_kernel(kind, step, dims, scalars, table, parts, diag, level, pivot, state, received):
+        out_shape=[
+            jax.ShapeDtypeStruct((per_row, rows, slots, block, block), parts[0].dtype),
+            jax.ShapeDtypeStruct((groups, per_row, block, block), parts[0].dtype),
+        ],
+        in_specs=[smem, smem] + [pl.BlockSpec(memory_space=pl.ANY)] * len(parts),
+        out_specs=[vmem, vmem],
+        scratch_shapes=[pltpu.SemaphoreType.DMA((len(parts),))],
+        compiler_params=pltpu.CompilerParams(vmem_limit_bytes=vmem_budget(parts)),
+        name="load_operator",
+    )(scalars, slot_of, *parts)
+
+
+def step_kernel(kind, step, dims, scalars, table, operator, level, pivot, state, received):
     rows, cols, groups, per_row, slots, block, kept = dims
-    half = per_row // 2
     lanes = groups * kept
     locals_here = per_row * groups
     flat = (per_row * lanes, block)
@@ -80,8 +103,9 @@
         refs = list(refs)
         sc = refs.pop(0)
         idx = refs.pop(0)
-        part_refs = [refs.pop(0) for _ in parts]
-        diag_ref = refs.pop(0)
+        if kind != "last":
+            whole = refs.pop(0)
+            diag = refs.pop(0)
         level_ref = refs.pop(0)
         pivot_ref = refs.pop(0)
         res_ref = refs.pop(0)
@@ -130,49 +154,38 @@
         for m in range(groups):
             xs[m, locals_here] = jnp.zeros((lanes, block), jnp.float32)
         acc[...] = jnp.zeros(acc.shape, jnp.float32)
-        here = sc[0]
-        row_high = sc[1]
+        col = sc[1]
         which = 3 + 4 * (step + (1 if kind == "updated" else 0)) + (2 if kind == "solved" else 0)
-        low = sc[which]
-        high = sc[which + 1]
 
         def contract(x, w):
             return lax.dot_general(
                 x.astype(jnp.bfloat16), w, (((1,), (1,)), ((), ())), preferred_element_type=jnp.float32
             )
 
-        def group(i, part):
-            for kk in range(cols):
+        def group(i, carry):
+            for cc in range(cols):
                 value = None
-                for mm in range(groups):
-                    k = kk + cols * mm
-                    m = row_high ^ mm
+                for m in range(groups):
+                    k = cc + cols * m
                     for s in range(slots):
-                        j = idx[(k * per_row + i) * slots + s]
-                        term = contract(xs[m, j], part_refs[2 * k + part][i - part * half, s])
+                        j = idx[(i * rows + k) * slots + s]
+                        term = contract(xs[m, j], whole[i, k, s])
                         value = term if value is None else value + term
-                acc[here ^ kk, i] = value
-            own = acc[0, i]
+                acc[cc, i] = value
+            own = acc[col, i]
             for m in range(groups):
-                own = own + contract(xs[m, i * groups + m], diag_ref[m, i])
-            acc[0, i] = own
-
-        for part in range(2):
-            begin = jnp.maximum(low, part * half)
-            end = jnp.minimum(high, (part + 1) * half)
-
-            def loop(i, carry, part=part):
-                group(i, part)
-                return carry
-
-            lax.fori_loop(begin, end, loop, 0)
-        sends[0][...] = acc[0].reshape(flat)
-        for d in range(1, cols):
-            sends[d][...] = acc[d].reshape(flat).astype(sends[d].dtype)
+                own = own + contract(xs[m, i * groups + m], diag[m, i])
+            acc[col, i] = own
+            return carry
+
+        lax.fori_loop(sc[which], sc[which + 1], group, 0)
+        for d in range(cols):
+            sends[d][...] = acc[col ^ d].reshape(flat).astype(sends[d].dtype)
 
     vmem = pl.BlockSpec(memory_space=pltpu.VMEM)
     smem = pl.BlockSpec(memory_space=pltpu.SMEM)
-    args = [scalars, table, *parts, diag, level, pivot, *state, *received]
+    budget = vmem_budget(operator)
+    args = [scalars, table] + ([] if kind == "last" else list(operator)) + [level, pivot, *state, *received]
     if kind == "last":
         out_shape = jax.ShapeDtypeStruct(flat, jnp.float32)
         out_specs = vmem
@@ -194,6 +207,7 @@
         in_specs=[smem, smem] + [vmem] * (len(args) - 2),
         out_specs=out_specs,
         scratch_shapes=scratch,
+        compiler_params=pltpu.CompilerParams(vmem_limit_bytes=budget),
         name="step_" + kind,
     )(*args)
 
@@ -232,9 +246,9 @@
     def look_up(values, index):
         return jnp.sum(jnp.where(index[..., None] == blocks, values, 0), axis=-1)
 
-    slot_ids = small[:, :, block:block + slots].astype(jnp.int32)
-    row_class = jnp.arange(rows, dtype=jnp.int32) ^ r
-    row_ids = jnp.arange(per_row, dtype=jnp.int32)[None, :] * rows + row_class[:, None]
+    small = flip_order(small, r)
+    slot_ids = small[:, :, block:block + slots].astype(jnp.int32).transpose(1, 0, 2)
+    row_ids = blocks.reshape(per_row, rows)
     valid = slot_ids < total
     slot_snode = look_up(snode_of_block, slot_ids)
     slot_level = look_up(levels, slot_ids)
@@ -244,8 +258,7 @@
     active = valid & jnp.where(slot_snode == row_snode, before, row_level > slot_level)
     table = jnp.where(active, slot_ids // cols, locals_here).reshape(-1)
 
-    own_k = (c + cols * jnp.arange(groups, dtype=jnp.int32)) ^ r
-    own_small = jnp.take(small, own_k, axis=0)
+    own_small = lax.dynamic_index_in_dim(small.reshape(groups, cols, *small.shape[1:]), c, 1, keepdims=False)
     own_ids = jnp.arange(per_row, dtype=jnp.int32)[None, :] * rows + c + cols * jnp.arange(groups)[:, None]
     own_slots = own_small[:, :, block:block + slots].astype(jnp.int32)
     slot_of = jnp.sum(
@@ -275,20 +288,19 @@
         ],
         axis=1,
     ).reshape(-1)
-    scalars = jnp.concatenate([jnp.stack([(r % cols) ^ c, r // cols, op]), bounds]).astype(jnp.int32)
+    scalars = jnp.concatenate([jnp.stack([r, c, op]), bounds]).astype(jnp.int32)
 
     chosen = jnp.where(op == 0, lower_rhs, upper_rhs)
     chosen = lax.dynamic_slice_in_dim(chosen, (r // 2) * kept, kept, 0)
     chosen = chosen.reshape(kept, per_row, groups, block).transpose(1, 2, 0, 3).reshape(-1, block)
 
-    diag = prepare_diagonal((scalars, slot_of), dims, parts)
+    operator = load_operator(scalars, slot_of, dims, parts)
     run = functools.partial(
         step_kernel,
         dims=dims + (kept,),
         scalars=scalars,
         table=table,
-        parts=parts,
-        diag=diag,
+        operator=operator,
         level=level,
         pivot=pivot,
     )
@@ -305,9 +317,7 @@
     sol = run("last", steps - 1, state=(res, sol), received=exchange(sends))
 
     whole = jnp.stack([sol] + [xor_permute(sol, "col", d) for d in range(1, cols)])
-    for bit in bits_of(cols):
-        paired = whole.reshape(cols // (2 * bit), 2, bit, *sol.shape)
-        whole = jnp.where((c & bit) != 0, paired[:, ::-1], paired).reshape(cols, *sol.shape)
+    whole = flip_order(whole, c)
     whole = whole.reshape(cols, per_row, groups, kept, block).transpose(2, 0, 1, 3, 4)
     whole = whole.reshape(rows, per_row * kept, block)
     got = lax.all_to_all(whole, "row", 0, 0).reshape(rows // 2, 2, per_row, kept, block)

time: 248 us -> 211 us (0.85); the launches traced: 251 us -> 209 us
  Pallas kernels: 79.9 us -> 30.6 us
  waiting for transfers between devices: 75.1 us -> 90.9 us
  local copies, waits for them, and re-layouts: 14.9 us -> 3.48 us
    pallas_call x12, Pallas kernels: 75.5 us -> 27.2 us  [step_kernel(): pl.pallas_call(body, out_shape=out_shape, in_specs=[smem, smem] + [vmem]...]
    ppermute x53, waiting for transfers between devices: 75.1 us -> 90.9 us  [xor_permute(): return lax.ppermute(value, axis, [(i, i ^ distance) for i in range(size)])]
    unnamed x88 -> x2, local copies, waits for them, and re-layouts: 7.57 us -> 0.22 us
  transfers between devices with their start and end apart: 53 -> 53, of which waited for: 28 -> 31; matrix products, arithmetic and copies ran while one was open for 3% -> 4% of each run, Pallas kernels for 0% -> 0%
where the time goes in v2:
time: 211 us; the launch traced here: 209 us
  waiting for transfers between devices  90.9 us (43%)
  starting transfers between devices  67.4 us (32%)
  Pallas kernels  30.6 us (15%)
  blocking collectives  9.02 us (4%)
  other arithmetic  6.79 us (3%)
  local copies, waits for them, and re-layouts  3.48 us (2%)
    ppermute x53, waiting for transfers between devices, xor_permute(): return lax.ppermute(value, axis, [(i, i ^ distance) for i in range(size)])  90.9 us
    ppermute x53, starting transfers between devices, xor_permute(): return lax.ppermute(value, axis, [(i, i ^ distance) for i in range(size)])  67.4 us
    pallas_call x12, Pallas kernels, step_kernel(): pl.pallas_call(body, out_shape=out_shape, in_specs=[smem, smem] + [vmem]...  27.2 us
    all_to_all x1, blocking collectives, shards(): lax.all_to_all(whole, 'row', 0, 0)  9.02 us
  transfers between devices with their start and end apart: 53, of which 31 were waited for; matrix products, arithmetic and copies ran while one was open for 4% of the time, Pallas kernels for 0%

profile of v2, /device:TPU:0, one launch (start us, length us, event | category | flops | bytes accessed | tf_op | source)
XLA Modules:
  0.0 209.2 jit_solution(12528835028077069167)
XLA Ops:
  0.6 1.3 fusion.10
  2.5 2.6 %collective-permute-start.5 = (bf16[4,4,128,128]{3,2,1,0:T(8,128)(2,1)S(1)}, bf16[4,4,128,128]{3,2,1,0:T(8,128)(2,1)S(1)}, u32[]{:S(2)}, u32[]{:S(2)}) collective-permute-start(bf16[4,4,128,128]{3,2,1,0:T(8,128)(2,1)S(1)} %get-tuple-element.123.refs_2_), channel_id=1, source_target_pairs={{0,8},{4,12},{8,0},{12,4},{16,24},{20,28},{24,16},{28,20},{1,9},{5... | collective-permute-start | bytes 1572872 | tf_op jit(solution)/shard_map/ppermute | solution.py:13
  7.9 1.1 select_reduce_fusion.3
  10.3 1.8 collective-permute-start.1
  12.3 16.8 %collective-permute-done.1 = f32[2,8,256]{2,1,0:T(8,128)S(1)} collective-permute-done((f32[2,8,256]{2,1,0:T(8,128)S(1)}, f32[2,8,256]{2,1,0:T(8,128)S(1)}, u32[]{:S(2)}, u32[]{:S(2)}) %collective-permute-start.1) | collective-permute-done | bytes 16416 | tf_op jit(solution)/shard_map/ppermute | solution.py:13
  29.1 1.8 collective-permute-start.2
  31.0 2.0 collective-permute-done.2
  33.0 1.8 collective-permute-start.10
  35.2 1.8 collective-permute-start.13
  37.0 10.9 %collective-permute-done.10.refs_11_ = bf16[4,4,128,128]{3,2,1,0:T(8,128)(2,1)} collective-permute-done((bf16[4,4,128,128]{3,2,1,0:T(8,128)(2,1)S(1)}, bf16[4,4,128,128]{3,2,1,0:T(8,128)(2,1)}, u32[]{:S(2)}, u32[]{:S(2)}) %collective-permute-start.10) | collective-permute-done | bytes 524320 | tf_op jit(solution)/shard_map/ppermute | solution.py:13
  47.9 1.7 collective-permute-start.14
  49.8 1.9 select_reduce_fusion.1
  51.8 7.4 %collective-permute-done.9.refs_10_ = bf16[4,4,128,128]{3,2,1,0:T(8,128)(2,1)} collective-permute-done((bf16[4,4,128,128]{3,2,1,0:T(8,128)(2,1)S(1)}, bf16[4,4,128,128]{3,2,1,0:T(8,128)(2,1)}, u32[]{:S(2)}, u32[]{:S(2)}) %collective-permute-start.9) | collective-permute-done | bytes 524320 | tf_op jit(solution)/shard_map/ppermute | solution.py:13
  59.7 8.5 %collective-permute-done.13.refs_14_ = bf16[4,4,128,128]{3,2,1,0:T(8,128)(2,1)} collective-permute-done((bf16[4,4,128,128]{3,2,1,0:T(8,128)(2,1)S(1)}, bf16[4,4,128,128]{3,2,1,0:T(8,128)(2,1)}, u32[]{:S(2)}, u32[]{:S(2)}) %collective-permute-start.13) | collective-permute-done | bytes 524320 | tf_op jit(solution)/shard_map/ppermute | solution.py:13
  69.3 1.1 collective-permute-done.15.refs_16_
  71.1 3.5 %load_operator.1 = (bf16[8,8,4,128,128]{4,3,2,1,0:T(8,128)(2,1)S(1)}, bf16[2,8,128,128]{3,2,1,0:T(8,128)(2,1)S(1)}) custom-call(s32[27]{0:T(128)S(1)} %pad_add_fusion.1.refs_0_, s32[16]{0:T(128)S(1)} %reshape.342.refs_1_, bf16[4,4,128,128]{3,2,1,0:T(8,128)(2,1)S(1)} %get-tuple-element.123.refs_2_, bf16[4,4,128,128]{3,2,1,0:T(8,128)(2,1)S(1)} %get-tuple-element.122.refs_3_, ...), custom_call_target="tpu_custom_call" | custom-call | tf_op jit(solution)/shard_map/load_operator/pallas_call | solution.py:81
  74.7 3.4 %step_first.1 = (f32[64,128]{1,0:T(8,128)S(1)}, bf16[64,128]{1,0:T(8,128)(2,1)S(1)}, bf16[64,128]{1,0:T(8,128)(2,1)S(1)}, bf16[64,128]{1,0:T(8,128)(2,1)S(1)}, f32[64,128]{1,0:T(8,128)S(1)}) custom-call(s32[27]{0:T(128)S(1)} %pad_add_fusion.1.refs_0_, s32[256]{0:T(256)S(1)} %reshape.339.refs_1_, bf16[8,8,4,128,128]{4,3,2,1,0:T(8,128)(2,1)S(1)} %get-tuple-element.59.refs_2_, ...), custom_call_target="tpu_custom_call" | custom-call | tf_op jit(solution)/shard_map/step_first/pallas_call | solution.py:204
  78.0 1.6 collective-permute-start.17
  79.7 2.6 %collective-permute-start.18 = (bf16[64,128]{1,0:T(8,128)(2,1)S(1)}, bf16[64,128]{1,0:T(8,128)(2,1)S(1)}, u32[]{:S(2)}, u32[]{:S(2)}) collective-permute-start(bf16[64,128]{1,0:T(8,128)(2,1)S(1)} %get-tuple-element.64), channel_id=1, source_target_pairs={{0,2},{1,3},{2,0},{3,1},{4,6},{5,7},{6,4},{7,5},{8,10},{9,11},{10,... | collective-permute-start | bytes 49160 | tf_op jit(solution)/shard_map/ppermute | solution.py:13
  82.5 2.1 collective-permute-done.18.refs_10_
  84.6 3.2 %collective-permute-done.19.refs_11_ = bf16[64,128]{1,0:T(8,128)(2,1)S(1)} collective-permute-done((bf16[64,128]{1,0:T(8,128)(2,1)S(1)}, bf16[64,128]{1,0:T(8,128)(2,1)S(1)}, u32[]{:S(2)}, u32[]{:S(2)}) %collective-permute-start.19) | collective-permute-done | bytes 16416 | tf_op jit(solution)/shard_map/ppermute | solution.py:13
  87.8 4.1 %step_solved.5 = (f32[64,128]{1,0:T(8,128)S(1)}, bf16[64,128]{1,0:T(8,128)(2,1)S(1)}, bf16[64,128]{1,0:T(8,128)(2,1)S(1)}, bf16[64,128]{1,0:T(8,128)(2,1)S(1)}, f32[64,128]{1,0:T(8,128)S(1)}) custom-call(s32[27]{0:T(128)S(1)} %pad_add_fusion.1.refs_0_, s32[256]{0:T(256)S(1)} %reshape.339.refs_1_, bf16[8,8,4,128,128]{4,3,2,1,0:T(8,128)(2,1)S(1)} %get-tuple-element.59.refs_2_, ...), custom_call_target="tpu_custom_call" | custom-call | tf_op jit(solution)/shard_map/step_solved/pallas_call | solution.py:204
  91.9 0.8 collective-permute-start.21
  92.7 3.6 %collective-permute-start.22 = (bf16[64,128]{1,0:T(8,128)(2,1)S(1)}, bf16[64,128]{1,0:T(8,128)(2,1)S(1)}, u32[]{:S(2)}, u32[]{:S(2)}) collective-permute-start(bf16[64,128]{1,0:T(8,128)(2,1)S(1)} %get-tuple-element.70), channel_id=1, source_target_pairs={{0,3},{1,2},{2,1},{3,0},{4,7},{5,6},{6,5},{7,4},{8,11},{9,10},{10,... | collective-permute-start | bytes 49160 | tf_op jit(solution)/shard_map/ppermute | solution.py:13
  96.6 1.6 collective-permute-done.22.refs_11_
  98.3 2.0 step_updated.5
  100.6 3.8 %collective-permute-start.24 = (bf16[64,128]{1,0:T(8,128)(2,1)S(1)}, bf16[64,128]{1,0:T(8,128)(2,1)S(1)}, u32[]{:S(2)}, u32[]{:S(2)}) collective-permute-start(bf16[64,128]{1,0:T(8,128)(2,1)S(1)} %get-tuple-element.74), channel_id=1, source_target_pairs={{0,2},{1,3},{2,0},{3,1},{4,6},{5,7},{6,4},{7,5},{8,10},{9,11},{10,... | collective-permute-start | bytes 49160 | tf_op jit(solution)/shard_map/ppermute | solution.py:13
  104.7 1.5 collective-permute-done.24.refs_10_
  106.2 3.8 %collective-permute-done.25.refs_11_ = bf16[64,128]{1,0:T(8,128)(2,1)S(1)} collective-permute-done((bf16[64,128]{1,0:T(8,128)(2,1)S(1)}, bf16[64,128]{1,0:T(8,128)(2,1)S(1)}, u32[]{:S(2)}, u32[]{:S(2)}) %collective-permute-start.25) | collective-permute-done | bytes 16416 | tf_op jit(solution)/shard_map/ppermute | solution.py:13
  110.0 3.4 %step_solved.6 = (f32[64,128]{1,0:T(8,128)S(1)}, bf16[64,128]{1,0:T(8,128)(2,1)S(1)}, bf16[64,128]{1,0:T(8,128)(2,1)S(1)}, bf16[64,128]{1,0:T(8,128)(2,1)S(1)}, f32[64,128]{1,0:T(8,128)S(1)}) custom-call(s32[27]{0:T(128)S(1)} %pad_add_fusion.1.refs_0_, s32[256]{0:T(256)S(1)} %reshape.339.refs_1_, bf16[8,8,4,128,128]{4,3,2,1,0:T(8,128)(2,1)S(1)} %get-tuple-element.59.refs_2_, ...), custom_call_target="tpu_custom_call" | custom-call | tf_op jit(solution)/shard_map/step_solved/pallas_call | solution.py:204
  113.5 0.8 collective-permute-start.27
  114.3 3.6 %collective-permute-start.28 = (bf16[64,128]{1,0:T(8,128)(2,1)S(1)}, bf16[64,128]{1,0:T(8,128)(2,1)S(1)}, u32[]{:S(2)}, u32[]{:S(2)}) collective-permute-start(bf16[64,128]{1,0:T(8,128)(2,1)S(1)} %get-tuple-element.80), channel_id=1, source_target_pairs={{0,3},{1,2},{2,1},{3,0},{4,7},{5,6},{6,5},{7,4},{8,11},{9,10},{10,... | collective-permute-start | bytes 49160 | tf_op jit(solution)/shard_map/ppermute | solution.py:13
  118.2 1.7 collective-permute-done.28.refs_11_
  119.8 2.0 step_updated.6
  122.2 3.8 %collective-permute-start.30 = (bf16[64,128]{1,0:T(8,128)(2,1)S(1)}, bf16[64,128]{1,0:T(8,128)(2,1)S(1)}, u32[]{:S(2)}, u32[]{:S(2)}) collective-permute-start(bf16[64,128]{1,0:T(8,128)(2,1)S(1)} %get-tuple-element.84), channel_id=1, source_target_pairs={{0,2},{1,3},{2,0},{3,1},{4,6},{5,7},{6,4},{7,5},{8,10},{9,11},{10,... | collective-permute-start | bytes 49160 | tf_op jit(solution)/shard_map/ppermute | solution.py:13
  126.2 1.4 collective-permute-done.30.refs_10_
  127.7 3.8 %collective-permute-done.31.refs_11_ = bf16[64,128]{1,0:T(8,128)(2,1)S(1)} collective-permute-done((bf16[64,128]{1,0:T(8,128)(2,1)S(1)}, bf16[64,128]{1,0:T(8,128)(2,1)S(1)}, u32[]{:S(2)}, u32[]{:S(2)}) %collective-permute-start.31) | collective-permute-done | bytes 16416 | tf_op jit(solution)/shard_map/ppermute | solution.py:13
  131.5 2.7 %step_solved.7 = (f32[64,128]{1,0:T(8,128)S(1)}, bf16[64,128]{1,0:T(8,128)(2,1)S(1)}, bf16[64,128]{1,0:T(8,128)(2,1)S(1)}, bf16[64,128]{1,0:T(8,128)(2,1)S(1)}, f32[64,128]{1,0:T(8,128)S(1)}) custom-call(s32[27]{0:T(128)S(1)} %pad_add_fusion.1.refs_0_, s32[256]{0:T(256)S(1)} %reshape.339.refs_1_, bf16[8,8,4,128,128]{4,3,2,1,0:T(8,128)(2,1)S(1)} %get-tuple-element.59.refs_2_, ...), custom_call_target="tpu_custom_call" | custom-call | tf_op jit(solution)/shard_map/step_solved/pallas_call | solution.py:204
  134.3 0.8 collective-permute-start.33
  135.1 3.6 %collective-permute-start.34 = (bf16[64,128]{1,0:T(8,128)(2,1)S(1)}, bf16[64,128]{1,0:T(8,128)(2,1)S(1)}, u32[]{:S(2)}, u32[]{:S(2)}) collective-permute-start(bf16[64,128]{1,0:T(8,128)(2,1)S(1)} %get-tuple-element.90), channel_id=1, source_target_pairs={{0,3},{1,2},{2,1},{3,0},{4,7},{5,6},{6,5},{7,4},{8,11},{9,10},{10,... | collective-permute-start | bytes 49160 | tf_op jit(solution)/shard_map/ppermute | solution.py:13
  139.0 1.7 collective-permute-done.34.refs_11_
  140.6 1.3 step_updated.7
  142.3 3.8 %collective-permute-start.36 = (bf16[64,128]{1,0:T(8,128)(2,1)S(1)}, bf16[64,128]{1,0:T(8,128)(2,1)S(1)}, u32[]{:S(2)}, u32[]{:S(2)}) collective-permute-start(bf16[64,128]{1,0:T(8,128)(2,1)S(1)} %get-tuple-element.94), channel_id=1, source_target_pairs={{0,2},{1,3},{2,0},{3,1},{4,6},{5,7},{6,4},{7,5},{8,10},{9,11},{10,... | collective-permute-start | bytes 49160 | tf_op jit(solution)/shard_map/ppermute | solution.py:13
  146.4 1.4 collective-permute-done.36.refs_10_
  147.8 3.8 %collective-permute-done.37.refs_11_ = bf16[64,128]{1,0:T(8,128)(2,1)S(1)} collective-permute-done((bf16[64,128]{1,0:T(8,128)(2,1)S(1)}, bf16[64,128]{1,0:T(8,128)(2,1)S(1)}, u32[]{:S(2)}, u32[]{:S(2)}) %collective-permute-start.37) | collective-permute-done | bytes 16416 | tf_op jit(solution)/shard_map/ppermute | solution.py:13
  151.6 2.7 %step_solved.8 = (f32[64,128]{1,0:T(8,128)S(1)}, bf16[64,128]{1,0:T(8,128)(2,1)S(1)}, bf16[64,128]{1,0:T(8,128)(2,1)S(1)}, bf16[64,128]{1,0:T(8,128)(2,1)S(1)}, f32[64,128]{1,0:T(8,128)S(1)}) custom-call(s32[27]{0:T(128)S(1)} %pad_add_fusion.1.refs_0_, s32[256]{0:T(256)S(1)} %reshape.339.refs_1_, bf16[8,8,4,128,128]{4,3,2,1,0:T(8,128)(2,1)S(1)} %get-tuple-element.59.refs_2_, ...), custom_call_target="tpu_custom_call" | custom-call | tf_op jit(solution)/shard_map/step_solved/pallas_call | solution.py:204
  154.4 0.8 collective-permute-start.39
  155.2 3.5 %collective-permute-start.40 = (bf16[64,128]{1,0:T(8,128)(2,1)S(1)}, bf16[64,128]{1,0:T(8,128)(2,1)S(1)}, u32[]{:S(2)}, u32[]{:S(2)}) collective-permute-start(bf16[64,128]{1,0:T(8,128)(2,1)S(1)} %get-tuple-element.100), channel_id=1, source_target_pairs={{0,3},{1,2},{2,1},{3,0},{4,7},{5,6},{6,5},{7,4},{8,11},{9,10},{10,... | collective-permute-start | bytes 49160 | tf_op jit(solution)/shard_map/ppermute | solution.py:13
  159.1 1.7 collective-permute-done.40.refs_11_
  160.8 2.7 %step_updated.8 = (f32[64,128]{1,0:T(8,128)S(1)}, bf16[64,128]{1,0:T(8,128)(2,1)S(1)}, bf16[64,128]{1,0:T(8,128)(2,1)S(1)}, bf16[64,128]{1,0:T(8,128)(2,1)S(1)}, f32[64,128]{1,0:T(8,128)S(1)}) custom-call(s32[27]{0:T(128)S(1)} %pad_add_fusion.1.refs_0_, s32[256]{0:T(256)S(1)} %reshape.339.refs_1_, ...), custom_call_target="tpu_custom_call" | custom-call | tf_op jit(solution)/shard_map/step_updated/pallas_call | solution.py:204
  163.8 3.8 %collective-permute-start.42 = (bf16[64,128]{1,0:T(8,128)(2,1)S(1)}, bf16[64,128]{1,0:T(8,128)(2,1)S(1)}, u32[]{:S(2)}, u32[]{:S(2)}) collective-permute-start(bf16[64,128]{1,0:T(8,128)(2,1)S(1)} %get-tuple-element.104), channel_id=1, source_target_pairs={{0,2},{1,3},{2,0},{3,1},{4,6},{5,7},{6,4},{7,5},{8,10},{9,11},{10,... | collective-permute-start | bytes 49160 | tf_op jit(solution)/shard_map/ppermute | solution.py:13
  167.9 1.5 collective-permute-done.42.refs_10_
  169.4 3.8 %collective-permute-done.43.refs_11_ = bf16[64,128]{1,0:T(8,128)(2,1)S(1)} collective-permute-done((bf16[64,128]{1,0:T(8,128)(2,1)S(1)}, bf16[64,128]{1,0:T(8,128)(2,1)S(1)}, u32[]{:S(2)}, u32[]{:S(2)}) %collective-permute-start.43) | collective-permute-done | bytes 16416 | tf_op jit(solution)/shard_map/ppermute | solution.py:13
  173.2 1.3 step_solved.9
  174.5 0.8 collective-permute-start.45
  175.3 3.6 %collective-permute-start.46 = (bf16[64,128]{1,0:T(8,128)(2,1)S(1)}, bf16[64,128]{1,0:T(8,128)(2,1)S(1)}, u32[]{:S(2)}, u32[]{:S(2)}) collective-permute-start(bf16[64,128]{1,0:T(8,128)(2,1)S(1)} %get-tuple-element.110), channel_id=1, source_target_pairs={{0,3},{1,2},{2,1},{3,0},{4,7},{5,6},{6,5},{7,4},{8,11},{9,10},{10,... | collective-permute-start | bytes 49160 | tf_op jit(solution)/shard_map/ppermute | solution.py:13
  179.2 1.7 collective-permute-done.46.refs_11_
  180.9 1.3 step_updated.9
  182.5 3.8 %collective-permute-start.48 = (bf16[64,128]{1,0:T(8,128)(2,1)S(1)}, bf16[64,128]{1,0:T(8,128)(2,1)S(1)}, u32[]{:S(2)}, u32[]{:S(2)}) collective-permute-start(bf16[64,128]{1,0:T(8,128)(2,1)S(1)} %get-tuple-element.114), channel_id=1, source_target_pairs={{0,2},{1,3},{2,0},{3,1},{4,6},{5,7},{6,4},{7,5},{8,10},{9,11},{10,... | collective-permute-start | bytes 49160 | tf_op jit(solution)/shard_map/ppermute | solution.py:13
  186.6 2.0 collective-permute-done.48.refs_8_
  188.6 3.3 %collective-permute-done.49.refs_9_ = bf16[64,128]{1,0:T(8,128)(2,1)S(1)} collective-permute-done((bf16[64,128]{1,0:T(8,128)(2,1)S(1)}, bf16[64,128]{1,0:T(8,128)(2,1)S(1)}, u32[]{:S(2)}, u32[]{:S(2)}) %collective-permute-start.49) | collective-permute-done | bytes 16416 | tf_op jit(solution)/shard_map/ppermute | solution.py:13
  192.8 4.1 %collective-permute-start.50 = (f32[64,128]{1,0:T(8,128)S(1)}, f32[64,128]{1,0:T(8,128)S(1)}, u32[]{:S(2)}, u32[]{:S(2)}) collective-permute-start(f32[64,128]{1,0:T(8,128)S(1)} %step_last.1), channel_id=1, source_target_pairs={{0,1},{1,0},{2,3},{3,2},{4,5},{5,4},{6,7},{7,6},{8,9},{9,8},{10,11... | collective-permute-start | bytes 98312 | tf_op jit(solution)/shard_map/ppermute | solution.py:13
  196.9 1.3 collective-permute-done.52
  198.9 9.0 %all_to_all.5 = f32[8,32,128]{2,1,0:T(8,128)S(1)} all-to-all(f32[8,32,128]{2,1,0:T(8,128)S(1)} %bitcast.97), channel_id=1, replica_groups=mesh['row'=8,'col'=4] {'row'}, dimensions={0} | all-to-all | bytes 262144 | tf_op jit(solution)/shard_map/all_to_all | solution.py:323
  (105 shorter events, 16.2 us)
Async XLA Ops:
  1.9 32.9 %collective-permute-start.3 = (bf16[4,4,128,128]{3,2,1,0:T(8,128)(2,1)S(1)}, bf16[4,4,128,128]{3,2,1,0:T(8,128)(2,1)S(1)}, u32[]{:S(2)}, u32[]{:S(2)}) collective-permute-start(bf16[4,4,128,128]{3,2,1,0:T(8,128)(2,1)S(1)} %get-tuple-element.123.refs_2_), channel_id=1, source_target_pairs={{0,4},{4,0},{8,12},{12,8},{16,20},{20,16},{24,28},{28,24},{1,5},{5... | collective-permute-start | bytes 1572872 | tf_op jit(solution)/shard_map/ppermute | solution.py:13
  2.5 32.7 %collective-permute-start.5 = (bf16[4,4,128,128]{3,2,1,0:T(8,128)(2,1)S(1)}, bf16[4,4,128,128]{3,2,1,0:T(8,128)(2,1)S(1)}, u32[]{:S(2)}, u32[]{:S(2)}) collective-permute-start(bf16[4,4,128,128]{3,2,1,0:T(8,128)(2,1)S(1)} %get-tuple-element.123.refs_2_), channel_id=1, source_target_pairs={{0,8},{4,12},{8,0},{12,4},{16,24},{20,28},{24,16},{28,20},{1,9},{5... | collective-permute-start | bytes 1572872 | tf_op jit(solution)/shard_map/ppermute | solution.py:13
  5.0 30.2 %collective-permute-start.4 = (bf16[4,4,128,128]{3,2,1,0:T(8,128)(2,1)S(1)}, bf16[4,4,128,128]{3,2,1,0:T(8,128)(2,1)S(1)}, u32[]{:S(2)}, u32[]{:S(2)}) collective-permute-start(bf16[4,4,128,128]{3,2,1,0:T(8,128)(2,1)S(1)} %get-tuple-element.122.refs_3_), channel_id=1, source_target_pairs={{0,4},{4,0},{8,12},{12,8},{16,20},{20,16},{24,28},{28,24},{1,5},{5... | collective-permute-start | bytes 1572872 | tf_op jit(solution)/shard_map/ppermute | solution.py:13
  5.2 46.6 %collective-permute-start.6 = (bf16[4,4,128,128]{3,2,1,0:T(8,128)(2,1)S(1)}, bf16[4,4,128,128]{3,2,1,0:T(8,128)(2,1)S(1)}, u32[]{:S(2)}, u32[]{:S(2)}) collective-permute-start(bf16[4,4,128,128]{3,2,1,0:T(8,128)(2,1)S(1)} %get-tuple-element.122.refs_3_), channel_id=1, source_target_pairs={{0,8},{4,12},{8,0},{12,4},{16,24},{20,28},{24,16},{28,20},{1,9},{5... | collective-permute-start | bytes 1572872 | tf_op jit(solution)/shard_map/ppermute | solution.py:13
  6.9 3.4 %collective-permute-start = (f32[1,8,256]{2,1,0:T(8,128)S(1)}, f32[1,8,256]{2,1,0:T(8,128)S(1)}, u32[]{:S(2)}, u32[]{:S(2)}) collective-permute-start(f32[1,8,256]{2,1,0:T(8,128)S(1)} %fusion.7), channel_id=1, source_target_pairs={{0,4},{4,0},{8,12},{12,8},{16,20},{20,16},{24,28},{28,24},{1,5},{5... | collective-permute-start | bytes 24584 | tf_op jit(solution)/shard_map/ppermute | solution.py:13
  10.3 18.8 %collective-permute-start.1 = (f32[2,8,256]{2,1,0:T(8,128)S(1)}, f32[2,8,256]{2,1,0:T(8,128)S(1)}, u32[]{:S(2)}, u32[]{:S(2)}) collective-permute-start(f32[2,8,256]{2,1,0:T(8,128)S(1)} %pad_maximum_fusion.3), channel_id=1, source_target_pairs={{0,8},{4,12},{8,0},{12,4},{16,24},{20,28},{24,16},{28,20},{1,9},{5... | collective-permute-start | bytes 49160 | tf_op jit(solution)/shard_map/ppermute | solution.py:13
  29.1 3.9 %collective-permute-start.2 = (f32[4,8,256]{2,1,0:T(8,128)S(1)}, f32[4,8,256]{2,1,0:T(8,128)S(1)}, u32[]{:S(2)}, u32[]{:S(2)}) collective-permute-start(f32[4,8,256]{2,1,0:T(8,128)S(1)} %pad_maximum_fusion.2), channel_id=1, source_target_pairs={{0,16},{4,20},{8,24},{12,28},{16,0},{20,4},{24,8},{28,12},{1,17},{... | collective-permute-start | bytes 98312 | tf_op jit(solution)/shard_map/ppermute | solution.py:13
  33.0 14.9 %collective-permute-start.10 = (bf16[4,4,128,128]{3,2,1,0:T(8,128)(2,1)S(1)}, bf16[4,4,128,128]{3,2,1,0:T(8,128)(2,1)}, u32[]{:S(2)}, u32[]{:S(2)}) collective-permute-start(bf16[4,4,128,128]{3,2,1,0:T(8,128)(2,1)S(1)} %get-tuple-element.122.refs_3_), channel_id=1, source_target_pairs={{0,16},{4,20},{8,24},{12,28},{16,0},{20,4},{24,8},{28,12},{1,17},{... | collective-permute-start | bytes 1572872 | tf_op jit(solution)/shard_map/ppermute | solution.py:13
  34.9 24.3 %collective-permute-start.9 = (bf16[4,4,128,128]{3,2,1,0:T(8,128)(2,1)S(1)}, bf16[4,4,128,128]{3,2,1,0:T(8,128)(2,1)}, u32[]{:S(2)}, u32[]{:S(2)}) collective-permute-start(bf16[4,4,128,128]{3,2,1,0:T(8,128)(2,1)S(1)} %get-tuple-element.123.refs_2_), channel_id=1, source_target_pairs={{0,16},{4,20},{8,24},{12,28},{16,0},{20,4},{24,8},{28,12},{1,17},{... | collective-permute-start | bytes 1572872 | tf_op jit(solution)/shard_map/ppermute | solution.py:13
  35.2 24.0 %collective-permute-start.7 = (bf16[4,4,128,128]{3,2,1,0:T(8,128)(2,1)S(1)}, bf16[4,4,128,128]{3,2,1,0:T(8,128)(2,1)}, u32[]{:S(2)}, u32[]{:S(2)}) collective-permute-start(bf16[4,4,128,128]{3,2,1,0:T(8,128)(2,1)S(1)} %collective-permute-done.5.refs_6_), channel_id=1, source_target_pairs={{0,4},{4,0},{8,12},{12,8},{16,20},{20,16},{24,28},{28,24},{1,5},{5... | collective-permute-start | bytes 1572872 | tf_op jit(solution)/shard_map/ppermute | solution.py:13
  35.2 33.0 %collective-permute-start.13 = (bf16[4,4,128,128]{3,2,1,0:T(8,128)(2,1)S(1)}, bf16[4,4,128,128]{3,2,1,0:T(8,128)(2,1)}, u32[]{:S(2)}, u32[]{:S(2)}) collective-permute-start(bf16[4,4,128,128]{3,2,1,0:T(8,128)(2,1)S(1)} %collective-permute-done.5.refs_6_), channel_id=1, source_target_pairs={{0,16},{4,20},{8,24},{12,28},{16,0},{20,4},{24,8},{28,12},{1,17},{... | collective-permute-start | bytes 1572872 | tf_op jit(solution)/shard_map/ppermute | solution.py:13
  47.9 20.2 %collective-permute-start.14 = (bf16[4,4,128,128]{3,2,1,0:T(8,128)(2,1)}, bf16[4,4,128,128]{3,2,1,0:T(8,128)(2,1)}, u32[]{:S(2)}, u32[]{:S(2)}) collective-permute-start(bf16[4,4,128,128]{3,2,1,0:T(8,128)(2,1)} %collective-permute-done.10.refs_11_), channel_id=1, source_target_pairs={{0,8},{4,12},{8,0},{12,4},{16,24},{20,28},{24,16},{28,20},{1,9},{5... | collective-permute-start | bytes 1572872 | tf_op jit(solution)/shard_map/ppermute | solution.py:13
  51.7 17.5 %collective-permute-start.12 = (bf16[4,4,128,128]{3,2,1,0:T(8,128)(2,1)}, bf16[4,4,128,128]{3,2,1,0:T(8,128)(2,1)}, u32[]{:S(2)}, u32[]{:S(2)}) collective-permute-start(bf16[4,4,128,128]{3,2,1,0:T(8,128)(2,1)} %collective-permute-done.10.refs_11_), channel_id=1, source_target_pairs={{0,4},{4,0},{8,12},{12,8},{16,20},{20,16},{24,28},{28,24},{1,5},{5... | collective-permute-start | bytes 1572872 | tf_op jit(solution)/shard_map/ppermute | solution.py:13
  59.2 10.1 %collective-permute-start.8 = (bf16[4,4,128,128]{3,2,1,0:T(8,128)(2,1)S(1)}, bf16[4,4,128,128]{3,2,1,0:T(8,128)(2,1)}, u32[]{:S(2)}, u32[]{:S(2)}) collective-permute-start(bf16[4,4,128,128]{3,2,1,0:T(8,128)(2,1)S(1)} %collective-permute-done.6.refs_7_), channel_id=1, source_target_pairs={{0,4},{4,0},{8,12},{12,8},{16,20},{20,16},{24,28},{28,24},{1,5},{5... | collective-permute-start | bytes 1572872 | tf_op jit(solution)/shard_map/ppermute | solution.py:13
  59.2 10.1 %collective-permute-start.11 = (bf16[4,4,128,128]{3,2,1,0:T(8,128)(2,1)}, bf16[4,4,128,128]{3,2,1,0:T(8,128)(2,1)}, u32[]{:S(2)}, u32[]{:S(2)}) collective-permute-start(bf16[4,4,128,128]{3,2,1,0:T(8,128)(2,1)} %collective-permute-done.9.refs_10_), channel_id=1, source_target_pairs={{0,4},{4,0},{8,12},{12,8},{16,20},{20,16},{24,28},{28,24},{1,5},{5... | collective-permute-start | bytes 1572872 | tf_op jit(solution)/shard_map/ppermute | solution.py:13
  68.1 2.3 %collective-permute-start.15 = (bf16[4,4,128,128]{3,2,1,0:T(8,128)(2,1)}, bf16[4,4,128,128]{3,2,1,0:T(8,128)(2,1)}, u32[]{:S(2)}, u32[]{:S(2)}) collective-permute-start(bf16[4,4,128,128]{3,2,1,0:T(8,128)(2,1)} %collective-permute-done.13.refs_14_), channel_id=1, source_target_pairs={{0,4},{4,0},{8,12},{12,8},{16,20},{20,16},{24,28},{28,24},{1,5},{5... | collective-permute-start | bytes 1572872 | tf_op jit(solution)/shard_map/ppermute | solution.py:13
  68.2 3.0 %collective-permute-start.16 = (bf16[4,4,128,128]{3,2,1,0:T(8,128)(2,1)}, bf16[4,4,128,128]{3,2,1,0:T(8,128)(2,1)}, u32[]{:S(2)}, u32[]{:S(2)}) collective-permute-start(bf16[4,4,128,128]{3,2,1,0:T(8,128)(2,1)} %collective-permute-done.14.refs_15_), channel_id=1, source_target_pairs={{0,4},{4,0},{8,12},{12,8},{16,20},{20,16},{24,28},{28,24},{1,5},{5... | collective-permute-start | bytes 1572872 | tf_op jit(solution)/shard_map/ppermute | solution.py:13
  78.0 4.5 %collective-permute-start.17 = (bf16[64,128]{1,0:T(8,128)(2,1)S(1)}, bf16[64,128]{1,0:T(8,128)(2,1)S(1)}, u32[]{:S(2)}, u32[]{:S(2)}) collective-permute-start(bf16[64,128]{1,0:T(8,128)(2,1)S(1)} %get-tuple-element.63), channel_id=1, source_target_pairs={{0,1},{1,0},{2,3},{3,2},{4,5},{5,4},{6,7},{7,6},{8,9},{9,8},{10,11... | collective-permute-start | bytes 49160 | tf_op jit(solution)/shard_map/ppermute | solution.py:13
  79.7 4.9 %collective-permute-start.18 = (bf16[64,128]{1,0:T(8,128)(2,1)S(1)}, bf16[64,128]{1,0:T(8,128)(2,1)S(1)}, u32[]{:S(2)}, u32[]{:S(2)}) collective-permute-start(bf16[64,128]{1,0:T(8,128)(2,1)S(1)} %get-tuple-element.64), channel_id=1, source_target_pairs={{0,2},{1,3},{2,0},{3,1},{4,6},{5,7},{6,4},{7,5},{8,10},{9,11},{10,... | collective-permute-start | bytes 49160 | tf_op jit(solution)/shard_map/ppermute | solution.py:13
  82.3 5.5 %collective-permute-start.19 = (bf16[64,128]{1,0:T(8,128)(2,1)S(1)}, bf16[64,128]{1,0:T(8,128)(2,1)S(1)}, u32[]{:S(2)}, u32[]{:S(2)}) collective-permute-start(bf16[64,128]{1,0:T(8,128)(2,1)S(1)} %get-tuple-element.65), channel_id=1, source_target_pairs={{0,3},{1,2},{2,1},{3,0},{4,7},{5,6},{6,5},{7,4},{8,11},{9,10},{10,... | collective-permute-start | bytes 49160 | tf_op jit(solution)/shard_map/ppermute | solution.py:13
  91.9 4.5 %collective-permute-start.20 = (bf16[64,128]{1,0:T(8,128)(2,1)S(1)}, bf16[64,128]{1,0:T(8,128)(2,1)S(1)}, u32[]{:S(2)}, u32[]{:S(2)}) collective-permute-start(bf16[64,128]{1,0:T(8,128)(2,1)S(1)} %get-tuple-element.68), channel_id=1, source_target_pairs={{0,1},{1,0},{2,3},{3,2},{4,5},{5,4},{6,7},{7,6},{8,9},{9,8},{10,11... | collective-permute-start | bytes 49160 | tf_op jit(solution)/shard_map/ppermute | solution.py:13
  91.9 4.7 %collective-permute-start.21 = (bf16[64,128]{1,0:T(8,128)(2,1)S(1)}, bf16[64,128]{1,0:T(8,128)(2,1)S(1)}, u32[]{:S(2)}, u32[]{:S(2)}) collective-permute-start(bf16[64,128]{1,0:T(8,128)(2,1)S(1)} %get-tuple-element.69), channel_id=1, source_target_pairs={{0,2},{1,3},{2,0},{3,1},{4,6},{5,7},{6,4},{7,5},{8,10},{9,11},{10,... | collective-permute-start | bytes 49160 | tf_op jit(solution)/shard_map/ppermute | solution.py:13
  92.7 5.5 %collective-permute-start.22 = (bf16[64,128]{1,0:T(8,128)(2,1)S(1)}, bf16[64,128]{1,0:T(8,128)(2,1)S(1)}, u32[]{:S(2)}, u32[]{:S(2)}) collective-permute-start(bf16[64,128]{1,0:T(8,128)(2,1)S(1)} %get-tuple-element.70), channel_id=1, source_target_pairs={{0,3},{1,2},{2,1},{3,0},{4,7},{5,6},{6,5},{7,4},{8,11},{9,10},{10,... | collective-permute-start | bytes 49160 | tf_op jit(solution)/shard_map/ppermute | solution.py:13
  100.3 4.5 %collective-permute-start.23 = (bf16[64,128]{1,0:T(8,128)(2,1)S(1)}, bf16[64,128]{1,0:T(8,128)(2,1)S(1)}, u32[]{:S(2)}, u32[]{:S(2)}) collective-permute-start(bf16[64,128]{1,0:T(8,128)(2,1)S(1)} %get-tuple-element.73), channel_id=1, source_target_pairs={{0,1},{1,0},{2,3},{3,2},{4,5},{5,4},{6,7},{7,6},{8,9},{9,8},{10,11... | collective-permute-start | bytes 49160 | tf_op jit(solution)/shard_map/ppermute | solution.py:13
  100.6 5.5 %collective-permute-start.24 = (bf16[64,128]{1,0:T(8,128)(2,1)S(1)}, bf16[64,128]{1,0:T(8,128)(2,1)S(1)}, u32[]{:S(2)}, u32[]{:S(2)}) collective-permute-start(bf16[64,128]{1,0:T(8,128)(2,1)S(1)} %get-tuple-element.74), channel_id=1, source_target_pairs={{0,2},{1,3},{2,0},{3,1},{4,6},{5,7},{6,4},{7,5},{8,10},{9,11},{10,... | collective-permute-start | bytes 49160 | tf_op jit(solution)/shard_map/ppermute | solution.py:13
  104.5 5.5 %collective-permute-start.25 = (bf16[64,128]{1,0:T(8,128)(2,1)S(1)}, bf16[64,128]{1,0:T(8,128)(2,1)S(1)}, u32[]{:S(2)}, u32[]{:S(2)}) collective-permute-start(bf16[64,128]{1,0:T(8,128)(2,1)S(1)} %get-tuple-element.75), channel_id=1, source_target_pairs={{0,3},{1,2},{2,1},{3,0},{4,7},{5,6},{6,5},{7,4},{8,11},{9,10},{10,... | collective-permute-start | bytes 49160 | tf_op jit(solution)/shard_map/ppermute | solution.py:13
  113.4 4.5 %collective-permute-start.26 = (bf16[64,128]{1,0:T(8,128)(2,1)S(1)}, bf16[64,128]{1,0:T(8,128)(2,1)S(1)}, u32[]{:S(2)}, u32[]{:S(2)}) collective-permute-start(bf16[64,128]{1,0:T(8,128)(2,1)S(1)} %get-tuple-element.78), channel_id=1, source_target_pairs={{0,1},{1,0},{2,3},{3,2},{4,5},{5,4},{6,7},{7,6},{8,9},{9,8},{10,11... | collective-permute-start | bytes 49160 | tf_op jit(solution)/shard_map/ppermute | solution.py:13
  113.5 4.7 %collective-permute-start.27 = (bf16[64,128]{1,0:T(8,128)(2,1)S(1)}, bf16[64,128]{1,0:T(8,128)(2,1)S(1)}, u32[]{:S(2)}, u32[]{:S(2)}) collective-permute-start(bf16[64,128]{1,0:T(8,128)(2,1)S(1)} %get-tuple-element.79), channel_id=1, source_target_pairs={{0,2},{1,3},{2,0},{3,1},{4,6},{5,7},{6,4},{7,5},{8,10},{9,11},{10,... | collective-permute-start | bytes 49160 | tf_op jit(solution)/shard_map/ppermute | solution.py:13
  114.3 5.5 %collective-permute-start.28 = (bf16[64,128]{1,0:T(8,128)(2,1)S(1)}, bf16[64,128]{1,0:T(8,128)(2,1)S(1)}, u32[]{:S(2)}, u32[]{:S(2)}) collective-permute-start(bf16[64,128]{1,0:T(8,128)(2,1)S(1)} %get-tuple-element.80), channel_id=1, source_target_pairs={{0,3},{1,2},{2,1},{3,0},{4,7},{5,6},{6,5},{7,4},{8,11},{9,10},{10,... | collective-permute-start | bytes 49160 | tf_op jit(solution)/shard_map/ppermute | solution.py:13
  121.8 4.5 %collective-permute-start.29 = (bf16[64,128]{1,0:T(8,128)(2,1)S(1)}, bf16[64,128]{1,0:T(8,128)(2,1)S(1)}, u32[]{:S(2)}, u32[]{:S(2)}) collective-permute-start(bf16[64,128]{1,0:T(8,128)(2,1)S(1)} %get-tuple-element.83), channel_id=1, source_target_pairs={{0,1},{1,0},{2,3},{3,2},{4,5},{5,4},{6,7},{7,6},{8,9},{9,8},{10,11... | collective-permute-start | bytes 49160 | tf_op jit(solution)/shard_map/ppermute | solution.py:13
  122.2 5.5 %collective-permute-start.30 = (bf16[64,128]{1,0:T(8,128)(2,1)S(1)}, bf16[64,128]{1,0:T(8,128)(2,1)S(1)}, u32[]{:S(2)}, u32[]{:S(2)}) collective-permute-start(bf16[64,128]{1,0:T(8,128)(2,1)S(1)} %get-tuple-element.84), channel_id=1, source_target_pairs={{0,2},{1,3},{2,0},{3,1},{4,6},{5,7},{6,4},{7,5},{8,10},{9,11},{10,... | collective-permute-start | bytes 49160 | tf_op jit(solution)/shard_map/ppermute | solution.py:13
  126.0 5.5 %collective-permute-start.31 = (bf16[64,128]{1,0:T(8,128)(2,1)S(1)}, bf16[64,128]{1,0:T(8,128)(2,1)S(1)}, u32[]{:S(2)}, u32[]{:S(2)}) collective-permute-start(bf16[64,128]{1,0:T(8,128)(2,1)S(1)} %get-tuple-element.85), channel_id=1, source_target_pairs={{0,3},{1,2},{2,1},{3,0},{4,7},{5,6},{6,5},{7,4},{8,11},{9,10},{10,... | collective-permute-start | bytes 49160 | tf_op jit(solution)/shard_map/ppermute | solution.py:13
  134.2 4.5 %collective-permute-start.32 = (bf16[64,128]{1,0:T(8,128)(2,1)S(1)}, bf16[64,128]{1,0:T(8,128)(2,1)S(1)}, u32[]{:S(2)}, u32[]{:S(2)}) collective-permute-start(bf16[64,128]{1,0:T(8,128)(2,1)S(1)} %get-tuple-element.88), channel_id=1, source_target_pairs={{0,1},{1,0},{2,3},{3,2},{4,5},{5,4},{6,7},{7,6},{8,9},{9,8},{10,11... | collective-permute-start | bytes 49160 | tf_op jit(solution)/shard_map/ppermute | solution.py:13
  134.3 4.7 %collective-permute-start.33 = (bf16[64,128]{1,0:T(8,128)(2,1)S(1)}, bf16[64,128]{1,0:T(8,128)(2,1)S(1)}, u32[]{:S(2)}, u32[]{:S(2)}) collective-permute-start(bf16[64,128]{1,0:T(8,128)(2,1)S(1)} %get-tuple-element.89), channel_id=1, source_target_pairs={{0,2},{1,3},{2,0},{3,1},{4,6},{5,7},{6,4},{7,5},{8,10},{9,11},{10,... | collective-permute-start | bytes 49160 | tf_op jit(solution)/shard_map/ppermute | solution.py:13
  135.1 5.5 %collective-permute-start.34 = (bf16[64,128]{1,0:T(8,128)(2,1)S(1)}, bf16[64,128]{1,0:T(8,128)(2,1)S(1)}, u32[]{:S(2)}, u32[]{:S(2)}) collective-permute-start(bf16[64,128]{1,0:T(8,128)(2,1)S(1)} %get-tuple-element.90), channel_id=1, source_target_pairs={{0,3},{1,2},{2,1},{3,0},{4,7},{5,6},{6,5},{7,4},{8,11},{9,10},{10,... | collective-permute-start | bytes 49160 | tf_op jit(solution)/shard_map/ppermute | solution.py:13
  141.9 4.5 %collective-permute-start.35 = (bf16[64,128]{1,0:T(8,128)(2,1)S(1)}, bf16[64,128]{1,0:T(8,128)(2,1)S(1)}, u32[]{:S(2)}, u32[]{:S(2)}) collective-permute-start(bf16[64,128]{1,0:T(8,128)(2,1)S(1)} %get-tuple-element.93), channel_id=1, source_target_pairs={{0,1},{1,0},{2,3},{3,2},{4,5},{5,4},{6,7},{7,6},{8,9},{9,8},{10,11... | collective-permute-start | bytes 49160 | tf_op jit(solution)/shard_map/ppermute | solution.py:13
  142.3 5.5 %collective-permute-start.36 = (bf16[64,128]{1,0:T(8,128)(2,1)S(1)}, bf16[64,128]{1,0:T(8,128)(2,1)S(1)}, u32[]{:S(2)}, u32[]{:S(2)}) collective-permute-start(bf16[64,128]{1,0:T(8,128)(2,1)S(1)} %get-tuple-element.94), channel_id=1, source_target_pairs={{0,2},{1,3},{2,0},{3,1},{4,6},{5,7},{6,4},{7,5},{8,10},{9,11},{10,... | collective-permute-start | bytes 49160 | tf_op jit(solution)/shard_map/ppermute | solution.py:13
  146.1 5.5 %collective-permute-start.37 = (bf16[64,128]{1,0:T(8,128)(2,1)S(1)}, bf16[64,128]{1,0:T(8,128)(2,1)S(1)}, u32[]{:S(2)}, u32[]{:S(2)}) collective-permute-start(bf16[64,128]{1,0:T(8,128)(2,1)S(1)} %get-tuple-element.95), channel_id=1, source_target_pairs={{0,3},{1,2},{2,1},{3,0},{4,7},{5,6},{6,5},{7,4},{8,11},{9,10},{10,... | collective-permute-start | bytes 49160 | tf_op jit(solution)/shard_map/ppermute | solution.py:13
  154.3 4.5 %collective-permute-start.38 = (bf16[64,128]{1,0:T(8,128)(2,1)S(1)}, bf16[64,128]{1,0:T(8,128)(2,1)S(1)}, u32[]{:S(2)}, u32[]{:S(2)}) collective-permute-start(bf16[64,128]{1,0:T(8,128)(2,1)S(1)} %get-tuple-element.98), channel_id=1, source_target_pairs={{0,1},{1,0},{2,3},{3,2},{4,5},{5,4},{6,7},{7,6},{8,9},{9,8},{10,11... | collective-permute-start | bytes 49160 | tf_op jit(solution)/shard_map/ppermute | solution.py:13
  154.4 4.7 %collective-permute-start.39 = (bf16[64,128]{1,0:T(8,128)(2,1)S(1)}, bf16[64,128]{1,0:T(8,128)(2,1)S(1)}, u32[]{:S(2)}, u32[]{:S(2)}) collective-permute-start(bf16[64,128]{1,0:T(8,128)(2,1)S(1)} %get-tuple-element.99), channel_id=1, source_target_pairs={{0,2},{1,3},{2,0},{3,1},{4,6},{5,7},{6,4},{7,5},{8,10},{9,11},{10,... | collective-permute-start | bytes 49160 | tf_op jit(solution)/shard_map/ppermute | solution.py:13
  155.2 5.5 %collective-permute-start.40 = (bf16[64,128]{1,0:T(8,128)(2,1)S(1)}, bf16[64,128]{1,0:T(8,128)(2,1)S(1)}, u32[]{:S(2)}, u32[]{:S(2)}) collective-permute-start(bf16[64,128]{1,0:T(8,128)(2,1)S(1)} %get-tuple-element.100), channel_id=1, source_target_pairs={{0,3},{1,2},{2,1},{3,0},{4,7},{5,6},{6,5},{7,4},{8,11},{9,10},{10,... | collective-permute-start | bytes 49160 | tf_op jit(solution)/shard_map/ppermute | solution.py:13
  163.4 4.5 %collective-permute-start.41 = (bf16[64,128]{1,0:T(8,128)(2,1)S(1)}, bf16[64,128]{1,0:T(8,128)(2,1)S(1)}, u32[]{:S(2)}, u32[]{:S(2)}) collective-permute-start(bf16[64,128]{1,0:T(8,128)(2,1)S(1)} %get-tuple-element.103), channel_id=1, source_target_pairs={{0,1},{1,0},{2,3},{3,2},{4,5},{5,4},{6,7},{7,6},{8,9},{9,8},{10,11... | collective-permute-start | bytes 49160 | tf_op jit(solution)/shard_map/ppermute | solution.py:13
  163.8 5.6 %collective-permute-start.42 = (bf16[64,128]{1,0:T(8,128)(2,1)S(1)}, bf16[64,128]{1,0:T(8,128)(2,1)S(1)}, u32[]{:S(2)}, u32[]{:S(2)}) collective-permute-start(bf16[64,128]{1,0:T(8,128)(2,1)S(1)} %get-tuple-element.104), channel_id=1, source_target_pairs={{0,2},{1,3},{2,0},{3,1},{4,6},{5,7},{6,4},{7,5},{8,10},{9,11},{10,... | collective-permute-start | bytes 49160 | tf_op jit(solution)/shard_map/ppermute | solution.py:13
  167.6 5.5 %collective-permute-start.43 = (bf16[64,128]{1,0:T(8,128)(2,1)S(1)}, bf16[64,128]{1,0:T(8,128)(2,1)S(1)}, u32[]{:S(2)}, u32[]{:S(2)}) collective-permute-start(bf16[64,128]{1,0:T(8,128)(2,1)S(1)} %get-tuple-element.105), channel_id=1, source_target_pairs={{0,3},{1,2},{2,1},{3,0},{4,7},{5,6},{6,5},{7,4},{8,11},{9,10},{10,... | collective-permute-start | bytes 49160 | tf_op jit(solution)/shard_map/ppermute | solution.py:13
  174.4 4.5 %collective-permute-start.44 = (bf16[64,128]{1,0:T(8,128)(2,1)S(1)}, bf16[64,128]{1,0:T(8,128)(2,1)S(1)}, u32[]{:S(2)}, u32[]{:S(2)}) collective-permute-start(bf16[64,128]{1,0:T(8,128)(2,1)S(1)} %get-tuple-element.108), channel_id=1, source_target_pairs={{0,1},{1,0},{2,3},{3,2},{4,5},{5,4},{6,7},{7,6},{8,9},{9,8},{10,11... | collective-permute-start | bytes 49160 | tf_op jit(solution)/shard_map/ppermute | solution.py:13
  174.5 4.7 %collective-permute-start.45 = (bf16[64,128]{1,0:T(8,128)(2,1)S(1)}, bf16[64,128]{1,0:T(8,128)(2,1)S(1)}, u32[]{:S(2)}, u32[]{:S(2)}) collective-permute-start(bf16[64,128]{1,0:T(8,128)(2,1)S(1)} %get-tuple-element.109), channel_id=1, source_target_pairs={{0,2},{1,3},{2,0},{3,1},{4,6},{5,7},{6,4},{7,5},{8,10},{9,11},{10,... | collective-permute-start | bytes 49160 | tf_op jit(solution)/shard_map/ppermute | solution.py:13
  175.3 5.5 %collective-permute-start.46 = (bf16[64,128]{1,0:T(8,128)(2,1)S(1)}, bf16[64,128]{1,0:T(8,128)(2,1)S(1)}, u32[]{:S(2)}, u32[]{:S(2)}) collective-permute-start(bf16[64,128]{1,0:T(8,128)(2,1)S(1)} %get-tuple-element.110), channel_id=1, source_target_pairs={{0,3},{1,2},{2,1},{3,0},{4,7},{5,6},{6,5},{7,4},{8,11},{9,10},{10,... | collective-permute-start | bytes 49160 | tf_op jit(solution)/shard_map/ppermute | solution.py:13
  182.2 4.5 %collective-permute-start.47 = (bf16[64,128]{1,0:T(8,128)(2,1)S(1)}, bf16[64,128]{1,0:T(8,128)(2,1)S(1)}, u32[]{:S(2)}, u32[]{:S(2)}) collective-permute-start(bf16[64,128]{1,0:T(8,128)(2,1)S(1)} %get-tuple-element.113), channel_id=1, source_target_pairs={{0,1},{1,0},{2,3},{3,2},{4,5},{5,4},{6,7},{7,6},{8,9},{9,8},{10,11... | collective-permute-start | bytes 49160 | tf_op jit(solution)/shard_map/ppermute | solution.py:13
  182.5 6.0 %collective-permute-start.48 = (bf16[64,128]{1,0:T(8,128)(2,1)S(1)}, bf16[64,128]{1,0:T(8,128)(2,1)S(1)}, u32[]{:S(2)}, u32[]{:S(2)}) collective-permute-start(bf16[64,128]{1,0:T(8,128)(2,1)S(1)} %get-tuple-element.114), channel_id=1, source_target_pairs={{0,2},{1,3},{2,0},{3,1},{4,6},{5,7},{6,4},{7,5},{8,10},{9,11},{10,... | collective-permute-start | bytes 49160 | tf_op jit(solution)/shard_map/ppermute | solution.py:13
  186.4 5.5 %collective-permute-start.49 = (bf16[64,128]{1,0:T(8,128)(2,1)S(1)}, bf16[64,128]{1,0:T(8,128)(2,1)S(1)}, u32[]{:S(2)}, u32[]{:S(2)}) collective-permute-start(bf16[64,128]{1,0:T(8,128)(2,1)S(1)} %get-tuple-element.115), channel_id=1, source_target_pairs={{0,3},{1,2},{2,1},{3,0},{4,7},{5,6},{6,5},{7,4},{8,11},{9,10},{10,... | collective-permute-start | bytes 49160 | tf_op jit(solution)/shard_map/ppermute | solution.py:13
  192.5 5.8 %collective-permute-start.52 = (f32[64,128]{1,0:T(8,128)S(1)}, f32[64,128]{1,0:T(8,128)S(1)}, u32[]{:S(2)}, u32[]{:S(2)}) collective-permute-start(f32[64,128]{1,0:T(8,128)S(1)} %step_last.1), channel_id=1, source_target_pairs={{0,3},{1,2},{2,1},{3,0},{4,7},{5,6},{6,5},{7,4},{8,11},{9,10},{10,... | collective-permute-start | bytes 98312 | tf_op jit(solution)/shard_map/ppermute | solution.py:13
  192.8 5.4 %collective-permute-start.51 = (f32[64,128]{1,0:T(8,128)S(1)}, f32[64,128]{1,0:T(8,128)S(1)}, u32[]{:S(2)}, u32[]{:S(2)}) collective-permute-start(f32[64,128]{1,0:T(8,128)S(1)} %step_last.1), channel_id=1, source_target_pairs={{0,2},{1,3},{2,0},{3,1},{4,6},{5,7},{6,4},{7,5},{8,10},{9,11},{10,... | collective-permute-start | bytes 98312 | tf_op jit(solution)/shard_map/ppermute | solution.py:13
  192.8 6.0 %collective-permute-start.50 = (f32[64,128]{1,0:T(8,128)S(1)}, f32[64,128]{1,0:T(8,128)S(1)}, u32[]{:S(2)}, u32[]{:S(2)}) collective-permute-start(f32[64,128]{1,0:T(8,128)S(1)} %step_last.1), channel_id=1, source_target_pairs={{0,1},{1,0},{2,3},{3,2},{4,5},{5,4},{6,7},{7,6},{8,9},{9,8},{10,11... | collective-permute-start | bytes 98312 | tf_op jit(solution)/shard_map/ppermute | solution.py:13

commit v3 on v2

--- a/solution.py
+++ b/solution.py
@@ -26,20 +26,23 @@
     return values
 
 
-def gather_rows(factor):
+def gather_rows(factor, small):
     size = lax.axis_size("row")
     half = factor.shape[0] // 2
+
+    def move(value, distance):
+        return xor_permute(value, "row", distance)
+
+    tables = jnp.stack([small] + [move(small, k) for k in range(2, size, 2)])
     pieces = {0: (factor[:half], factor[half:])}
     for k in range(2, size, 2):
         high = 1 << (k.bit_length() - 1)
         low = k & -k
-        pieces[k] = (
-            xor_permute(pieces[k ^ high][0], "row", high),
-            xor_permute(pieces[k ^ low][1], "row", low),
-        )
+        pieces[k] = (move(pieces[k ^ high][0], high), move(pieces[k ^ low][1], low))
     for k in range(0, size, 2):
-        pieces[k ^ 1] = tuple(xor_permute(part, "row", 1) for part in pieces[k])
-    return [part for k in range(size) for part in pieces[k]]
+        pieces[k ^ 1] = tuple(move(part, 1) for part in pieces[k])
+    tables = jnp.stack([tables, move(tables, 1)], axis=1).reshape(size, *small.shape)
+    return [part for k in range(size) for part in pieces[k]], tables
 
 
 def vmem_budget(parts):
@@ -164,18 +167,17 @@
 
         def group(i, carry):
             for cc in range(cols):
-                value = None
+                left = []
+                right = []
                 for m in range(groups):
                     k = cc + cols * m
                     for s in range(slots):
-                        j = idx[(i * rows + k) * slots + s]
-                        term = contract(xs[m, j], whole[i, k, s])
-                        value = term if value is None else value + term
-                acc[cc, i] = value
-            own = acc[col, i]
-            for m in range(groups):
-                own = own + contract(xs[m, i * groups + m], diag[m, i])
-            acc[col, i] = own
+                        left.append(xs[m, idx[(i * rows + k) * slots + s]])
+                        right.append(whole[i, k, s])
+                acc[cc, i] = contract(jnp.concatenate(left, axis=1), jnp.concatenate(right, axis=1))
+            left = [xs[m, i * groups + m] for m in range(groups)]
+            right = [diag[m, i] for m in range(groups)]
+            acc[col, i] += contract(jnp.concatenate(left, axis=1), jnp.concatenate(right, axis=1))
             return carry
 
         lax.fori_loop(sc[which], sc[which + 1], group, 0)
@@ -208,7 +210,6 @@
         out_specs=out_specs,
         scratch_shapes=scratch,
         compiler_params=pltpu.CompilerParams(vmem_limit_bytes=budget),
-        name="step_" + kind,
     )(*args)
 
 
@@ -227,16 +228,13 @@
     groups = rows // cols
     kept = 2 * rhs_count // rows
     locals_here = per_row * groups
-    lanes = groups * kept
     op = r % 2
     dims = (rows, cols, groups, per_row, slots, block)
 
     small = jnp.concatenate(
         [inverse_pivot, jnp.pad(slot_columns.astype(jnp.float32), ((0, 0), (0, block - slots)))], axis=1
-    )[None]
-    for bit in bits_of(rows):
-        small = jnp.concatenate([small, xor_permute(small, "row", bit)], axis=0)
-    parts = gather_rows(factor)
+    )
+    parts, small = gather_rows(factor, small)
 
     blocks = jnp.arange(total, dtype=jnp.int32)
     onehot = snode_of_block[:, None] == jnp.arange(snodes, dtype=jnp.int32)[None, :]
@@ -306,7 +304,10 @@
     )
 
     def exchange(sends):
-        return [sends[0]] + [xor_permute(sends[d], "col", d) for d in range(1, cols)]
+        got = [sends[0]]
+        for d in range(1, cols):
+            got.append(xor_permute(sends[d], "col", d))
+        return got
 
     res = chosen
     sol = jnp.zeros(chosen.shape, jnp.float32)
@@ -316,7 +317,7 @@
         *sends, res = run("updated", step, state=(res, sol), received=exchange(sends))
     sol = run("last", steps - 1, state=(res, sol), received=exchange(sends))
 
-    whole = jnp.stack([sol] + [xor_permute(sol, "col", d) for d in range(1, cols)])
+    whole = jnp.stack(exchange([sol] * cols))
     whole = flip_order(whole, c)
     whole = whole.reshape(cols, per_row, groups, kept, block).transpose(2, 0, 1, 3, 4)
     whole = whole.reshape(rows, per_row * kept, block)

time: 211 us -> 189 us (0.90)
  waiting for transfers between devices: 90.9 us -> 75 us
  Pallas kernels: 30.6 us -> 26.5 us
    ppermute x53 -> x54, waiting for transfers between devices: 90.9 us -> 75 us  [xor_permute(): return lax.ppermute(value, axis, [(i, i ^ distance) for i in range(size)])]
    pallas_call x12, Pallas kernels: 27.2 us -> 23 us  [step_kernel(): pl.pallas_call(body, out_shape=out_shape, in_specs=[smem, smem] + [vmem]...]
    ppermute x53 -> x54, starting transfers between devices: 67.4 us -> 67.2 us  [xor_permute(): return lax.ppermute(value, axis, [(i, i ^ distance) for i in range(size)])]
  transfers between devices with their start and end apart: 53 -> 54, of which waited for: 31 -> 32; matrix products, arithmetic and copies ran while one was open for 4% -> 4% of each run, Pallas kernels for 0% -> 0%
where the time goes in v3:
time: 189 us
  waiting for transfers between devices  75 us (40%)
  starting transfers between devices  67.2 us (36%)
  Pallas kernels  26.5 us (14%)
  blocking collectives  9.02 us (5%)
  other arithmetic  6.79 us (4%)
  local copies, waits for them, and re-layouts  3.48 us (2%)
    ppermute x54, waiting for transfers between devices, xor_permute(): return lax.ppermute(value, axis, [(i, i ^ distance) for i in range(size)])  75 us
    ppermute x54, starting transfers between devices, xor_permute(): return lax.ppermute(value, axis, [(i, i ^ distance) for i in range(size)])  67.2 us
    pallas_call x12, Pallas kernels, step_kernel(): pl.pallas_call(body, out_shape=out_shape, in_specs=[smem, smem] + [vmem]...  23 us
    all_to_all x1, blocking collectives, shards(): lax.all_to_all(whole, 'row', 0, 0)  9.02 us
  transfers between devices with their start and end apart: 54, of which 32 were waited for; matrix products, arithmetic and copies ran while one was open for 4% of the time, Pallas kernels for 0%

profile of v3, /device:TPU:0, one launch (start us, length us, event | category | flops | bytes accessed | tf_op | source)
XLA Modules:
  0.0 189.0 jit_solution(5527923270776727899)
XLA Ops:
  2.1 3.9 %collective-permute-start.2 = (f32[8,256]{1,0:T(8,128)S(1)}, f32[8,256]{1,0:T(8,128)S(1)}, u32[]{:S(2)}, u32[]{:S(2)}) collective-permute-start(f32[8,256]{1,0:T(8,128)S(1)} %get-tuple-element.129), channel_id=1, source_target_pairs={{0,24},{4,28},{8,16},{12,20},{16,8},{20,12},{24,0},{28,4},{1,25},{... | collective-permute-start | bytes 24584 | tf_op jit(solution)/shard_map/ppermute | solution.py:13
  6.6 1.3 fusion.11
  7.9 2.0 %collective-permute-start.6 = (bf16[4,4,128,128]{3,2,1,0:T(8,128)(2,1)S(1)}, bf16[4,4,128,128]{3,2,1,0:T(8,128)(2,1)S(1)}, u32[]{:S(2)}, u32[]{:S(2)}) collective-permute-start(bf16[4,4,128,128]{3,2,1,0:T(8,128)(2,1)S(1)} %get-tuple-element.123.refs_2_), channel_id=1, source_target_pairs={{0,8},{4,12},{8,0},{12,4},{16,24},{20,28},{24,16},{28,20},{1,9},{5... | collective-permute-start | bytes 1572872 | tf_op jit(solution)/shard_map/ppermute | solution.py:13
  10.0 0.8 select_reduce_fusion.6
  10.9 1.1 select_reduce_fusion.3
  12.5 0.8 dynamic-slice_select_fusion
  14.2 1.3 collective-permute-done.3
  15.4 1.5 collective-permute-start.11
  17.6 5.2 %collective-permute-done.6.refs_6_ = bf16[4,4,128,128]{3,2,1,0:T(8,128)(2,1)S(1)} collective-permute-done((bf16[4,4,128,128]{3,2,1,0:T(8,128)(2,1)S(1)}, bf16[4,4,128,128]{3,2,1,0:T(8,128)(2,1)S(1)}, u32[]{:S(2)}, u32[]{:S(2)}) %collective-permute-start.6) | collective-permute-done | bytes 524320 | tf_op jit(solution)/shard_map/ppermute | solution.py:13
  22.8 2.0 %collective-permute-start.14 = (bf16[4,4,128,128]{3,2,1,0:T(8,128)(2,1)S(1)}, bf16[4,4,128,128]{3,2,1,0:T(8,128)(2,1)}, u32[]{:S(2)}, u32[]{:S(2)}) collective-permute-start(bf16[4,4,128,128]{3,2,1,0:T(8,128)(2,1)S(1)} %collective-permute-done.6.refs_6_), channel_id=1, source_target_pairs={{0,16},{4,20},{8,24},{12,28},{16,0},{20,4},{24,8},{28,12},{1,17},{... | collective-permute-start | bytes 1572872 | tf_op jit(solution)/shard_map/ppermute | solution.py:13
  24.8 5.5 %collective-permute-done.11.refs_11_ = bf16[4,4,128,128]{3,2,1,0:T(8,128)(2,1)} collective-permute-done((bf16[4,4,128,128]{3,2,1,0:T(8,128)(2,1)S(1)}, bf16[4,4,128,128]{3,2,1,0:T(8,128)(2,1)}, u32[]{:S(2)}, u32[]{:S(2)}) %collective-permute-start.11) | collective-permute-done | bytes 524320 | tf_op jit(solution)/shard_map/ppermute | solution.py:13
  30.3 1.5 collective-permute-start.15
  32.0 1.9 %select_reduce_fusion.1 = (s32[8,8,4]{1,2,0:T(4,128)S(1)}, s32[8,8,4]{1,2,0:T(4,128)S(1)}) fusion(s32[64]{0:T(128)} %param.11, s32[8,8,4]{1,2,0:T(4,128)S(1)} %bitcast.110, s32[64]{0:T(128)S(1)} %broadcast_select_fusion), kind=kLoop, calls=%fused_computation.5 | loop fusion | flops 81408 | bytes 3584 | tf_op jit(solution)/shard_map/reduce_sum | solution.py:245
  34.0 7.5 %collective-permute-done.10.refs_10_ = bf16[4,4,128,128]{3,2,1,0:T(8,128)(2,1)} collective-permute-done((bf16[4,4,128,128]{3,2,1,0:T(8,128)(2,1)S(1)}, bf16[4,4,128,128]{3,2,1,0:T(8,128)(2,1)}, u32[]{:S(2)}, u32[]{:S(2)}) %collective-permute-start.10) | collective-permute-done | bytes 524320 | tf_op jit(solution)/shard_map/ppermute | solution.py:13
  42.1 9.9 %collective-permute-done.14.refs_14_ = bf16[4,4,128,128]{3,2,1,0:T(8,128)(2,1)} collective-permute-done((bf16[4,4,128,128]{3,2,1,0:T(8,128)(2,1)S(1)}, bf16[4,4,128,128]{3,2,1,0:T(8,128)(2,1)}, u32[]{:S(2)}, u32[]{:S(2)}) %collective-permute-start.14) | collective-permute-done | bytes 524320 | tf_op jit(solution)/shard_map/ppermute | solution.py:13
  53.1 1.1 collective-permute-done.16.refs_16_
  54.2 0.7 collective-permute-done.17.refs_17_
  55.0 3.5 %load_operator.1 = (bf16[8,8,4,128,128]{4,3,2,1,0:T(8,128)(2,1)S(1)}, bf16[2,8,128,128]{3,2,1,0:T(8,128)(2,1)S(1)}) custom-call(s32[27]{0:T(128)S(1)} %pad_add_fusion.1.refs_0_, s32[16]{0:T(128)S(1)} %reshape.341.refs_1_, bf16[4,4,128,128]{3,2,1,0:T(8,128)(2,1)S(1)} %get-tuple-element.123.refs_2_, bf16[4,4,128,128]{3,2,1,0:T(8,128)(2,1)S(1)} %get-tuple-element.122.refs_3_, ...), custom_call_target="tpu_custom_call" | custom-call | tf_op jit(solution)/shard_map/load_operator/pallas_call | solution.py:84
  58.5 1.0 shard_map.86
  59.5 1.7 collective-permute-start.18
  61.2 2.6 %collective-permute-start.19 = (bf16[64,128]{1,0:T(8,128)(2,1)S(1)}, bf16[64,128]{1,0:T(8,128)(2,1)S(1)}, u32[]{:S(2)}, u32[]{:S(2)}) collective-permute-start(bf16[64,128]{1,0:T(8,128)(2,1)S(1)} %get-tuple-element.64), channel_id=1, source_target_pairs={{0,2},{1,3},{2,0},{3,1},{4,6},{5,7},{6,4},{7,5},{8,10},{9,11},{10,... | collective-permute-start | bytes 49160 | tf_op jit(solution)/shard_map/ppermute | solution.py:13
  64.0 1.9 %collective-permute-done.19.refs_10_ = bf16[64,128]{1,0:T(8,128)(2,1)S(1)} collective-permute-done((bf16[64,128]{1,0:T(8,128)(2,1)S(1)}, bf16[64,128]{1,0:T(8,128)(2,1)S(1)}, u32[]{:S(2)}, u32[]{:S(2)}) %collective-permute-start.19) | collective-permute-done | bytes 16416 | tf_op jit(solution)/shard_map/ppermute | solution.py:13
  65.9 3.4 %collective-permute-done.20.refs_11_ = bf16[64,128]{1,0:T(8,128)(2,1)S(1)} collective-permute-done((bf16[64,128]{1,0:T(8,128)(2,1)S(1)}, bf16[64,128]{1,0:T(8,128)(2,1)S(1)}, u32[]{:S(2)}, u32[]{:S(2)}) %collective-permute-start.20) | collective-permute-done | bytes 16416 | tf_op jit(solution)/shard_map/ppermute | solution.py:13
  69.3 4.0 %shard_map.87 = (f32[64,128]{1,0:T(8,128)S(1)}, bf16[64,128]{1,0:T(8,128)(2,1)S(1)}, bf16[64,128]{1,0:T(8,128)(2,1)S(1)}, bf16[64,128]{1,0:T(8,128)(2,1)S(1)}, f32[64,128]{1,0:T(8,128)S(1)}) custom-call(s32[27]{0:T(128)S(1)} %pad_add_fusion.1.refs_0_, s32[256]{0:T(256)S(1)} %reshape.338.refs_1_, bf16[8,8,4,128,128]{4,3,2,1,0:T(8,128)(2,1)S(1)} %get-tuple-element.59.refs_2_, ...), custom_call_target="tpu_custom_call" | custom-call | tf_op jit(solution)/shard_map/pallas_call | solution.py:206
  74.1 3.6 %collective-permute-start.23 = (bf16[64,128]{1,0:T(8,128)(2,1)S(1)}, bf16[64,128]{1,0:T(8,128)(2,1)S(1)}, u32[]{:S(2)}, u32[]{:S(2)}) collective-permute-start(bf16[64,128]{1,0:T(8,128)(2,1)S(1)} %get-tuple-element.70), channel_id=1, source_target_pairs={{0,3},{1,2},{2,1},{3,0},{4,7},{5,6},{6,5},{7,4},{8,11},{9,10},{10,... | collective-permute-start | bytes 49160 | tf_op jit(solution)/shard_map/ppermute | solution.py:13
  78.1 1.6 collective-permute-done.23.refs_11_
  79.6 1.4 shard_map.88
  81.5 3.8 %collective-permute-start.25 = (bf16[64,128]{1,0:T(8,128)(2,1)S(1)}, bf16[64,128]{1,0:T(8,128)(2,1)S(1)}, u32[]{:S(2)}, u32[]{:S(2)}) collective-permute-start(bf16[64,128]{1,0:T(8,128)(2,1)S(1)} %get-tuple-element.74), channel_id=1, source_target_pairs={{0,2},{1,3},{2,0},{3,1},{4,6},{5,7},{6,4},{7,5},{8,10},{9,11},{10,... | collective-permute-start | bytes 49160 | tf_op jit(solution)/shard_map/ppermute | solution.py:13
  85.5 1.5 collective-permute-done.25.refs_10_
  87.1 3.8 %collective-permute-done.26.refs_11_ = bf16[64,128]{1,0:T(8,128)(2,1)S(1)} collective-permute-done((bf16[64,128]{1,0:T(8,128)(2,1)S(1)}, bf16[64,128]{1,0:T(8,128)(2,1)S(1)}, u32[]{:S(2)}, u32[]{:S(2)}) %collective-permute-start.26) | collective-permute-done | bytes 16416 | tf_op jit(solution)/shard_map/ppermute | solution.py:13
  90.9 3.5 %shard_map.89 = (f32[64,128]{1,0:T(8,128)S(1)}, bf16[64,128]{1,0:T(8,128)(2,1)S(1)}, bf16[64,128]{1,0:T(8,128)(2,1)S(1)}, bf16[64,128]{1,0:T(8,128)(2,1)S(1)}, f32[64,128]{1,0:T(8,128)S(1)}) custom-call(s32[27]{0:T(128)S(1)} %pad_add_fusion.1.refs_0_, s32[256]{0:T(256)S(1)} %reshape.338.refs_1_, bf16[8,8,4,128,128]{4,3,2,1,0:T(8,128)(2,1)S(1)} %get-tuple-element.59.refs_2_, ...), custom_call_target="tpu_custom_call" | custom-call | tf_op jit(solution)/shard_map/pallas_call | solution.py:206
  95.3 3.6 %collective-permute-start.29 = (bf16[64,128]{1,0:T(8,128)(2,1)S(1)}, bf16[64,128]{1,0:T(8,128)(2,1)S(1)}, u32[]{:S(2)}, u32[]{:S(2)}) collective-permute-start(bf16[64,128]{1,0:T(8,128)(2,1)S(1)} %get-tuple-element.80), channel_id=1, source_target_pairs={{0,3},{1,2},{2,1},{3,0},{4,7},{5,6},{6,5},{7,4},{8,11},{9,10},{10,... | collective-permute-start | bytes 49160 | tf_op jit(solution)/shard_map/ppermute | solution.py:13
  99.2 1.6 collective-permute-done.29.refs_11_
  100.8 1.4 shard_map.90
  102.7 3.8 %collective-permute-start.31 = (bf16[64,128]{1,0:T(8,128)(2,1)S(1)}, bf16[64,128]{1,0:T(8,128)(2,1)S(1)}, u32[]{:S(2)}, u32[]{:S(2)}) collective-permute-start(bf16[64,128]{1,0:T(8,128)(2,1)S(1)} %get-tuple-element.84), channel_id=1, source_target_pairs={{0,2},{1,3},{2,0},{3,1},{4,6},{5,7},{6,4},{7,5},{8,10},{9,11},{10,... | collective-permute-start | bytes 49160 | tf_op jit(solution)/shard_map/ppermute | solution.py:13
  106.7 1.5 collective-permute-done.31.refs_10_
  108.2 3.8 %collective-permute-done.32.refs_11_ = bf16[64,128]{1,0:T(8,128)(2,1)S(1)} collective-permute-done((bf16[64,128]{1,0:T(8,128)(2,1)S(1)}, bf16[64,128]{1,0:T(8,128)(2,1)S(1)}, u32[]{:S(2)}, u32[]{:S(2)}) %collective-permute-start.32) | collective-permute-done | bytes 16416 | tf_op jit(solution)/shard_map/ppermute | solution.py:13
  112.0 3.1 %shard_map.91 = (f32[64,128]{1,0:T(8,128)S(1)}, bf16[64,128]{1,0:T(8,128)(2,1)S(1)}, bf16[64,128]{1,0:T(8,128)(2,1)S(1)}, bf16[64,128]{1,0:T(8,128)(2,1)S(1)}, f32[64,128]{1,0:T(8,128)S(1)}) custom-call(s32[27]{0:T(128)S(1)} %pad_add_fusion.1.refs_0_, s32[256]{0:T(256)S(1)} %reshape.338.refs_1_, bf16[8,8,4,128,128]{4,3,2,1,0:T(8,128)(2,1)S(1)} %get-tuple-element.59.refs_2_, ...), custom_call_target="tpu_custom_call" | custom-call | tf_op jit(solution)/shard_map/pallas_call | solution.py:206
  115.2 0.7 collective-permute-start.34
  116.0 3.6 %collective-permute-start.35 = (bf16[64,128]{1,0:T(8,128)(2,1)S(1)}, bf16[64,128]{1,0:T(8,128)(2,1)S(1)}, u32[]{:S(2)}, u32[]{:S(2)}) collective-permute-start(bf16[64,128]{1,0:T(8,128)(2,1)S(1)} %get-tuple-element.90), channel_id=1, source_target_pairs={{0,3},{1,2},{2,1},{3,0},{4,7},{5,6},{6,5},{7,4},{8,11},{9,10},{10,... | collective-permute-start | bytes 49160 | tf_op jit(solution)/shard_map/ppermute | solution.py:13
  119.9 1.6 collective-permute-done.35.refs_11_
  121.5 2.3 %shard_map.92 = (f32[64,128]{1,0:T(8,128)S(1)}, bf16[64,128]{1,0:T(8,128)(2,1)S(1)}, bf16[64,128]{1,0:T(8,128)(2,1)S(1)}, bf16[64,128]{1,0:T(8,128)(2,1)S(1)}, f32[64,128]{1,0:T(8,128)S(1)}) custom-call(s32[27]{0:T(128)S(1)} %pad_add_fusion.1.refs_0_, s32[256]{0:T(256)S(1)} %reshape.338.refs_1_, bf16[8,8,4,128,128]{4,3,2,1,0:T(8,128)(2,1)S(1)} %get-tuple-element.59.refs_2_, ...), custom_call_target="tpu_custom_call" | custom-call | tf_op jit(solution)/shard_map/pallas_call | solution.py:206
  124.2 3.8 %collective-permute-start.37 = (bf16[64,128]{1,0:T(8,128)(2,1)S(1)}, bf16[64,128]{1,0:T(8,128)(2,1)S(1)}, u32[]{:S(2)}, u32[]{:S(2)}) collective-permute-start(bf16[64,128]{1,0:T(8,128)(2,1)S(1)} %get-tuple-element.94), channel_id=1, source_target_pairs={{0,2},{1,3},{2,0},{3,1},{4,6},{5,7},{6,4},{7,5},{8,10},{9,11},{10,... | collective-permute-start | bytes 49160 | tf_op jit(solution)/shard_map/ppermute | solution.py:13
  128.2 1.5 collective-permute-done.37.refs_10_
  129.8 3.8 %collective-permute-done.38.refs_11_ = bf16[64,128]{1,0:T(8,128)(2,1)S(1)} collective-permute-done((bf16[64,128]{1,0:T(8,128)(2,1)S(1)}, bf16[64,128]{1,0:T(8,128)(2,1)S(1)}, u32[]{:S(2)}, u32[]{:S(2)}) %collective-permute-start.38) | collective-permute-done | bytes 16416 | tf_op jit(solution)/shard_map/ppermute | solution.py:13
  133.6 1.8 shard_map.93
  135.5 0.8 collective-permute-start.40
  136.3 3.6 %collective-permute-start.41 = (bf16[64,128]{1,0:T(8,128)(2,1)S(1)}, bf16[64,128]{1,0:T(8,128)(2,1)S(1)}, u32[]{:S(2)}, u32[]{:S(2)}) collective-permute-start(bf16[64,128]{1,0:T(8,128)(2,1)S(1)} %get-tuple-element.100), channel_id=1, source_target_pairs={{0,3},{1,2},{2,1},{3,0},{4,7},{5,6},{6,5},{7,4},{8,11},{9,10},{10,... | collective-permute-start | bytes 49160 | tf_op jit(solution)/shard_map/ppermute | solution.py:13
  140.3 1.5 collective-permute-done.41.refs_11_
  141.8 1.8 shard_map.94
  144.1 3.8 %collective-permute-start.43 = (bf16[64,128]{1,0:T(8,128)(2,1)S(1)}, bf16[64,128]{1,0:T(8,128)(2,1)S(1)}, u32[]{:S(2)}, u32[]{:S(2)}) collective-permute-start(bf16[64,128]{1,0:T(8,128)(2,1)S(1)} %get-tuple-element.104), channel_id=1, source_target_pairs={{0,2},{1,3},{2,0},{3,1},{4,6},{5,7},{6,4},{7,5},{8,10},{9,11},{10,... | collective-permute-start | bytes 49160 | tf_op jit(solution)/shard_map/ppermute | solution.py:13
  148.1 1.5 collective-permute-done.43.refs_10_
  149.6 3.8 %collective-permute-done.44.refs_11_ = bf16[64,128]{1,0:T(8,128)(2,1)S(1)} collective-permute-done((bf16[64,128]{1,0:T(8,128)(2,1)S(1)}, bf16[64,128]{1,0:T(8,128)(2,1)S(1)}, u32[]{:S(2)}, u32[]{:S(2)}) %collective-permute-start.44) | collective-permute-done | bytes 16416 | tf_op jit(solution)/shard_map/ppermute | solution.py:13
  153.5 1.0 shard_map.95
  154.5 0.8 collective-permute-start.46
  155.3 3.6 %collective-permute-start.47 = (bf16[64,128]{1,0:T(8,128)(2,1)S(1)}, bf16[64,128]{1,0:T(8,128)(2,1)S(1)}, u32[]{:S(2)}, u32[]{:S(2)}) collective-permute-start(bf16[64,128]{1,0:T(8,128)(2,1)S(1)} %get-tuple-element.110), channel_id=1, source_target_pairs={{0,3},{1,2},{2,1},{3,0},{4,7},{5,6},{6,5},{7,4},{8,11},{9,10},{10,... | collective-permute-start | bytes 49160 | tf_op jit(solution)/shard_map/ppermute | solution.py:13
  159.3 1.6 collective-permute-done.47.refs_11_
  160.8 1.0 shard_map.96
  162.3 3.8 %collective-permute-start.49 = (bf16[64,128]{1,0:T(8,128)(2,1)S(1)}, bf16[64,128]{1,0:T(8,128)(2,1)S(1)}, u32[]{:S(2)}, u32[]{:S(2)}) collective-permute-start(bf16[64,128]{1,0:T(8,128)(2,1)S(1)} %get-tuple-element.114), channel_id=1, source_target_pairs={{0,2},{1,3},{2,0},{3,1},{4,6},{5,7},{6,4},{7,5},{8,10},{9,11},{10,... | collective-permute-start | bytes 49160 | tf_op jit(solution)/shard_map/ppermute | solution.py:13
  166.3 1.5 collective-permute-done.49.refs_8_
  167.8 3.8 %collective-permute-done.50.refs_9_ = bf16[64,128]{1,0:T(8,128)(2,1)S(1)} collective-permute-done((bf16[64,128]{1,0:T(8,128)(2,1)S(1)}, bf16[64,128]{1,0:T(8,128)(2,1)S(1)}, u32[]{:S(2)}, u32[]{:S(2)}) %collective-permute-start.50) | collective-permute-done | bytes 16416 | tf_op jit(solution)/shard_map/ppermute | solution.py:13
  172.5 4.2 %collective-permute-start.51 = (f32[64,128]{1,0:T(8,128)S(1)}, f32[64,128]{1,0:T(8,128)S(1)}, u32[]{:S(2)}, u32[]{:S(2)}) collective-permute-start(f32[64,128]{1,0:T(8,128)S(1)} %shard_map.97), channel_id=1, source_target_pairs={{0,1},{1,0},{2,3},{3,2},{4,5},{5,4},{6,7},{7,6},{8,9},{9,8},{10,11... | collective-permute-start | bytes 98312 | tf_op jit(solution)/shard_map/ppermute | solution.py:13
  176.7 1.3 collective-permute-done.53
  178.7 9.0 %all_to_all.5 = f32[8,32,128]{2,1,0:T(8,128)S(1)} all-to-all(f32[8,32,128]{2,1,0:T(8,128)S(1)} %bitcast.106), channel_id=1, replica_groups=mesh['row'=8,'col'=4] {'row'}, dimensions={0} | all-to-all | bytes 262144 | tf_op jit(solution)/shard_map/all_to_all | solution.py:324
  (106 shorter events, 15.8 us)
Async XLA Ops:
  2.1 11.3 %collective-permute-start.2 = (f32[8,256]{1,0:T(8,128)S(1)}, f32[8,256]{1,0:T(8,128)S(1)}, u32[]{:S(2)}, u32[]{:S(2)}) collective-permute-start(f32[8,256]{1,0:T(8,128)S(1)} %get-tuple-element.129), channel_id=1, source_target_pairs={{0,24},{4,28},{8,16},{12,20},{16,8},{20,12},{24,0},{28,4},{1,25},{... | collective-permute-start | bytes 24584 | tf_op jit(solution)/shard_map/ppermute | solution.py:13
  6.0 7.6 %collective-permute-start.1 = (f32[8,256]{1,0:T(8,128)S(1)}, f32[8,256]{1,0:T(8,128)S(1)}, u32[]{:S(2)}, u32[]{:S(2)}) collective-permute-start(f32[8,256]{1,0:T(8,128)S(1)} %get-tuple-element.129), channel_id=1, source_target_pairs={{0,16},{4,20},{8,24},{12,28},{16,0},{20,4},{24,8},{28,12},{1,17},{... | collective-permute-start | bytes 24584 | tf_op jit(solution)/shard_map/ppermute | solution.py:13
  6.5 7.4 %collective-permute-start = (f32[8,256]{1,0:T(8,128)S(1)}, f32[8,256]{1,0:T(8,128)S(1)}, u32[]{:S(2)}, u32[]{:S(2)}) collective-permute-start(f32[8,256]{1,0:T(8,128)S(1)} %get-tuple-element.129), channel_id=1, source_target_pairs={{0,8},{4,12},{8,0},{12,4},{16,24},{20,28},{24,16},{28,20},{1,9},{5... | collective-permute-start | bytes 24584 | tf_op jit(solution)/shard_map/ppermute | solution.py:13
  7.9 9.2 %collective-permute-start.4 = (bf16[4,4,128,128]{3,2,1,0:T(8,128)(2,1)S(1)}, bf16[4,4,128,128]{3,2,1,0:T(8,128)(2,1)S(1)}, u32[]{:S(2)}, u32[]{:S(2)}) collective-permute-start(bf16[4,4,128,128]{3,2,1,0:T(8,128)(2,1)S(1)} %get-tuple-element.123.refs_2_), channel_id=1, source_target_pairs={{0,4},{4,0},{8,12},{12,8},{16,20},{20,16},{24,28},{28,24},{1,5},{5... | collective-permute-start | bytes 1572872 | tf_op jit(solution)/shard_map/ppermute | solution.py:13
  7.9 14.9 %collective-permute-start.6 = (bf16[4,4,128,128]{3,2,1,0:T(8,128)(2,1)S(1)}, bf16[4,4,128,128]{3,2,1,0:T(8,128)(2,1)S(1)}, u32[]{:S(2)}, u32[]{:S(2)}) collective-permute-start(bf16[4,4,128,128]{3,2,1,0:T(8,128)(2,1)S(1)} %get-tuple-element.123.refs_2_), channel_id=1, source_target_pairs={{0,8},{4,12},{8,0},{12,4},{16,24},{20,28},{24,16},{28,20},{1,9},{5... | collective-permute-start | bytes 1572872 | tf_op jit(solution)/shard_map/ppermute | solution.py:13
  13.4 9.4 %collective-permute-start.5 = (bf16[4,4,128,128]{3,2,1,0:T(8,128)(2,1)S(1)}, bf16[4,4,128,128]{3,2,1,0:T(8,128)(2,1)S(1)}, u32[]{:S(2)}, u32[]{:S(2)}) collective-permute-start(bf16[4,4,128,128]{3,2,1,0:T(8,128)(2,1)S(1)} %get-tuple-element.122.refs_3_), channel_id=1, source_target_pairs={{0,4},{4,0},{8,12},{12,8},{16,20},{20,16},{24,28},{28,24},{1,5},{5... | collective-permute-start | bytes 1572872 | tf_op jit(solution)/shard_map/ppermute | solution.py:13
  13.6 20.4 %collective-permute-start.7 = (bf16[4,4,128,128]{3,2,1,0:T(8,128)(2,1)S(1)}, bf16[4,4,128,128]{3,2,1,0:T(8,128)(2,1)S(1)}, u32[]{:S(2)}, u32[]{:S(2)}) collective-permute-start(bf16[4,4,128,128]{3,2,1,0:T(8,128)(2,1)S(1)} %get-tuple-element.122.refs_3_), channel_id=1, source_target_pairs={{0,8},{4,12},{8,0},{12,4},{16,24},{20,28},{24,16},{28,20},{1,9},{5... | collective-permute-start | bytes 1572872 | tf_op jit(solution)/shard_map/ppermute | solution.py:13
  13.9 1.5 collective-permute-start.3
  15.4 14.9 %collective-permute-start.11 = (bf16[4,4,128,128]{3,2,1,0:T(8,128)(2,1)S(1)}, bf16[4,4,128,128]{3,2,1,0:T(8,128)(2,1)}, u32[]{:S(2)}, u32[]{:S(2)}) collective-permute-start(bf16[4,4,128,128]{3,2,1,0:T(8,128)(2,1)S(1)} %get-tuple-element.122.refs_3_), channel_id=1, source_target_pairs={{0,16},{4,20},{8,24},{12,28},{16,0},{20,4},{24,8},{28,12},{1,17},{... | collective-permute-start | bytes 1572872 | tf_op jit(solution)/shard_map/ppermute | solution.py:13
  17.0 24.6 %collective-permute-start.10 = (bf16[4,4,128,128]{3,2,1,0:T(8,128)(2,1)S(1)}, bf16[4,4,128,128]{3,2,1,0:T(8,128)(2,1)}, u32[]{:S(2)}, u32[]{:S(2)}) collective-permute-start(bf16[4,4,128,128]{3,2,1,0:T(8,128)(2,1)S(1)} %get-tuple-element.123.refs_2_), channel_id=1, source_target_pairs={{0,16},{4,20},{8,24},{12,28},{16,0},{20,4},{24,8},{28,12},{1,17},{... | collective-permute-start | bytes 1572872 | tf_op jit(solution)/shard_map/ppermute | solution.py:13
  22.8 18.8 %collective-permute-start.8 = (bf16[4,4,128,128]{3,2,1,0:T(8,128)(2,1)S(1)}, bf16[4,4,128,128]{3,2,1,0:T(8,128)(2,1)}, u32[]{:S(2)}, u32[]{:S(2)}) collective-permute-start(bf16[4,4,128,128]{3,2,1,0:T(8,128)(2,1)S(1)} %collective-permute-done.6.refs_6_), channel_id=1, source_target_pairs={{0,4},{4,0},{8,12},{12,8},{16,20},{20,16},{24,28},{28,24},{1,5},{5... | collective-permute-start | bytes 1572872 | tf_op jit(solution)/shard_map/ppermute | solution.py:13
  22.8 29.2 %collective-permute-start.14 = (bf16[4,4,128,128]{3,2,1,0:T(8,128)(2,1)S(1)}, bf16[4,4,128,128]{3,2,1,0:T(8,128)(2,1)}, u32[]{:S(2)}, u32[]{:S(2)}) collective-permute-start(bf16[4,4,128,128]{3,2,1,0:T(8,128)(2,1)S(1)} %collective-permute-done.6.refs_6_), channel_id=1, source_target_pairs={{0,16},{4,20},{8,24},{12,28},{16,0},{20,4},{24,8},{28,12},{1,17},{... | collective-permute-start | bytes 1572872 | tf_op jit(solution)/shard_map/ppermute | solution.py:13
  30.3 21.7 %collective-permute-start.15 = (bf16[4,4,128,128]{3,2,1,0:T(8,128)(2,1)}, bf16[4,4,128,128]{3,2,1,0:T(8,128)(2,1)}, u32[]{:S(2)}, u32[]{:S(2)}) collective-permute-start(bf16[4,4,128,128]{3,2,1,0:T(8,128)(2,1)} %collective-permute-done.11.refs_11_), channel_id=1, source_target_pairs={{0,8},{4,12},{8,0},{12,4},{16,24},{20,28},{24,16},{28,20},{1,9},{5... | collective-permute-start | bytes 1572872 | tf_op jit(solution)/shard_map/ppermute | solution.py:13
  34.0 19.1 %collective-permute-start.13 = (bf16[4,4,128,128]{3,2,1,0:T(8,128)(2,1)}, bf16[4,4,128,128]{3,2,1,0:T(8,128)(2,1)}, u32[]{:S(2)}, u32[]{:S(2)}) collective-permute-start(bf16[4,4,128,128]{3,2,1,0:T(8,128)(2,1)} %collective-permute-done.11.refs_11_), channel_id=1, source_target_pairs={{0,4},{4,0},{8,12},{12,8},{16,20},{20,16},{24,28},{28,24},{1,5},{5... | collective-permute-start | bytes 1572872 | tf_op jit(solution)/shard_map/ppermute | solution.py:13
  41.6 11.5 %collective-permute-start.9 = (bf16[4,4,128,128]{3,2,1,0:T(8,128)(2,1)S(1)}, bf16[4,4,128,128]{3,2,1,0:T(8,128)(2,1)}, u32[]{:S(2)}, u32[]{:S(2)}) collective-permute-start(bf16[4,4,128,128]{3,2,1,0:T(8,128)(2,1)S(1)} %collective-permute-done.7.refs_7_), channel_id=1, source_target_pairs={{0,4},{4,0},{8,12},{12,8},{16,20},{20,16},{24,28},{28,24},{1,5},{5... | collective-permute-start | bytes 1572872 | tf_op jit(solution)/shard_map/ppermute | solution.py:13
  41.6 11.5 %collective-permute-start.12 = (bf16[4,4,128,128]{3,2,1,0:T(8,128)(2,1)}, bf16[4,4,128,128]{3,2,1,0:T(8,128)(2,1)}, u32[]{:S(2)}, u32[]{:S(2)}) collective-permute-start(bf16[4,4,128,128]{3,2,1,0:T(8,128)(2,1)} %collective-permute-done.10.refs_10_), channel_id=1, source_target_pairs={{0,4},{4,0},{8,12},{12,8},{16,20},{20,16},{24,28},{28,24},{1,5},{5... | collective-permute-start | bytes 1572872 | tf_op jit(solution)/shard_map/ppermute | solution.py:13
  52.0 2.3 %collective-permute-start.16 = (bf16[4,4,128,128]{3,2,1,0:T(8,128)(2,1)}, bf16[4,4,128,128]{3,2,1,0:T(8,128)(2,1)}, u32[]{:S(2)}, u32[]{:S(2)}) collective-permute-start(bf16[4,4,128,128]{3,2,1,0:T(8,128)(2,1)} %collective-permute-done.14.refs_14_), channel_id=1, source_target_pairs={{0,4},{4,0},{8,12},{12,8},{16,20},{20,16},{24,28},{28,24},{1,5},{5... | collective-permute-start | bytes 1572872 | tf_op jit(solution)/shard_map/ppermute | solution.py:13
  52.0 3.0 %collective-permute-start.17 = (bf16[4,4,128,128]{3,2,1,0:T(8,128)(2,1)}, bf16[4,4,128,128]{3,2,1,0:T(8,128)(2,1)}, u32[]{:S(2)}, u32[]{:S(2)}) collective-permute-start(bf16[4,4,128,128]{3,2,1,0:T(8,128)(2,1)} %collective-permute-done.15.refs_15_), channel_id=1, source_target_pairs={{0,4},{4,0},{8,12},{12,8},{16,20},{20,16},{24,28},{28,24},{1,5},{5... | collective-permute-start | bytes 1572872 | tf_op jit(solution)/shard_map/ppermute | solution.py:13
  59.5 4.5 %collective-permute-start.18 = (bf16[64,128]{1,0:T(8,128)(2,1)S(1)}, bf16[64,128]{1,0:T(8,128)(2,1)S(1)}, u32[]{:S(2)}, u32[]{:S(2)}) collective-permute-start(bf16[64,128]{1,0:T(8,128)(2,1)S(1)} %get-tuple-element.63), channel_id=1, source_target_pairs={{0,1},{1,0},{2,3},{3,2},{4,5},{5,4},{6,7},{7,6},{8,9},{9,8},{10,11... | collective-permute-start | bytes 49160 | tf_op jit(solution)/shard_map/ppermute | solution.py:13
  61.2 4.7 %collective-permute-start.19 = (bf16[64,128]{1,0:T(8,128)(2,1)S(1)}, bf16[64,128]{1,0:T(8,128)(2,1)S(1)}, u32[]{:S(2)}, u32[]{:S(2)}) collective-permute-start(bf16[64,128]{1,0:T(8,128)(2,1)S(1)} %get-tuple-element.64), channel_id=1, source_target_pairs={{0,2},{1,3},{2,0},{3,1},{4,6},{5,7},{6,4},{7,5},{8,10},{9,11},{10,... | collective-permute-start | bytes 49160 | tf_op jit(solution)/shard_map/ppermute | solution.py:13
  63.8 5.5 %collective-permute-start.20 = (bf16[64,128]{1,0:T(8,128)(2,1)S(1)}, bf16[64,128]{1,0:T(8,128)(2,1)S(1)}, u32[]{:S(2)}, u32[]{:S(2)}) collective-permute-start(bf16[64,128]{1,0:T(8,128)(2,1)S(1)} %get-tuple-element.65), channel_id=1, source_target_pairs={{0,3},{1,2},{2,1},{3,0},{4,7},{5,6},{6,5},{7,4},{8,11},{9,10},{10,... | collective-permute-start | bytes 49160 | tf_op jit(solution)/shard_map/ppermute | solution.py:13
  73.3 4.5 %collective-permute-start.21 = (bf16[64,128]{1,0:T(8,128)(2,1)S(1)}, bf16[64,128]{1,0:T(8,128)(2,1)S(1)}, u32[]{:S(2)}, u32[]{:S(2)}) collective-permute-start(bf16[64,128]{1,0:T(8,128)(2,1)S(1)} %get-tuple-element.68), channel_id=1, source_target_pairs={{0,1},{1,0},{2,3},{3,2},{4,5},{5,4},{6,7},{7,6},{8,9},{9,8},{10,11... | collective-permute-start | bytes 49160 | tf_op jit(solution)/shard_map/ppermute | solution.py:13
  73.4 4.7 %collective-permute-start.22 = (bf16[64,128]{1,0:T(8,128)(2,1)S(1)}, bf16[64,128]{1,0:T(8,128)(2,1)S(1)}, u32[]{:S(2)}, u32[]{:S(2)}) collective-permute-start(bf16[64,128]{1,0:T(8,128)(2,1)S(1)} %get-tuple-element.69), channel_id=1, source_target_pairs={{0,2},{1,3},{2,0},{3,1},{4,6},{5,7},{6,4},{7,5},{8,10},{9,11},{10,... | collective-permute-start | bytes 49160 | tf_op jit(solution)/shard_map/ppermute | solution.py:13
  74.1 5.5 %collective-permute-start.23 = (bf16[64,128]{1,0:T(8,128)(2,1)S(1)}, bf16[64,128]{1,0:T(8,128)(2,1)S(1)}, u32[]{:S(2)}, u32[]{:S(2)}) collective-permute-start(bf16[64,128]{1,0:T(8,128)(2,1)S(1)} %get-tuple-element.70), channel_id=1, source_target_pairs={{0,3},{1,2},{2,1},{3,0},{4,7},{5,6},{6,5},{7,4},{8,11},{9,10},{10,... | collective-permute-start | bytes 49160 | tf_op jit(solution)/shard_map/ppermute | solution.py:13
  81.1 4.5 %collective-permute-start.24 = (bf16[64,128]{1,0:T(8,128)(2,1)S(1)}, bf16[64,128]{1,0:T(8,128)(2,1)S(1)}, u32[]{:S(2)}, u32[]{:S(2)}) collective-permute-start(bf16[64,128]{1,0:T(8,128)(2,1)S(1)} %get-tuple-element.73), channel_id=1, source_target_pairs={{0,1},{1,0},{2,3},{3,2},{4,5},{5,4},{6,7},{7,6},{8,9},{9,8},{10,11... | collective-permute-start | bytes 49160 | tf_op jit(solution)/shard_map/ppermute | solution.py:13
  81.5 5.5 %collective-permute-start.25 = (bf16[64,128]{1,0:T(8,128)(2,1)S(1)}, bf16[64,128]{1,0:T(8,128)(2,1)S(1)}, u32[]{:S(2)}, u32[]{:S(2)}) collective-permute-start(bf16[64,128]{1,0:T(8,128)(2,1)S(1)} %get-tuple-element.74), channel_id=1, source_target_pairs={{0,2},{1,3},{2,0},{3,1},{4,6},{5,7},{6,4},{7,5},{8,10},{9,11},{10,... | collective-permute-start | bytes 49160 | tf_op jit(solution)/shard_map/ppermute | solution.py:13
  85.3 5.5 %collective-permute-start.26 = (bf16[64,128]{1,0:T(8,128)(2,1)S(1)}, bf16[64,128]{1,0:T(8,128)(2,1)S(1)}, u32[]{:S(2)}, u32[]{:S(2)}) collective-permute-start(bf16[64,128]{1,0:T(8,128)(2,1)S(1)} %get-tuple-element.75), channel_id=1, source_target_pairs={{0,3},{1,2},{2,1},{3,0},{4,7},{5,6},{6,5},{7,4},{8,11},{9,10},{10,... | collective-permute-start | bytes 49160 | tf_op jit(solution)/shard_map/ppermute | solution.py:13
  94.4 4.5 %collective-permute-start.27 = (bf16[64,128]{1,0:T(8,128)(2,1)S(1)}, bf16[64,128]{1,0:T(8,128)(2,1)S(1)}, u32[]{:S(2)}, u32[]{:S(2)}) collective-permute-start(bf16[64,128]{1,0:T(8,128)(2,1)S(1)} %get-tuple-element.78), channel_id=1, source_target_pairs={{0,1},{1,0},{2,3},{3,2},{4,5},{5,4},{6,7},{7,6},{8,9},{9,8},{10,11... | collective-permute-start | bytes 49160 | tf_op jit(solution)/shard_map/ppermute | solution.py:13
  94.5 4.7 %collective-permute-start.28 = (bf16[64,128]{1,0:T(8,128)(2,1)S(1)}, bf16[64,128]{1,0:T(8,128)(2,1)S(1)}, u32[]{:S(2)}, u32[]{:S(2)}) collective-permute-start(bf16[64,128]{1,0:T(8,128)(2,1)S(1)} %get-tuple-element.79), channel_id=1, source_target_pairs={{0,2},{1,3},{2,0},{3,1},{4,6},{5,7},{6,4},{7,5},{8,10},{9,11},{10,... | collective-permute-start | bytes 49160 | tf_op jit(solution)/shard_map/ppermute | solution.py:13
  95.3 5.5 %collective-permute-start.29 = (bf16[64,128]{1,0:T(8,128)(2,1)S(1)}, bf16[64,128]{1,0:T(8,128)(2,1)S(1)}, u32[]{:S(2)}, u32[]{:S(2)}) collective-permute-start(bf16[64,128]{1,0:T(8,128)(2,1)S(1)} %get-tuple-element.80), channel_id=1, source_target_pairs={{0,3},{1,2},{2,1},{3,0},{4,7},{5,6},{6,5},{7,4},{8,11},{9,10},{10,... | collective-permute-start | bytes 49160 | tf_op jit(solution)/shard_map/ppermute | solution.py:13
  102.2 4.5 %collective-permute-start.30 = (bf16[64,128]{1,0:T(8,128)(2,1)S(1)}, bf16[64,128]{1,0:T(8,128)(2,1)S(1)}, u32[]{:S(2)}, u32[]{:S(2)}) collective-permute-start(bf16[64,128]{1,0:T(8,128)(2,1)S(1)} %get-tuple-element.83), channel_id=1, source_target_pairs={{0,1},{1,0},{2,3},{3,2},{4,5},{5,4},{6,7},{7,6},{8,9},{9,8},{10,11... | collective-permute-start | bytes 49160 | tf_op jit(solution)/shard_map/ppermute | solution.py:13
  102.7 5.5 %collective-permute-start.31 = (bf16[64,128]{1,0:T(8,128)(2,1)S(1)}, bf16[64,128]{1,0:T(8,128)(2,1)S(1)}, u32[]{:S(2)}, u32[]{:S(2)}) collective-permute-start(bf16[64,128]{1,0:T(8,128)(2,1)S(1)} %get-tuple-element.84), channel_id=1, source_target_pairs={{0,2},{1,3},{2,0},{3,1},{4,6},{5,7},{6,4},{7,5},{8,10},{9,11},{10,... | collective-permute-start | bytes 49160 | tf_op jit(solution)/shard_map/ppermute | solution.py:13
  106.5 5.5 %collective-permute-start.32 = (bf16[64,128]{1,0:T(8,128)(2,1)S(1)}, bf16[64,128]{1,0:T(8,128)(2,1)S(1)}, u32[]{:S(2)}, u32[]{:S(2)}) collective-permute-start(bf16[64,128]{1,0:T(8,128)(2,1)S(1)} %get-tuple-element.85), channel_id=1, source_target_pairs={{0,3},{1,2},{2,1},{3,0},{4,7},{5,6},{6,5},{7,4},{8,11},{9,10},{10,... | collective-permute-start | bytes 49160 | tf_op jit(solution)/shard_map/ppermute | solution.py:13
  115.1 4.5 %collective-permute-start.33 = (bf16[64,128]{1,0:T(8,128)(2,1)S(1)}, bf16[64,128]{1,0:T(8,128)(2,1)S(1)}, u32[]{:S(2)}, u32[]{:S(2)}) collective-permute-start(bf16[64,128]{1,0:T(8,128)(2,1)S(1)} %get-tuple-element.88), channel_id=1, source_target_pairs={{0,1},{1,0},{2,3},{3,2},{4,5},{5,4},{6,7},{7,6},{8,9},{9,8},{10,11... | collective-permute-start | bytes 49160 | tf_op jit(solution)/shard_map/ppermute | solution.py:13
  115.2 4.7 %collective-permute-start.34 = (bf16[64,128]{1,0:T(8,128)(2,1)S(1)}, bf16[64,128]{1,0:T(8,128)(2,1)S(1)}, u32[]{:S(2)}, u32[]{:S(2)}) collective-permute-start(bf16[64,128]{1,0:T(8,128)(2,1)S(1)} %get-tuple-element.89), channel_id=1, source_target_pairs={{0,2},{1,3},{2,0},{3,1},{4,6},{5,7},{6,4},{7,5},{8,10},{9,11},{10,... | collective-permute-start | bytes 49160 | tf_op jit(solution)/shard_map/ppermute | solution.py:13
  116.0 5.5 %collective-permute-start.35 = (bf16[64,128]{1,0:T(8,128)(2,1)S(1)}, bf16[64,128]{1,0:T(8,128)(2,1)S(1)}, u32[]{:S(2)}, u32[]{:S(2)}) collective-permute-start(bf16[64,128]{1,0:T(8,128)(2,1)S(1)} %get-tuple-element.90), channel_id=1, source_target_pairs={{0,3},{1,2},{2,1},{3,0},{4,7},{5,6},{6,5},{7,4},{8,11},{9,10},{10,... | collective-permute-start | bytes 49160 | tf_op jit(solution)/shard_map/ppermute | solution.py:13
  123.8 4.5 %collective-permute-start.36 = (bf16[64,128]{1,0:T(8,128)(2,1)S(1)}, bf16[64,128]{1,0:T(8,128)(2,1)S(1)}, u32[]{:S(2)}, u32[]{:S(2)}) collective-permute-start(bf16[64,128]{1,0:T(8,128)(2,1)S(1)} %get-tuple-element.93), channel_id=1, source_target_pairs={{0,1},{1,0},{2,3},{3,2},{4,5},{5,4},{6,7},{7,6},{8,9},{9,8},{10,11... | collective-permute-start | bytes 49160 | tf_op jit(solution)/shard_map/ppermute | solution.py:13
  124.2 5.5 %collective-permute-start.37 = (bf16[64,128]{1,0:T(8,128)(2,1)S(1)}, bf16[64,128]{1,0:T(8,128)(2,1)S(1)}, u32[]{:S(2)}, u32[]{:S(2)}) collective-permute-start(bf16[64,128]{1,0:T(8,128)(2,1)S(1)} %get-tuple-element.94), channel_id=1, source_target_pairs={{0,2},{1,3},{2,0},{3,1},{4,6},{5,7},{6,4},{7,5},{8,10},{9,11},{10,... | collective-permute-start | bytes 49160 | tf_op jit(solution)/shard_map/ppermute | solution.py:13
  128.0 5.5 %collective-permute-start.38 = (bf16[64,128]{1,0:T(8,128)(2,1)S(1)}, bf16[64,128]{1,0:T(8,128)(2,1)S(1)}, u32[]{:S(2)}, u32[]{:S(2)}) collective-permute-start(bf16[64,128]{1,0:T(8,128)(2,1)S(1)} %get-tuple-element.95), channel_id=1, source_target_pairs={{0,3},{1,2},{2,1},{3,0},{4,7},{5,6},{6,5},{7,4},{8,11},{9,10},{10,... | collective-permute-start | bytes 49160 | tf_op jit(solution)/shard_map/ppermute | solution.py:13
  135.4 4.5 %collective-permute-start.39 = (bf16[64,128]{1,0:T(8,128)(2,1)S(1)}, bf16[64,128]{1,0:T(8,128)(2,1)S(1)}, u32[]{:S(2)}, u32[]{:S(2)}) collective-permute-start(bf16[64,128]{1,0:T(8,128)(2,1)S(1)} %get-tuple-element.98), channel_id=1, source_target_pairs={{0,1},{1,0},{2,3},{3,2},{4,5},{5,4},{6,7},{7,6},{8,9},{9,8},{10,11... | collective-permute-start | bytes 49160 | tf_op jit(solution)/shard_map/ppermute | solution.py:13
  135.5 4.7 %collective-permute-start.40 = (bf16[64,128]{1,0:T(8,128)(2,1)S(1)}, bf16[64,128]{1,0:T(8,128)(2,1)S(1)}, u32[]{:S(2)}, u32[]{:S(2)}) collective-permute-start(bf16[64,128]{1,0:T(8,128)(2,1)S(1)} %get-tuple-element.99), channel_id=1, source_target_pairs={{0,2},{1,3},{2,0},{3,1},{4,6},{5,7},{6,4},{7,5},{8,10},{9,11},{10,... | collective-permute-start | bytes 49160 | tf_op jit(solution)/shard_map/ppermute | solution.py:13
  136.3 5.5 %collective-permute-start.41 = (bf16[64,128]{1,0:T(8,128)(2,1)S(1)}, bf16[64,128]{1,0:T(8,128)(2,1)S(1)}, u32[]{:S(2)}, u32[]{:S(2)}) collective-permute-start(bf16[64,128]{1,0:T(8,128)(2,1)S(1)} %get-tuple-element.100), channel_id=1, source_target_pairs={{0,3},{1,2},{2,1},{3,0},{4,7},{5,6},{6,5},{7,4},{8,11},{9,10},{10,... | collective-permute-start | bytes 49160 | tf_op jit(solution)/shard_map/ppermute | solution.py:13
  143.7 4.5 %collective-permute-start.42 = (bf16[64,128]{1,0:T(8,128)(2,1)S(1)}, bf16[64,128]{1,0:T(8,128)(2,1)S(1)}, u32[]{:S(2)}, u32[]{:S(2)}) collective-permute-start(bf16[64,128]{1,0:T(8,128)(2,1)S(1)} %get-tuple-element.103), channel_id=1, source_target_pairs={{0,1},{1,0},{2,3},{3,2},{4,5},{5,4},{6,7},{7,6},{8,9},{9,8},{10,11... | collective-permute-start | bytes 49160 | tf_op jit(solution)/shard_map/ppermute | solution.py:13
  144.1 5.5 %collective-permute-start.43 = (bf16[64,128]{1,0:T(8,128)(2,1)S(1)}, bf16[64,128]{1,0:T(8,128)(2,1)S(1)}, u32[]{:S(2)}, u32[]{:S(2)}) collective-permute-start(bf16[64,128]{1,0:T(8,128)(2,1)S(1)} %get-tuple-element.104), channel_id=1, source_target_pairs={{0,2},{1,3},{2,0},{3,1},{4,6},{5,7},{6,4},{7,5},{8,10},{9,11},{10,... | collective-permute-start | bytes 49160 | tf_op jit(solution)/shard_map/ppermute | solution.py:13
  147.9 5.5 %collective-permute-start.44 = (bf16[64,128]{1,0:T(8,128)(2,1)S(1)}, bf16[64,128]{1,0:T(8,128)(2,1)S(1)}, u32[]{:S(2)}, u32[]{:S(2)}) collective-permute-start(bf16[64,128]{1,0:T(8,128)(2,1)S(1)} %get-tuple-element.105), channel_id=1, source_target_pairs={{0,3},{1,2},{2,1},{3,0},{4,7},{5,6},{6,5},{7,4},{8,11},{9,10},{10,... | collective-permute-start | bytes 49160 | tf_op jit(solution)/shard_map/ppermute | solution.py:13
  154.5 4.5 %collective-permute-start.45 = (bf16[64,128]{1,0:T(8,128)(2,1)S(1)}, bf16[64,128]{1,0:T(8,128)(2,1)S(1)}, u32[]{:S(2)}, u32[]{:S(2)}) collective-permute-start(bf16[64,128]{1,0:T(8,128)(2,1)S(1)} %get-tuple-element.108), channel_id=1, source_target_pairs={{0,1},{1,0},{2,3},{3,2},{4,5},{5,4},{6,7},{7,6},{8,9},{9,8},{10,11... | collective-permute-start | bytes 49160 | tf_op jit(solution)/shard_map/ppermute | solution.py:13
  154.5 4.7 %collective-permute-start.46 = (bf16[64,128]{1,0:T(8,128)(2,1)S(1)}, bf16[64,128]{1,0:T(8,128)(2,1)S(1)}, u32[]{:S(2)}, u32[]{:S(2)}) collective-permute-start(bf16[64,128]{1,0:T(8,128)(2,1)S(1)} %get-tuple-element.109), channel_id=1, source_target_pairs={{0,2},{1,3},{2,0},{3,1},{4,6},{5,7},{6,4},{7,5},{8,10},{9,11},{10,... | collective-permute-start | bytes 49160 | tf_op jit(solution)/shard_map/ppermute | solution.py:13
  155.3 5.5 %collective-permute-start.47 = (bf16[64,128]{1,0:T(8,128)(2,1)S(1)}, bf16[64,128]{1,0:T(8,128)(2,1)S(1)}, u32[]{:S(2)}, u32[]{:S(2)}) collective-permute-start(bf16[64,128]{1,0:T(8,128)(2,1)S(1)} %get-tuple-element.110), channel_id=1, source_target_pairs={{0,3},{1,2},{2,1},{3,0},{4,7},{5,6},{6,5},{7,4},{8,11},{9,10},{10,... | collective-permute-start | bytes 49160 | tf_op jit(solution)/shard_map/ppermute | solution.py:13
  161.9 4.5 %collective-permute-start.48 = (bf16[64,128]{1,0:T(8,128)(2,1)S(1)}, bf16[64,128]{1,0:T(8,128)(2,1)S(1)}, u32[]{:S(2)}, u32[]{:S(2)}) collective-permute-start(bf16[64,128]{1,0:T(8,128)(2,1)S(1)} %get-tuple-element.113), channel_id=1, source_target_pairs={{0,1},{1,0},{2,3},{3,2},{4,5},{5,4},{6,7},{7,6},{8,9},{9,8},{10,11... | collective-permute-start | bytes 49160 | tf_op jit(solution)/shard_map/ppermute | solution.py:13
  162.3 5.5 %collective-permute-start.49 = (bf16[64,128]{1,0:T(8,128)(2,1)S(1)}, bf16[64,128]{1,0:T(8,128)(2,1)S(1)}, u32[]{:S(2)}, u32[]{:S(2)}) collective-permute-start(bf16[64,128]{1,0:T(8,128)(2,1)S(1)} %get-tuple-element.114), channel_id=1, source_target_pairs={{0,2},{1,3},{2,0},{3,1},{4,6},{5,7},{6,4},{7,5},{8,10},{9,11},{10,... | collective-permute-start | bytes 49160 | tf_op jit(solution)/shard_map/ppermute | solution.py:13
  166.1 5.5 %collective-permute-start.50 = (bf16[64,128]{1,0:T(8,128)(2,1)S(1)}, bf16[64,128]{1,0:T(8,128)(2,1)S(1)}, u32[]{:S(2)}, u32[]{:S(2)}) collective-permute-start(bf16[64,128]{1,0:T(8,128)(2,1)S(1)} %get-tuple-element.115), channel_id=1, source_target_pairs={{0,3},{1,2},{2,1},{3,0},{4,7},{5,6},{6,5},{7,4},{8,11},{9,10},{10,... | collective-permute-start | bytes 49160 | tf_op jit(solution)/shard_map/ppermute | solution.py:13
  172.2 5.8 %collective-permute-start.53 = (f32[64,128]{1,0:T(8,128)S(1)}, f32[64,128]{1,0:T(8,128)S(1)}, u32[]{:S(2)}, u32[]{:S(2)}) collective-permute-start(f32[64,128]{1,0:T(8,128)S(1)} %shard_map.97), channel_id=1, source_target_pairs={{0,3},{1,2},{2,1},{3,0},{4,7},{5,6},{6,5},{7,4},{8,11},{9,10},{10,... | collective-permute-start | bytes 98312 | tf_op jit(solution)/shard_map/ppermute | solution.py:13
  172.5 5.5 %collective-permute-start.52 = (f32[64,128]{1,0:T(8,128)S(1)}, f32[64,128]{1,0:T(8,128)S(1)}, u32[]{:S(2)}, u32[]{:S(2)}) collective-permute-start(f32[64,128]{1,0:T(8,128)S(1)} %shard_map.97), channel_id=1, source_target_pairs={{0,2},{1,3},{2,0},{3,1},{4,6},{5,7},{6,4},{7,5},{8,10},{9,11},{10,... | collective-permute-start | bytes 98312 | tf_op jit(solution)/shard_map/ppermute | solution.py:13
  172.5 6.1 %collective-permute-start.51 = (f32[64,128]{1,0:T(8,128)S(1)}, f32[64,128]{1,0:T(8,128)S(1)}, u32[]{:S(2)}, u32[]{:S(2)}) collective-permute-start(f32[64,128]{1,0:T(8,128)S(1)} %shard_map.97), channel_id=1, source_target_pairs={{0,1},{1,0},{2,3},{3,2},{4,5},{5,4},{6,7},{7,6},{8,9},{9,8},{10,11... | collective-permute-start | bytes 98312 | tf_op jit(solution)/shard_map/ppermute | solution.py:13

commit v4 on v3

--- a/solution.py
+++ b/solution.py
@@ -1,4 +1,5 @@
 import functools
+import math
 
 import jax
 import jax.numpy as jnp
@@ -49,50 +50,66 @@
     return sum(part.size * part.dtype.itemsize for part in parts) * 5 // 4 + (2 << 20)
 
 
-def load_operator(scalars, slot_of, dims, parts):
+def load_blocks(scalars, slot_of, extras, dims, which, parts, whole, last):
     rows, cols, groups, per_row, slots, block = dims
     half = per_row // 2
+    dtype = parts[0].dtype
 
     def body(*refs):
-        sc, slots_own = refs[0], refs[1]
-        part_refs = refs[2:2 + 2 * rows]
-        whole, diag, sems = refs[2 + 2 * rows:]
+        sc, slots_own = refs[:2]
+        part_refs = refs[2:2 + len(parts)]
+        outs = refs[len(args):]
+        out = outs[0]
         row = sc[0]
-        col = sc[1]
-        op = sc[2]
-        copies = []
-        for k in range(rows):
-            for h in range(2):
-                copies.append(
-                    pltpu.make_async_copy(
-                        part_refs[2 * k + h], whole.at[pl.ds(h * half, half), row ^ k], sems.at[2 * k + h]
-                    )
-                )
-                copies[-1].start()
-        for copy in copies:
-            copy.wait()
-        row_i = lax.broadcasted_iota(jnp.int32, (block, block), 0)
-        col_i = lax.broadcasted_iota(jnp.int32, (block, block), 1)
-        ahead = jnp.where(op == 0, row_i - col_i, col_i - row_i) > 0
-        for m in range(groups):
-            for i in range(per_row):
-                value = whole[i, col + cols * m, slots_own[m * per_row + i]].astype(jnp.float32)
-                diag[m, i] = jnp.where(ahead, value, 0.0).astype(diag.dtype)
+        for n in range(len(parts)):
+            def move(i, carry, n=n):
+                for s in range(slots):
+                    out[n % 2 * half + i, row ^ which[n // 2], s] = part_refs[n][i, s].T
+                return carry
+
+            lax.fori_loop(0, half, move, 0, unroll=2)
+        if last:
+            diag = outs[1]
+            col = sc[1]
+            op = sc[2]
+            row_i = lax.broadcasted_iota(jnp.int32, (block, block), 0)
+            col_i = lax.broadcasted_iota(jnp.int32, (block, block), 1)
+            ahead = jnp.where(op == 0, col_i - row_i, row_i - col_i) > 0
+            for m in range(groups):
+                for i in range(per_row):
+                    value = out[i, col + cols * m, slots_own[m * per_row + i]].astype(jnp.float32)
+                    diag[m, i] = jnp.where(ahead, value, 0.0).astype(dtype)
 
     vmem = pl.BlockSpec(memory_space=pltpu.VMEM)
     smem = pl.BlockSpec(memory_space=pltpu.SMEM)
+    hbm = pl.BlockSpec(memory_space=pl.ANY)
+    args = [scalars, slot_of, *parts, *extras] + ([] if whole is None else [whole])
+    shapes = [jax.ShapeDtypeStruct((per_row, rows, slots, block, block), dtype)]
+    if last:
+        shapes.append(jax.ShapeDtypeStruct((groups, per_row, block, block), dtype))
+    need = sum(math.prod(shape.shape) for shape in shapes) + sum(part.size for part in parts)
     return pl.pallas_call(
         body,
-        out_shape=[
-            jax.ShapeDtypeStruct((per_row, rows, slots, block, block), parts[0].dtype),
-            jax.ShapeDtypeStruct((groups, per_row, block, block), parts[0].dtype),
-        ],
-        in_specs=[smem, smem] + [pl.BlockSpec(memory_space=pl.ANY)] * len(parts),
-        out_specs=[vmem, vmem],
-        scratch_shapes=[pltpu.SemaphoreType.DMA((len(parts),))],
-        compiler_params=pltpu.CompilerParams(vmem_limit_bytes=vmem_budget(parts)),
-        name="load_operator",
-    )(scalars, slot_of, *parts)
+        out_shape=shapes,
+        in_specs=[smem] * 2 + [vmem] * len(parts) + [hbm] * (len(args) - 2 - len(parts)),
+        out_specs=[vmem] * len(shapes),
+        input_output_aliases={} if whole is None else {len(args) - 1: 0},
+        compiler_params=pltpu.CompilerParams(vmem_limit_bytes=need * dtype.itemsize + (2 << 20)),
+        name="load_blocks",
+    )(*args)
+
+
+def load_operator(scalars, slot_of, extras, dims, parts):
+    early = [k for k in range(dims[0]) if (k >> 1) & ((k >> 1) - 1) == 0]
+    late = [k for k in range(dims[0]) if k not in early]
+    stages = [which for which in (early, late) if which]
+    loaded = [None]
+    for n, which in enumerate(stages):
+        chosen = [part for k in which for part in parts[2 * k:2 * k + 2]]
+        loaded = load_blocks(
+            scalars, slot_of, extras if n == 0 else [], dims, which, chosen, loaded[0], n + 1 == len(stages)
+        )
+    return loaded
 
 
 def step_kernel(kind, step, dims, scalars, table, operator, level, pivot, state, received):
@@ -112,7 +129,7 @@
         level_ref = refs.pop(0)
         pivot_ref = refs.pop(0)
         res_ref = refs.pop(0)
-        sol_ref = refs.pop(0)
+        sol_ref = refs.pop(0) if len(state) > 1 else None
         got = [refs.pop(0) for _ in received]
         if kind == "last":
             out_sol = refs.pop(0)
@@ -129,7 +146,7 @@
         if kind in ("solved", "last"):
             rounded = res.astype(jnp.bfloat16).astype(jnp.float32)
             y = jnp.where(lv == step, total + pivot_ref[...] * rounded, 0.0)
-            sol = sol_ref[...] + y
+            sol = y if sol_ref is None else sol_ref[...] + y
             if kind == "last":
                 out_sol[...] = sol
                 return
@@ -162,7 +179,7 @@
 
         def contract(x, w):
             return lax.dot_general(
-                x.astype(jnp.bfloat16), w, (((1,), (1,)), ((), ())), preferred_element_type=jnp.float32
+                x.astype(jnp.bfloat16), w, (((1,), (0,)), ((), ())), preferred_element_type=jnp.float32
             )
 
         def group(i, carry):
@@ -174,10 +191,10 @@
                     for s in range(slots):
                         left.append(xs[m, idx[(i * rows + k) * slots + s]])
                         right.append(whole[i, k, s])
-                acc[cc, i] = contract(jnp.concatenate(left, axis=1), jnp.concatenate(right, axis=1))
+                acc[cc, i] = contract(jnp.concatenate(left, axis=1), jnp.concatenate(right, axis=0))
             left = [xs[m, i * groups + m] for m in range(groups)]
             right = [diag[m, i] for m in range(groups)]
-            acc[col, i] += contract(jnp.concatenate(left, axis=1), jnp.concatenate(right, axis=1))
+            acc[col, i] += contract(jnp.concatenate(left, axis=1), jnp.concatenate(right, axis=0))
             return carry
 
         lax.fori_loop(sc[which], sc[which + 1], group, 0)
@@ -292,7 +309,7 @@
     chosen = lax.dynamic_slice_in_dim(chosen, (r // 2) * kept, kept, 0)
     chosen = chosen.reshape(kept, per_row, groups, block).transpose(1, 2, 0, 3).reshape(-1, block)
 
-    operator = load_operator(scalars, slot_of, dims, parts)
+    operator = load_operator(scalars, slot_of, [table, level, pivot, chosen], dims, parts)
     run = functools.partial(
         step_kernel,
         dims=dims + (kept,),
@@ -310,11 +327,10 @@
         return got
 
     res = chosen
-    sol = jnp.zeros(chosen.shape, jnp.float32)
-    *sends, res = run("first", 0, state=(res, sol), received=[])
+    *sends, res = run("first", 0, state=(res,), received=[])
     for step in range(steps - 1):
-        *sends, sol = run("solved", step, state=(res, sol), received=exchange(sends))
-        *sends, res = run("updated", step, state=(res, sol), received=exchange(sends))
+        *sends, sol = run("solved", step, state=(res, sol) if step else (res,), received=exchange(sends))
+        *sends, res = run("updated", step, state=(res,), received=exchange(sends))
     sol = run("last", steps - 1, state=(res, sol), received=exchange(sends))
 
     whole = jnp.stack(exchange([sol] * cols))

time: 189 us -> 182 us (0.963)
  waiting for transfers between devices: 75 us -> 71.3 us
    pallas_call x12, Pallas kernels: 23 us -> 17.4 us  [step_kernel(): pl.pallas_call(body, out_shape=out_shape, in_specs=[smem, smem] + [vmem]...]
    pallas_call x1 -> x2, Pallas kernels: 3.47 us -> 7.38 us  [load_blocks(): pl.pallas_call(body, out_shape=shapes, in_specs=[smem] * 2 + [vmem] * len...]
    ppermute x54, waiting for transfers between devices: 75 us -> 71.3 us  [xor_permute(): return lax.ppermute(value, axis, [(i, i ^ distance) for i in range(size)])]
  transfers between devices with their start and end apart: 54 -> 54, of which waited for: 32 -> 28; matrix products, arithmetic and copies ran while one was open for 4% -> 4% of each run, Pallas kernels for 0% -> 3%
where the time goes in v4:
time: 182 us
  waiting for transfers between devices  71.3 us (39%)
  starting transfers between devices  65.8 us (36%)
  Pallas kernels  24.8 us (14%)
  blocking collectives  8.68 us (5%)
  other arithmetic  6.8 us (4%)
  local copies, waits for them, and re-layouts  3.48 us (2%)
    ppermute x54, waiting for transfers between devices, xor_permute(): return lax.ppermute(value, axis, [(i, i ^ distance) for i in range(size)])  71.3 us
    ppermute x54, starting transfers between devices, xor_permute(): return lax.ppermute(value, axis, [(i, i ^ distance) for i in range(size)])  65.8 us
    pallas_call x12, Pallas kernels, step_kernel(): pl.pallas_call(body, out_shape=out_shape, in_specs=[smem, smem] + [vmem]...  17.4 us
    all_to_all x1, blocking collectives, shards(): lax.all_to_all(whole, 'row', 0, 0)  8.68 us
    pallas_call x2, Pallas kernels, load_blocks(): pl.pallas_call(body, out_shape=shapes, in_specs=[smem] * 2 + [vmem] * len...  7.38 us
  transfers between devices with their start and end apart: 54, of which 28 were waited for; matrix products, arithmetic and copies ran while one was open for 4% of the time, Pallas kernels for 3%

profile of v4, /device:TPU:0, one launch (start us, length us, event | category | flops | bytes accessed | tf_op | source)
XLA Modules:
  0.0 181.8 jit_solution(9789728534831043826)
XLA Ops:
  2.1 3.0 %collective-permute-start = (f32[8,256]{1,0:T(8,128)S(1)}, f32[8,256]{1,0:T(8,128)S(1)}, u32[]{:S(2)}, u32[]{:S(2)}) collective-permute-start(f32[8,256]{1,0:T(8,128)S(1)} %get-tuple-element.129), channel_id=1, source_target_pairs={{0,8},{4,12},{8,0},{12,4},{16,24},{20,28},{24,16},{28,20},{1,9},{5... | collective-permute-start | bytes 24584 | tf_op jit(solution)/shard_map/ppermute | solution.py:14
  5.1 1.5 collective-permute-start.1
  6.6 1.3 fusion.11
  7.9 2.1 %collective-permute-start.6 = (bf16[4,4,128,128]{3,2,1,0:T(8,128)(2,1)S(1)}, bf16[4,4,128,128]{3,2,1,0:T(8,128)(2,1)S(1)}, u32[]{:S(2)}, u32[]{:S(2)}) collective-permute-start(bf16[4,4,128,128]{3,2,1,0:T(8,128)(2,1)S(1)} %get-tuple-element.122.refs_3_), channel_id=1, source_target_pairs={{0,16},{4,20},{8,24},{12,28},{16,0},{20,4},{24,8},{28,12},{1,17},{... | collective-permute-start | bytes 1572872 | tf_op jit(solution)/shard_map/ppermute | solution.py:14
  9.9 1.5 collective-permute-start.12
  11.4 0.8 select_reduce_fusion.6
  12.3 1.1 select_reduce_fusion.3
  13.9 0.8 dynamic-slice_select_fusion
  15.7 1.1 collective-permute-done.3
  17.0 16.7 %collective-permute-done.4.refs_6_ = bf16[4,4,128,128]{3,2,1,0:T(8,128)(2,1)S(1)} collective-permute-done((bf16[4,4,128,128]{3,2,1,0:T(8,128)(2,1)S(1)}, bf16[4,4,128,128]{3,2,1,0:T(8,128)(2,1)S(1)}, u32[]{:S(2)}, u32[]{:S(2)}) %collective-permute-start.4) | collective-permute-done | bytes 524320 | tf_op jit(solution)/shard_map/ppermute | solution.py:14
  34.7 1.6 collective-permute-start.7
  36.4 1.9 %select_reduce_fusion.1 = (s32[8,8,4]{1,2,0:T(4,128)S(1)}, s32[8,8,4]{1,2,0:T(4,128)S(1)}) fusion(s32[64]{0:T(128)} %param.11, s32[8,8,4]{1,2,0:T(4,128)S(1)} %bitcast.113, s32[64]{0:T(128)S(1)} %broadcast_select_fusion), kind=kLoop, calls=%fused_computation.5 | loop fusion | flops 81408 | bytes 3584 | tf_op jit(solution)/shard_map/reduce_sum | solution.py:262
  38.9 9.3 %collective-permute-done.5.refs_2_ = bf16[4,4,128,128]{3,2,1,0:T(8,128)(2,1)} collective-permute-done((bf16[4,4,128,128]{3,2,1,0:T(8,128)(2,1)S(1)}, bf16[4,4,128,128]{3,2,1,0:T(8,128)(2,1)}, u32[]{:S(2)}, u32[]{:S(2)}) %collective-permute-start.5) | collective-permute-done | bytes 524320 | tf_op jit(solution)/shard_map/ppermute | solution.py:14
  49.4 4.8 %load_blocks.2.refs_6_ = bf16[8,8,4,128,128]{4,3,2,1,0:T(8,128)(2,1)S(1)} custom-call(s32[27]{0:T(128)S(1)} %pad_add_fusion.1.refs_0_, s32[16]{0:T(128)S(1)} %reshape.341.refs_1_, bf16[4,4,128,128]{3,2,1,0:T(8,128)(2,1)S(1)} %get-tuple-element.123.refs_2_, bf16[4,4,128,128]{3,2,1,0:T(8,128)(2,1)S(1)} %get-tuple-element.122.refs_3_, ...), custom_call_target="tpu_custom_call" | custom-call | tf_op jit(solution)/shard_map/load_blocks/pallas_call | solution.py:91
  54.2 2.6 %load_blocks.3 = (bf16[8,8,4,128,128]{4,3,2,1,0:T(8,128)(2,1)S(1)}, bf16[2,8,128,128]{3,2,1,0:T(8,128)(2,1)S(1)}) custom-call(s32[27]{0:T(128)S(1)} %pad_add_fusion.1.refs_0_, s32[16]{0:T(128)S(1)} %reshape.341.refs_1_, bf16[4,4,128,128]{3,2,1,0:T(8,128)(2,1)} %collective-permute-done.5.refs_2_, ...), custom_call_target="tpu_custom_call", output_to_operand_aliasing={{0}: (6, {})} | custom-call | tf_op jit(solution)/shard_map/load_blocks/pallas_call | solution.py:91
  56.8 0.9 shard_map.86
  57.7 1.6 collective-permute-start.18
  59.3 2.6 %collective-permute-start.19 = (bf16[64,128]{1,0:T(8,128)(2,1)S(1)}, bf16[64,128]{1,0:T(8,128)(2,1)S(1)}, u32[]{:S(2)}, u32[]{:S(2)}) collective-permute-start(bf16[64,128]{1,0:T(8,128)(2,1)S(1)} %get-tuple-element.64), channel_id=1, source_target_pairs={{0,2},{1,3},{2,0},{3,1},{4,6},{5,7},{6,4},{7,5},{8,10},{9,11},{10,... | collective-permute-start | bytes 49160 | tf_op jit(solution)/shard_map/ppermute | solution.py:14
  62.1 1.9 %collective-permute-done.19.refs_9_ = bf16[64,128]{1,0:T(8,128)(2,1)S(1)} collective-permute-done((bf16[64,128]{1,0:T(8,128)(2,1)S(1)}, bf16[64,128]{1,0:T(8,128)(2,1)S(1)}, u32[]{:S(2)}, u32[]{:S(2)}) %collective-permute-start.19) | collective-permute-done | bytes 16416 | tf_op jit(solution)/shard_map/ppermute | solution.py:14
  64.0 3.4 %collective-permute-done.20.refs_10_ = bf16[64,128]{1,0:T(8,128)(2,1)S(1)} collective-permute-done((bf16[64,128]{1,0:T(8,128)(2,1)S(1)}, bf16[64,128]{1,0:T(8,128)(2,1)S(1)}, u32[]{:S(2)}, u32[]{:S(2)}) %collective-permute-start.20) | collective-permute-done | bytes 16416 | tf_op jit(solution)/shard_map/ppermute | solution.py:14
  67.4 2.8 %shard_map.87 = (f32[64,128]{1,0:T(8,128)S(1)}, bf16[64,128]{1,0:T(8,128)(2,1)S(1)}, bf16[64,128]{1,0:T(8,128)(2,1)S(1)}, bf16[64,128]{1,0:T(8,128)(2,1)S(1)}, f32[64,128]{1,0:T(8,128)S(1)}) custom-call(s32[27]{0:T(128)S(1)} %pad_add_fusion.1.refs_0_, s32[256]{0:T(256)S(1)} %reshape.338.refs_14_.refs_1_, ...), custom_call_target="tpu_custom_call" | custom-call | tf_op jit(solution)/shard_map/pallas_call | solution.py:223
  70.3 0.8 collective-permute-start.22
  71.1 3.6 %collective-permute-start.23 = (bf16[64,128]{1,0:T(8,128)(2,1)S(1)}, bf16[64,128]{1,0:T(8,128)(2,1)S(1)}, u32[]{:S(2)}, u32[]{:S(2)}) collective-permute-start(bf16[64,128]{1,0:T(8,128)(2,1)S(1)} %get-tuple-element.69), channel_id=1, source_target_pairs={{0,3},{1,2},{2,1},{3,0},{4,7},{5,6},{6,5},{7,4},{8,11},{9,10},{10,... | collective-permute-start | bytes 49160 | tf_op jit(solution)/shard_map/ppermute | solution.py:14
  75.0 1.6 collective-permute-done.23.refs_10_
  76.6 1.1 shard_map.88
  78.2 3.9 %collective-permute-start.25 = (bf16[64,128]{1,0:T(8,128)(2,1)S(1)}, bf16[64,128]{1,0:T(8,128)(2,1)S(1)}, u32[]{:S(2)}, u32[]{:S(2)}) collective-permute-start(bf16[64,128]{1,0:T(8,128)(2,1)S(1)} %get-tuple-element.74), channel_id=1, source_target_pairs={{0,2},{1,3},{2,0},{3,1},{4,6},{5,7},{6,4},{7,5},{8,10},{9,11},{10,... | collective-permute-start | bytes 49160 | tf_op jit(solution)/shard_map/ppermute | solution.py:14
  82.2 1.5 collective-permute-done.25.refs_10_
  83.7 3.8 %collective-permute-done.26.refs_11_ = bf16[64,128]{1,0:T(8,128)(2,1)S(1)} collective-permute-done((bf16[64,128]{1,0:T(8,128)(2,1)S(1)}, bf16[64,128]{1,0:T(8,128)(2,1)S(1)}, u32[]{:S(2)}, u32[]{:S(2)}) %collective-permute-start.26) | collective-permute-done | bytes 16416 | tf_op jit(solution)/shard_map/ppermute | solution.py:14
  87.6 2.5 %shard_map.89 = (f32[64,128]{1,0:T(8,128)S(1)}, bf16[64,128]{1,0:T(8,128)(2,1)S(1)}, bf16[64,128]{1,0:T(8,128)(2,1)S(1)}, bf16[64,128]{1,0:T(8,128)(2,1)S(1)}, f32[64,128]{1,0:T(8,128)S(1)}) custom-call(s32[27]{0:T(128)S(1)} %pad_add_fusion.1.refs_0_, s32[256]{0:T(256)S(1)} %reshape.338.refs_14_.refs_1_, ...), custom_call_target="tpu_custom_call" | custom-call | tf_op jit(solution)/shard_map/pallas_call | solution.py:223
  90.2 0.7 collective-permute-start.28
  90.9 3.6 %collective-permute-start.29 = (bf16[64,128]{1,0:T(8,128)(2,1)S(1)}, bf16[64,128]{1,0:T(8,128)(2,1)S(1)}, u32[]{:S(2)}, u32[]{:S(2)}) collective-permute-start(bf16[64,128]{1,0:T(8,128)(2,1)S(1)} %get-tuple-element.79), channel_id=1, source_target_pairs={{0,3},{1,2},{2,1},{3,0},{4,7},{5,6},{6,5},{7,4},{8,11},{9,10},{10,... | collective-permute-start | bytes 49160 | tf_op jit(solution)/shard_map/ppermute | solution.py:14
  94.9 1.9 %collective-permute-done.29.refs_10_ = bf16[64,128]{1,0:T(8,128)(2,1)S(1)} collective-permute-done((bf16[64,128]{1,0:T(8,128)(2,1)S(1)}, bf16[64,128]{1,0:T(8,128)(2,1)S(1)}, u32[]{:S(2)}, u32[]{:S(2)}) %collective-permute-start.29) | collective-permute-done | bytes 16416 | tf_op jit(solution)/shard_map/ppermute | solution.py:14
  96.7 1.1 shard_map.90
  98.3 3.7 %collective-permute-start.31 = (bf16[64,128]{1,0:T(8,128)(2,1)S(1)}, bf16[64,128]{1,0:T(8,128)(2,1)S(1)}, u32[]{:S(2)}, u32[]{:S(2)}) collective-permute-start(bf16[64,128]{1,0:T(8,128)(2,1)S(1)} %get-tuple-element.84), channel_id=1, source_target_pairs={{0,2},{1,3},{2,0},{3,1},{4,6},{5,7},{6,4},{7,5},{8,10},{9,11},{10,... | collective-permute-start | bytes 49160 | tf_op jit(solution)/shard_map/ppermute | solution.py:14
  102.3 1.4 collective-permute-done.31.refs_10_
  103.7 3.8 %collective-permute-done.32.refs_11_ = bf16[64,128]{1,0:T(8,128)(2,1)S(1)} collective-permute-done((bf16[64,128]{1,0:T(8,128)(2,1)S(1)}, bf16[64,128]{1,0:T(8,128)(2,1)S(1)}, u32[]{:S(2)}, u32[]{:S(2)}) %collective-permute-start.32) | collective-permute-done | bytes 16416 | tf_op jit(solution)/shard_map/ppermute | solution.py:14
  107.5 2.2 %shard_map.91 = (f32[64,128]{1,0:T(8,128)S(1)}, bf16[64,128]{1,0:T(8,128)(2,1)S(1)}, bf16[64,128]{1,0:T(8,128)(2,1)S(1)}, bf16[64,128]{1,0:T(8,128)(2,1)S(1)}, f32[64,128]{1,0:T(8,128)S(1)}) custom-call(s32[27]{0:T(128)S(1)} %pad_add_fusion.1.refs_0_, s32[256]{0:T(256)S(1)} %reshape.338.refs_14_.refs_1_, ...), custom_call_target="tpu_custom_call" | custom-call | tf_op jit(solution)/shard_map/pallas_call | solution.py:223
  109.9 0.9 collective-permute-start.34
  110.7 3.5 %collective-permute-start.35 = (bf16[64,128]{1,0:T(8,128)(2,1)S(1)}, bf16[64,128]{1,0:T(8,128)(2,1)S(1)}, u32[]{:S(2)}, u32[]{:S(2)}) collective-permute-start(bf16[64,128]{1,0:T(8,128)(2,1)S(1)} %get-tuple-element.89), channel_id=1, source_target_pairs={{0,3},{1,2},{2,1},{3,0},{4,7},{5,6},{6,5},{7,4},{8,11},{9,10},{10,... | collective-permute-start | bytes 49160 | tf_op jit(solution)/shard_map/ppermute | solution.py:14
  114.6 1.7 collective-permute-done.35.refs_10_
  116.3 1.7 shard_map.92
  118.3 3.9 %collective-permute-start.37 = (bf16[64,128]{1,0:T(8,128)(2,1)S(1)}, bf16[64,128]{1,0:T(8,128)(2,1)S(1)}, u32[]{:S(2)}, u32[]{:S(2)}) collective-permute-start(bf16[64,128]{1,0:T(8,128)(2,1)S(1)} %get-tuple-element.94), channel_id=1, source_target_pairs={{0,2},{1,3},{2,0},{3,1},{4,6},{5,7},{6,4},{7,5},{8,10},{9,11},{10,... | collective-permute-start | bytes 49160 | tf_op jit(solution)/shard_map/ppermute | solution.py:14
  122.4 1.4 collective-permute-done.37.refs_10_
  123.8 3.8 %collective-permute-done.38.refs_11_ = bf16[64,128]{1,0:T(8,128)(2,1)S(1)} collective-permute-done((bf16[64,128]{1,0:T(8,128)(2,1)S(1)}, bf16[64,128]{1,0:T(8,128)(2,1)S(1)}, u32[]{:S(2)}, u32[]{:S(2)}) %collective-permute-start.38) | collective-permute-done | bytes 16416 | tf_op jit(solution)/shard_map/ppermute | solution.py:14
  127.7 1.4 shard_map.93
  129.2 0.8 collective-permute-start.40
  130.0 3.5 %collective-permute-start.41 = (bf16[64,128]{1,0:T(8,128)(2,1)S(1)}, bf16[64,128]{1,0:T(8,128)(2,1)S(1)}, u32[]{:S(2)}, u32[]{:S(2)}) collective-permute-start(bf16[64,128]{1,0:T(8,128)(2,1)S(1)} %get-tuple-element.99), channel_id=1, source_target_pairs={{0,3},{1,2},{2,1},{3,0},{4,7},{5,6},{6,5},{7,4},{8,11},{9,10},{10,... | collective-permute-start | bytes 49160 | tf_op jit(solution)/shard_map/ppermute | solution.py:14
  133.9 1.6 collective-permute-done.41.refs_10_
  135.5 1.4 shard_map.94
  137.3 3.8 %collective-permute-start.43 = (bf16[64,128]{1,0:T(8,128)(2,1)S(1)}, bf16[64,128]{1,0:T(8,128)(2,1)S(1)}, u32[]{:S(2)}, u32[]{:S(2)}) collective-permute-start(bf16[64,128]{1,0:T(8,128)(2,1)S(1)} %get-tuple-element.104), channel_id=1, source_target_pairs={{0,2},{1,3},{2,0},{3,1},{4,6},{5,7},{6,4},{7,5},{8,10},{9,11},{10,... | collective-permute-start | bytes 49160 | tf_op jit(solution)/shard_map/ppermute | solution.py:14
  141.4 1.5 collective-permute-done.43.refs_10_
  142.9 3.8 %collective-permute-done.44.refs_11_ = bf16[64,128]{1,0:T(8,128)(2,1)S(1)} collective-permute-done((bf16[64,128]{1,0:T(8,128)(2,1)S(1)}, bf16[64,128]{1,0:T(8,128)(2,1)S(1)}, u32[]{:S(2)}, u32[]{:S(2)}) %collective-permute-start.44) | collective-permute-done | bytes 16416 | tf_op jit(solution)/shard_map/ppermute | solution.py:14
  146.6 0.9 shard_map.95
  147.6 0.8 collective-permute-start.46
  148.4 3.5 %collective-permute-start.47 = (bf16[64,128]{1,0:T(8,128)(2,1)S(1)}, bf16[64,128]{1,0:T(8,128)(2,1)S(1)}, u32[]{:S(2)}, u32[]{:S(2)}) collective-permute-start(bf16[64,128]{1,0:T(8,128)(2,1)S(1)} %get-tuple-element.109), channel_id=1, source_target_pairs={{0,3},{1,2},{2,1},{3,0},{4,7},{5,6},{6,5},{7,4},{8,11},{9,10},{10,... | collective-permute-start | bytes 49160 | tf_op jit(solution)/shard_map/ppermute | solution.py:14
  152.3 1.7 collective-permute-done.47.refs_10_
  154.0 0.9 shard_map.96
  155.2 3.8 %collective-permute-start.49 = (bf16[64,128]{1,0:T(8,128)(2,1)S(1)}, bf16[64,128]{1,0:T(8,128)(2,1)S(1)}, u32[]{:S(2)}, u32[]{:S(2)}) collective-permute-start(bf16[64,128]{1,0:T(8,128)(2,1)S(1)} %get-tuple-element.114), channel_id=1, source_target_pairs={{0,2},{1,3},{2,0},{3,1},{4,6},{5,7},{6,4},{7,5},{8,10},{9,11},{10,... | collective-permute-start | bytes 49160 | tf_op jit(solution)/shard_map/ppermute | solution.py:14
  159.3 1.4 collective-permute-done.49.refs_8_
  160.7 3.8 %collective-permute-done.50.refs_9_ = bf16[64,128]{1,0:T(8,128)(2,1)S(1)} collective-permute-done((bf16[64,128]{1,0:T(8,128)(2,1)S(1)}, bf16[64,128]{1,0:T(8,128)(2,1)S(1)}, u32[]{:S(2)}, u32[]{:S(2)}) %collective-permute-start.50) | collective-permute-done | bytes 16416 | tf_op jit(solution)/shard_map/ppermute | solution.py:14
  165.2 0.8 collective-permute-start.52
  166.0 3.5 %collective-permute-start.53 = (f32[64,128]{1,0:T(8,128)S(1)}, f32[64,128]{1,0:T(8,128)S(1)}, u32[]{:S(2)}, u32[]{:S(2)}) collective-permute-start(f32[64,128]{1,0:T(8,128)S(1)} %shard_map.97), channel_id=1, source_target_pairs={{0,3},{1,2},{2,1},{3,0},{4,7},{5,6},{6,5},{7,4},{8,11},{9,10},{10,... | collective-permute-start | bytes 98312 | tf_op jit(solution)/shard_map/ppermute | solution.py:14
  170.1 1.7 collective-permute-done.53
  171.9 8.7 %all_to_all.5 = f32[8,32,128]{2,1,0:T(8,128)S(1)} all-to-all(f32[8,32,128]{2,1,0:T(8,128)S(1)} %bitcast.109), channel_id=1, replica_groups=mesh['row'=8,'col'=4] {'row'}, dimensions={0} | all-to-all | bytes 262144 | tf_op jit(solution)/shard_map/all_to_all | solution.py:340
  (106 shorter events, 14.1 us)
Async XLA Ops:
  2.1 12.8 %collective-permute-start = (f32[8,256]{1,0:T(8,128)S(1)}, f32[8,256]{1,0:T(8,128)S(1)}, u32[]{:S(2)}, u32[]{:S(2)}) collective-permute-start(f32[8,256]{1,0:T(8,128)S(1)} %get-tuple-element.129), channel_id=1, source_target_pairs={{0,8},{4,12},{8,0},{12,4},{16,24},{20,28},{24,16},{28,20},{1,9},{5... | collective-permute-start | bytes 24584 | tf_op jit(solution)/shard_map/ppermute | solution.py:14
  5.1 10.4 %collective-permute-start.1 = (f32[8,256]{1,0:T(8,128)S(1)}, f32[8,256]{1,0:T(8,128)S(1)}, u32[]{:S(2)}, u32[]{:S(2)}) collective-permute-start(f32[8,256]{1,0:T(8,128)S(1)} %get-tuple-element.129), channel_id=1, source_target_pairs={{0,16},{4,20},{8,24},{12,28},{16,0},{20,4},{24,8},{28,12},{1,17},{... | collective-permute-start | bytes 24584 | tf_op jit(solution)/shard_map/ppermute | solution.py:14
  6.6 9.0 %collective-permute-start.2 = (f32[8,256]{1,0:T(8,128)S(1)}, f32[8,256]{1,0:T(8,128)S(1)}, u32[]{:S(2)}, u32[]{:S(2)}) collective-permute-start(f32[8,256]{1,0:T(8,128)S(1)} %get-tuple-element.129), channel_id=1, source_target_pairs={{0,24},{4,28},{8,16},{12,20},{16,8},{20,12},{24,0},{28,4},{1,25},{... | collective-permute-start | bytes 24584 | tf_op jit(solution)/shard_map/ppermute | solution.py:14
  7.9 25.8 %collective-permute-start.6 = (bf16[4,4,128,128]{3,2,1,0:T(8,128)(2,1)S(1)}, bf16[4,4,128,128]{3,2,1,0:T(8,128)(2,1)S(1)}, u32[]{:S(2)}, u32[]{:S(2)}) collective-permute-start(bf16[4,4,128,128]{3,2,1,0:T(8,128)(2,1)S(1)} %get-tuple-element.122.refs_3_), channel_id=1, source_target_pairs={{0,16},{4,20},{8,24},{12,28},{16,0},{20,4},{24,8},{28,12},{1,17},{... | collective-permute-start | bytes 1572872 | tf_op jit(solution)/shard_map/ppermute | solution.py:14
  9.9 24.3 %collective-permute-start.12 = (bf16[4,4,128,128]{3,2,1,0:T(8,128)(2,1)S(1)}, bf16[4,4,128,128]{3,2,1,0:T(8,128)(2,1)S(1)}, u32[]{:S(2)}, u32[]{:S(2)}) collective-permute-start(bf16[4,4,128,128]{3,2,1,0:T(8,128)(2,1)S(1)} %get-tuple-element.122.refs_3_), channel_id=1, source_target_pairs={{0,8},{4,12},{8,0},{12,4},{16,24},{20,28},{24,16},{28,20},{1,9},{5... | collective-permute-start | bytes 1572872 | tf_op jit(solution)/shard_map/ppermute | solution.py:14
  14.9 18.8 %collective-permute-start.4 = (bf16[4,4,128,128]{3,2,1,0:T(8,128)(2,1)S(1)}, bf16[4,4,128,128]{3,2,1,0:T(8,128)(2,1)S(1)}, u32[]{:S(2)}, u32[]{:S(2)}) collective-permute-start(bf16[4,4,128,128]{3,2,1,0:T(8,128)(2,1)S(1)} %get-tuple-element.123.refs_2_), channel_id=1, source_target_pairs={{0,8},{4,12},{8,0},{12,4},{16,24},{20,28},{24,16},{28,20},{1,9},{5... | collective-permute-start | bytes 1572872 | tf_op jit(solution)/shard_map/ppermute | solution.py:14
  15.5 19.2 %collective-permute-start.15 = (bf16[4,4,128,128]{3,2,1,0:T(8,128)(2,1)S(1)}, bf16[4,4,128,128]{3,2,1,0:T(8,128)(2,1)S(1)}, u32[]{:S(2)}, u32[]{:S(2)}) collective-permute-start(bf16[4,4,128,128]{3,2,1,0:T(8,128)(2,1)S(1)} %get-tuple-element.123.refs_2_), channel_id=1, source_target_pairs={{0,16},{4,20},{8,24},{12,28},{16,0},{20,4},{24,8},{28,12},{1,17},{... | collective-permute-start | bytes 1572872 | tf_op jit(solution)/shard_map/ppermute | solution.py:14
  15.6 1.3 collective-permute-start.3
  16.8 21.4 %collective-permute-start.10 = (bf16[4,4,128,128]{3,2,1,0:T(8,128)(2,1)S(1)}, bf16[4,4,128,128]{3,2,1,0:T(8,128)(2,1)}, u32[]{:S(2)}, u32[]{:S(2)}) collective-permute-start(bf16[4,4,128,128]{3,2,1,0:T(8,128)(2,1)S(1)} %get-tuple-element.123.refs_2_), channel_id=1, source_target_pairs={{0,4},{4,0},{8,12},{12,8},{16,20},{20,16},{24,28},{28,24},{1,5},{5... | collective-permute-start | bytes 1572872 | tf_op jit(solution)/shard_map/ppermute | solution.py:14
  33.7 4.7 %collective-permute-start.11 = (bf16[4,4,128,128]{3,2,1,0:T(8,128)(2,1)S(1)}, bf16[4,4,128,128]{3,2,1,0:T(8,128)(2,1)}, u32[]{:S(2)}, u32[]{:S(2)}) collective-permute-start(bf16[4,4,128,128]{3,2,1,0:T(8,128)(2,1)S(1)} %get-tuple-element.122.refs_3_), channel_id=1, source_target_pairs={{0,4},{4,0},{8,12},{12,8},{16,20},{20,16},{24,28},{28,24},{1,5},{5... | collective-permute-start | bytes 1572872 | tf_op jit(solution)/shard_map/ppermute | solution.py:14
  33.7 5.2 %collective-permute-start.13 = (bf16[4,4,128,128]{3,2,1,0:T(8,128)(2,1)S(1)}, bf16[4,4,128,128]{3,2,1,0:T(8,128)(2,1)}, u32[]{:S(2)}, u32[]{:S(2)}) collective-permute-start(bf16[4,4,128,128]{3,2,1,0:T(8,128)(2,1)S(1)} %collective-permute-done.4.refs_6_), channel_id=1, source_target_pairs={{0,4},{4,0},{8,12},{12,8},{16,20},{20,16},{24,28},{28,24},{1,5},{5... | collective-permute-start | bytes 1572872 | tf_op jit(solution)/shard_map/ppermute | solution.py:14
  34.2 14.0 %collective-permute-start.5 = (bf16[4,4,128,128]{3,2,1,0:T(8,128)(2,1)S(1)}, bf16[4,4,128,128]{3,2,1,0:T(8,128)(2,1)}, u32[]{:S(2)}, u32[]{:S(2)}) collective-permute-start(bf16[4,4,128,128]{3,2,1,0:T(8,128)(2,1)S(1)} %collective-permute-done.4.refs_6_), channel_id=1, source_target_pairs={{0,16},{4,20},{8,24},{12,28},{16,0},{20,4},{24,8},{28,12},{1,17},{... | collective-permute-start | bytes 1572872 | tf_op jit(solution)/shard_map/ppermute | solution.py:14
  34.7 13.7 %collective-permute-start.7 = (bf16[4,4,128,128]{3,2,1,0:T(8,128)(2,1)S(1)}, bf16[4,4,128,128]{3,2,1,0:T(8,128)(2,1)}, u32[]{:S(2)}, u32[]{:S(2)}) collective-permute-start(bf16[4,4,128,128]{3,2,1,0:T(8,128)(2,1)S(1)} %collective-permute-done.6.refs_11_), channel_id=1, source_target_pairs={{0,8},{4,12},{8,0},{12,4},{16,24},{20,28},{24,16},{28,20},{1,9},{5... | collective-permute-start | bytes 1572872 | tf_op jit(solution)/shard_map/ppermute | solution.py:14
  38.3 11.1 %collective-permute-start.17 = (bf16[4,4,128,128]{3,2,1,0:T(8,128)(2,1)S(1)}, bf16[4,4,128,128]{3,2,1,0:T(8,128)(2,1)}, u32[]{:S(2)}, u32[]{:S(2)}) collective-permute-start(bf16[4,4,128,128]{3,2,1,0:T(8,128)(2,1)S(1)} %collective-permute-done.6.refs_11_), channel_id=1, source_target_pairs={{0,4},{4,0},{8,12},{12,8},{16,20},{20,16},{24,28},{28,24},{1,5},{5... | collective-permute-start | bytes 1572872 | tf_op jit(solution)/shard_map/ppermute | solution.py:14
  38.4 11.0 %collective-permute-start.14 = (bf16[4,4,128,128]{3,2,1,0:T(8,128)(2,1)S(1)}, bf16[4,4,128,128]{3,2,1,0:T(8,128)(2,1)}, u32[]{:S(2)}, u32[]{:S(2)}) collective-permute-start(bf16[4,4,128,128]{3,2,1,0:T(8,128)(2,1)S(1)} %collective-permute-done.12.refs_7_), channel_id=1, source_target_pairs={{0,4},{4,0},{8,12},{12,8},{16,20},{20,16},{24,28},{28,24},{1,5},{5... | collective-permute-start | bytes 1572872 | tf_op jit(solution)/shard_map/ppermute | solution.py:14
  38.9 10.5 %collective-permute-start.16 = (bf16[4,4,128,128]{3,2,1,0:T(8,128)(2,1)S(1)}, bf16[4,4,128,128]{3,2,1,0:T(8,128)(2,1)}, u32[]{:S(2)}, u32[]{:S(2)}) collective-permute-start(bf16[4,4,128,128]{3,2,1,0:T(8,128)(2,1)S(1)} %collective-permute-done.15.refs_10_), channel_id=1, source_target_pairs={{0,4},{4,0},{8,12},{12,8},{16,20},{20,16},{24,28},{28,24},{1,5},{5... | collective-permute-start | bytes 1572872 | tf_op jit(solution)/shard_map/ppermute | solution.py:14
  48.2 6.0 %collective-permute-start.8 = (bf16[4,4,128,128]{3,2,1,0:T(8,128)(2,1)}, bf16[4,4,128,128]{3,2,1,0:T(8,128)(2,1)}, u32[]{:S(2)}, u32[]{:S(2)}) collective-permute-start(bf16[4,4,128,128]{3,2,1,0:T(8,128)(2,1)} %collective-permute-done.5.refs_2_), channel_id=1, source_target_pairs={{0,4},{4,0},{8,12},{12,8},{16,20},{20,16},{24,28},{28,24},{1,5},{5... | collective-permute-start | bytes 1572872 | tf_op jit(solution)/shard_map/ppermute | solution.py:14
  48.4 5.8 %collective-permute-start.9 = (bf16[4,4,128,128]{3,2,1,0:T(8,128)(2,1)}, bf16[4,4,128,128]{3,2,1,0:T(8,128)(2,1)}, u32[]{:S(2)}, u32[]{:S(2)}) collective-permute-start(bf16[4,4,128,128]{3,2,1,0:T(8,128)(2,1)} %collective-permute-done.7.refs_3_), channel_id=1, source_target_pairs={{0,4},{4,0},{8,12},{12,8},{16,20},{20,16},{24,28},{28,24},{1,5},{5... | collective-permute-start | bytes 1572872 | tf_op jit(solution)/shard_map/ppermute | solution.py:14
  57.7 4.5 %collective-permute-start.18 = (bf16[64,128]{1,0:T(8,128)(2,1)S(1)}, bf16[64,128]{1,0:T(8,128)(2,1)S(1)}, u32[]{:S(2)}, u32[]{:S(2)}) collective-permute-start(bf16[64,128]{1,0:T(8,128)(2,1)S(1)} %get-tuple-element.63), channel_id=1, source_target_pairs={{0,1},{1,0},{2,3},{3,2},{4,5},{5,4},{6,7},{7,6},{8,9},{9,8},{10,11... | collective-permute-start | bytes 49160 | tf_op jit(solution)/shard_map/ppermute | solution.py:14
  59.3 4.7 %collective-permute-start.19 = (bf16[64,128]{1,0:T(8,128)(2,1)S(1)}, bf16[64,128]{1,0:T(8,128)(2,1)S(1)}, u32[]{:S(2)}, u32[]{:S(2)}) collective-permute-start(bf16[64,128]{1,0:T(8,128)(2,1)S(1)} %get-tuple-element.64), channel_id=1, source_target_pairs={{0,2},{1,3},{2,0},{3,1},{4,6},{5,7},{6,4},{7,5},{8,10},{9,11},{10,... | collective-permute-start | bytes 49160 | tf_op jit(solution)/shard_map/ppermute | solution.py:14
  61.9 5.5 %collective-permute-start.20 = (bf16[64,128]{1,0:T(8,128)(2,1)S(1)}, bf16[64,128]{1,0:T(8,128)(2,1)S(1)}, u32[]{:S(2)}, u32[]{:S(2)}) collective-permute-start(bf16[64,128]{1,0:T(8,128)(2,1)S(1)} %get-tuple-element.65), channel_id=1, source_target_pairs={{0,3},{1,2},{2,1},{3,0},{4,7},{5,6},{6,5},{7,4},{8,11},{9,10},{10,... | collective-permute-start | bytes 49160 | tf_op jit(solution)/shard_map/ppermute | solution.py:14
  70.2 4.5 %collective-permute-start.21 = (bf16[64,128]{1,0:T(8,128)(2,1)S(1)}, bf16[64,128]{1,0:T(8,128)(2,1)S(1)}, u32[]{:S(2)}, u32[]{:S(2)}) collective-permute-start(bf16[64,128]{1,0:T(8,128)(2,1)S(1)} %get-tuple-element.67), channel_id=1, source_target_pairs={{0,1},{1,0},{2,3},{3,2},{4,5},{5,4},{6,7},{7,6},{8,9},{9,8},{10,11... | collective-permute-start | bytes 49160 | tf_op jit(solution)/shard_map/ppermute | solution.py:14
  70.3 4.7 %collective-permute-start.22 = (bf16[64,128]{1,0:T(8,128)(2,1)S(1)}, bf16[64,128]{1,0:T(8,128)(2,1)S(1)}, u32[]{:S(2)}, u32[]{:S(2)}) collective-permute-start(bf16[64,128]{1,0:T(8,128)(2,1)S(1)} %get-tuple-element.68), channel_id=1, source_target_pairs={{0,2},{1,3},{2,0},{3,1},{4,6},{5,7},{6,4},{7,5},{8,10},{9,11},{10,... | collective-permute-start | bytes 49160 | tf_op jit(solution)/shard_map/ppermute | solution.py:14
  71.1 5.5 %collective-permute-start.23 = (bf16[64,128]{1,0:T(8,128)(2,1)S(1)}, bf16[64,128]{1,0:T(8,128)(2,1)S(1)}, u32[]{:S(2)}, u32[]{:S(2)}) collective-permute-start(bf16[64,128]{1,0:T(8,128)(2,1)S(1)} %get-tuple-element.69), channel_id=1, source_target_pairs={{0,3},{1,2},{2,1},{3,0},{4,7},{5,6},{6,5},{7,4},{8,11},{9,10},{10,... | collective-permute-start | bytes 49160 | tf_op jit(solution)/shard_map/ppermute | solution.py:14
  77.8 4.5 %collective-permute-start.24 = (bf16[64,128]{1,0:T(8,128)(2,1)S(1)}, bf16[64,128]{1,0:T(8,128)(2,1)S(1)}, u32[]{:S(2)}, u32[]{:S(2)}) collective-permute-start(bf16[64,128]{1,0:T(8,128)(2,1)S(1)} %get-tuple-element.73), channel_id=1, source_target_pairs={{0,1},{1,0},{2,3},{3,2},{4,5},{5,4},{6,7},{7,6},{8,9},{9,8},{10,11... | collective-permute-start | bytes 49160 | tf_op jit(solution)/shard_map/ppermute | solution.py:14
  78.2 5.6 %collective-permute-start.25 = (bf16[64,128]{1,0:T(8,128)(2,1)S(1)}, bf16[64,128]{1,0:T(8,128)(2,1)S(1)}, u32[]{:S(2)}, u32[]{:S(2)}) collective-permute-start(bf16[64,128]{1,0:T(8,128)(2,1)S(1)} %get-tuple-element.74), channel_id=1, source_target_pairs={{0,2},{1,3},{2,0},{3,1},{4,6},{5,7},{6,4},{7,5},{8,10},{9,11},{10,... | collective-permute-start | bytes 49160 | tf_op jit(solution)/shard_map/ppermute | solution.py:14
  82.0 5.5 %collective-permute-start.26 = (bf16[64,128]{1,0:T(8,128)(2,1)S(1)}, bf16[64,128]{1,0:T(8,128)(2,1)S(1)}, u32[]{:S(2)}, u32[]{:S(2)}) collective-permute-start(bf16[64,128]{1,0:T(8,128)(2,1)S(1)} %get-tuple-element.75), channel_id=1, source_target_pairs={{0,3},{1,2},{2,1},{3,0},{4,7},{5,6},{6,5},{7,4},{8,11},{9,10},{10,... | collective-permute-start | bytes 49160 | tf_op jit(solution)/shard_map/ppermute | solution.py:14
  90.1 4.5 %collective-permute-start.27 = (bf16[64,128]{1,0:T(8,128)(2,1)S(1)}, bf16[64,128]{1,0:T(8,128)(2,1)S(1)}, u32[]{:S(2)}, u32[]{:S(2)}) collective-permute-start(bf16[64,128]{1,0:T(8,128)(2,1)S(1)} %get-tuple-element.77), channel_id=1, source_target_pairs={{0,1},{1,0},{2,3},{3,2},{4,5},{5,4},{6,7},{7,6},{8,9},{9,8},{10,11... | collective-permute-start | bytes 49160 | tf_op jit(solution)/shard_map/ppermute | solution.py:14
  90.2 4.7 %collective-permute-start.28 = (bf16[64,128]{1,0:T(8,128)(2,1)S(1)}, bf16[64,128]{1,0:T(8,128)(2,1)S(1)}, u32[]{:S(2)}, u32[]{:S(2)}) collective-permute-start(bf16[64,128]{1,0:T(8,128)(2,1)S(1)} %get-tuple-element.78), channel_id=1, source_target_pairs={{0,2},{1,3},{2,0},{3,1},{4,6},{5,7},{6,4},{7,5},{8,10},{9,11},{10,... | collective-permute-start | bytes 49160 | tf_op jit(solution)/shard_map/ppermute | solution.py:14
  90.9 5.9 %collective-permute-start.29 = (bf16[64,128]{1,0:T(8,128)(2,1)S(1)}, bf16[64,128]{1,0:T(8,128)(2,1)S(1)}, u32[]{:S(2)}, u32[]{:S(2)}) collective-permute-start(bf16[64,128]{1,0:T(8,128)(2,1)S(1)} %get-tuple-element.79), channel_id=1, source_target_pairs={{0,3},{1,2},{2,1},{3,0},{4,7},{5,6},{6,5},{7,4},{8,11},{9,10},{10,... | collective-permute-start | bytes 49160 | tf_op jit(solution)/shard_map/ppermute | solution.py:14
  97.9 4.5 %collective-permute-start.30 = (bf16[64,128]{1,0:T(8,128)(2,1)S(1)}, bf16[64,128]{1,0:T(8,128)(2,1)S(1)}, u32[]{:S(2)}, u32[]{:S(2)}) collective-permute-start(bf16[64,128]{1,0:T(8,128)(2,1)S(1)} %get-tuple-element.83), channel_id=1, source_target_pairs={{0,1},{1,0},{2,3},{3,2},{4,5},{5,4},{6,7},{7,6},{8,9},{9,8},{10,11... | collective-permute-start | bytes 49160 | tf_op jit(solution)/shard_map/ppermute | solution.py:14
  98.3 5.4 %collective-permute-start.31 = (bf16[64,128]{1,0:T(8,128)(2,1)S(1)}, bf16[64,128]{1,0:T(8,128)(2,1)S(1)}, u32[]{:S(2)}, u32[]{:S(2)}) collective-permute-start(bf16[64,128]{1,0:T(8,128)(2,1)S(1)} %get-tuple-element.84), channel_id=1, source_target_pairs={{0,2},{1,3},{2,0},{3,1},{4,6},{5,7},{6,4},{7,5},{8,10},{9,11},{10,... | collective-permute-start | bytes 49160 | tf_op jit(solution)/shard_map/ppermute | solution.py:14
  102.0 5.5 %collective-permute-start.32 = (bf16[64,128]{1,0:T(8,128)(2,1)S(1)}, bf16[64,128]{1,0:T(8,128)(2,1)S(1)}, u32[]{:S(2)}, u32[]{:S(2)}) collective-permute-start(bf16[64,128]{1,0:T(8,128)(2,1)S(1)} %get-tuple-element.85), channel_id=1, source_target_pairs={{0,3},{1,2},{2,1},{3,0},{4,7},{5,6},{6,5},{7,4},{8,11},{9,10},{10,... | collective-permute-start | bytes 49160 | tf_op jit(solution)/shard_map/ppermute | solution.py:14
  109.8 4.5 %collective-permute-start.33 = (bf16[64,128]{1,0:T(8,128)(2,1)S(1)}, bf16[64,128]{1,0:T(8,128)(2,1)S(1)}, u32[]{:S(2)}, u32[]{:S(2)}) collective-permute-start(bf16[64,128]{1,0:T(8,128)(2,1)S(1)} %get-tuple-element.87), channel_id=1, source_target_pairs={{0,1},{1,0},{2,3},{3,2},{4,5},{5,4},{6,7},{7,6},{8,9},{9,8},{10,11... | collective-permute-start | bytes 49160 | tf_op jit(solution)/shard_map/ppermute | solution.py:14
  109.9 4.7 %collective-permute-start.34 = (bf16[64,128]{1,0:T(8,128)(2,1)S(1)}, bf16[64,128]{1,0:T(8,128)(2,1)S(1)}, u32[]{:S(2)}, u32[]{:S(2)}) collective-permute-start(bf16[64,128]{1,0:T(8,128)(2,1)S(1)} %get-tuple-element.88), channel_id=1, source_target_pairs={{0,2},{1,3},{2,0},{3,1},{4,6},{5,7},{6,4},{7,5},{8,10},{9,11},{10,... | collective-permute-start | bytes 49160 | tf_op jit(solution)/shard_map/ppermute | solution.py:14
  110.7 5.5 %collective-permute-start.35 = (bf16[64,128]{1,0:T(8,128)(2,1)S(1)}, bf16[64,128]{1,0:T(8,128)(2,1)S(1)}, u32[]{:S(2)}, u32[]{:S(2)}) collective-permute-start(bf16[64,128]{1,0:T(8,128)(2,1)S(1)} %get-tuple-element.89), channel_id=1, source_target_pairs={{0,3},{1,2},{2,1},{3,0},{4,7},{5,6},{6,5},{7,4},{8,11},{9,10},{10,... | collective-permute-start | bytes 49160 | tf_op jit(solution)/shard_map/ppermute | solution.py:14
  118.0 4.5 %collective-permute-start.36 = (bf16[64,128]{1,0:T(8,128)(2,1)S(1)}, bf16[64,128]{1,0:T(8,128)(2,1)S(1)}, u32[]{:S(2)}, u32[]{:S(2)}) collective-permute-start(bf16[64,128]{1,0:T(8,128)(2,1)S(1)} %get-tuple-element.93), channel_id=1, source_target_pairs={{0,1},{1,0},{2,3},{3,2},{4,5},{5,4},{6,7},{7,6},{8,9},{9,8},{10,11... | collective-permute-start | bytes 49160 | tf_op jit(solution)/shard_map/ppermute | solution.py:14
  118.3 5.6 %collective-permute-start.37 = (bf16[64,128]{1,0:T(8,128)(2,1)S(1)}, bf16[64,128]{1,0:T(8,128)(2,1)S(1)}, u32[]{:S(2)}, u32[]{:S(2)}) collective-permute-start(bf16[64,128]{1,0:T(8,128)(2,1)S(1)} %get-tuple-element.94), channel_id=1, source_target_pairs={{0,2},{1,3},{2,0},{3,1},{4,6},{5,7},{6,4},{7,5},{8,10},{9,11},{10,... | collective-permute-start | bytes 49160 | tf_op jit(solution)/shard_map/ppermute | solution.py:14
  122.1 5.5 %collective-permute-start.38 = (bf16[64,128]{1,0:T(8,128)(2,1)S(1)}, bf16[64,128]{1,0:T(8,128)(2,1)S(1)}, u32[]{:S(2)}, u32[]{:S(2)}) collective-permute-start(bf16[64,128]{1,0:T(8,128)(2,1)S(1)} %get-tuple-element.95), channel_id=1, source_target_pairs={{0,3},{1,2},{2,1},{3,0},{4,7},{5,6},{6,5},{7,4},{8,11},{9,10},{10,... | collective-permute-start | bytes 49160 | tf_op jit(solution)/shard_map/ppermute | solution.py:14
  129.1 4.5 %collective-permute-start.39 = (bf16[64,128]{1,0:T(8,128)(2,1)S(1)}, bf16[64,128]{1,0:T(8,128)(2,1)S(1)}, u32[]{:S(2)}, u32[]{:S(2)}) collective-permute-start(bf16[64,128]{1,0:T(8,128)(2,1)S(1)} %get-tuple-element.97), channel_id=1, source_target_pairs={{0,1},{1,0},{2,3},{3,2},{4,5},{5,4},{6,7},{7,6},{8,9},{9,8},{10,11... | collective-permute-start | bytes 49160 | tf_op jit(solution)/shard_map/ppermute | solution.py:14
  129.2 4.7 %collective-permute-start.40 = (bf16[64,128]{1,0:T(8,128)(2,1)S(1)}, bf16[64,128]{1,0:T(8,128)(2,1)S(1)}, u32[]{:S(2)}, u32[]{:S(2)}) collective-permute-start(bf16[64,128]{1,0:T(8,128)(2,1)S(1)} %get-tuple-element.98), channel_id=1, source_target_pairs={{0,2},{1,3},{2,0},{3,1},{4,6},{5,7},{6,4},{7,5},{8,10},{9,11},{10,... | collective-permute-start | bytes 49160 | tf_op jit(solution)/shard_map/ppermute | solution.py:14
  130.0 5.5 %collective-permute-start.41 = (bf16[64,128]{1,0:T(8,128)(2,1)S(1)}, bf16[64,128]{1,0:T(8,128)(2,1)S(1)}, u32[]{:S(2)}, u32[]{:S(2)}) collective-permute-start(bf16[64,128]{1,0:T(8,128)(2,1)S(1)} %get-tuple-element.99), channel_id=1, source_target_pairs={{0,3},{1,2},{2,1},{3,0},{4,7},{5,6},{6,5},{7,4},{8,11},{9,10},{10,... | collective-permute-start | bytes 49160 | tf_op jit(solution)/shard_map/ppermute | solution.py:14
  136.9 4.5 %collective-permute-start.42 = (bf16[64,128]{1,0:T(8,128)(2,1)S(1)}, bf16[64,128]{1,0:T(8,128)(2,1)S(1)}, u32[]{:S(2)}, u32[]{:S(2)}) collective-permute-start(bf16[64,128]{1,0:T(8,128)(2,1)S(1)} %get-tuple-element.103), channel_id=1, source_target_pairs={{0,1},{1,0},{2,3},{3,2},{4,5},{5,4},{6,7},{7,6},{8,9},{9,8},{10,11... | collective-permute-start | bytes 49160 | tf_op jit(solution)/shard_map/ppermute | solution.py:14
  137.3 5.6 %collective-permute-start.43 = (bf16[64,128]{1,0:T(8,128)(2,1)S(1)}, bf16[64,128]{1,0:T(8,128)(2,1)S(1)}, u32[]{:S(2)}, u32[]{:S(2)}) collective-permute-start(bf16[64,128]{1,0:T(8,128)(2,1)S(1)} %get-tuple-element.104), channel_id=1, source_target_pairs={{0,2},{1,3},{2,0},{3,1},{4,6},{5,7},{6,4},{7,5},{8,10},{9,11},{10,... | collective-permute-start | bytes 49160 | tf_op jit(solution)/shard_map/ppermute | solution.py:14
  141.1 5.5 %collective-permute-start.44 = (bf16[64,128]{1,0:T(8,128)(2,1)S(1)}, bf16[64,128]{1,0:T(8,128)(2,1)S(1)}, u32[]{:S(2)}, u32[]{:S(2)}) collective-permute-start(bf16[64,128]{1,0:T(8,128)(2,1)S(1)} %get-tuple-element.105), channel_id=1, source_target_pairs={{0,3},{1,2},{2,1},{3,0},{4,7},{5,6},{6,5},{7,4},{8,11},{9,10},{10,... | collective-permute-start | bytes 49160 | tf_op jit(solution)/shard_map/ppermute | solution.py:14
  147.5 4.5 %collective-permute-start.45 = (bf16[64,128]{1,0:T(8,128)(2,1)S(1)}, bf16[64,128]{1,0:T(8,128)(2,1)S(1)}, u32[]{:S(2)}, u32[]{:S(2)}) collective-permute-start(bf16[64,128]{1,0:T(8,128)(2,1)S(1)} %get-tuple-element.107), channel_id=1, source_target_pairs={{0,1},{1,0},{2,3},{3,2},{4,5},{5,4},{6,7},{7,6},{8,9},{9,8},{10,11... | collective-permute-start | bytes 49160 | tf_op jit(solution)/shard_map/ppermute | solution.py:14
  147.6 4.7 %collective-permute-start.46 = (bf16[64,128]{1,0:T(8,128)(2,1)S(1)}, bf16[64,128]{1,0:T(8,128)(2,1)S(1)}, u32[]{:S(2)}, u32[]{:S(2)}) collective-permute-start(bf16[64,128]{1,0:T(8,128)(2,1)S(1)} %get-tuple-element.108), channel_id=1, source_target_pairs={{0,2},{1,3},{2,0},{3,1},{4,6},{5,7},{6,4},{7,5},{8,10},{9,11},{10,... | collective-permute-start | bytes 49160 | tf_op jit(solution)/shard_map/ppermute | solution.py:14
  148.4 5.5 %collective-permute-start.47 = (bf16[64,128]{1,0:T(8,128)(2,1)S(1)}, bf16[64,128]{1,0:T(8,128)(2,1)S(1)}, u32[]{:S(2)}, u32[]{:S(2)}) collective-permute-start(bf16[64,128]{1,0:T(8,128)(2,1)S(1)} %get-tuple-element.109), channel_id=1, source_target_pairs={{0,3},{1,2},{2,1},{3,0},{4,7},{5,6},{6,5},{7,4},{8,11},{9,10},{10,... | collective-permute-start | bytes 49160 | tf_op jit(solution)/shard_map/ppermute | solution.py:14
  154.8 4.5 %collective-permute-start.48 = (bf16[64,128]{1,0:T(8,128)(2,1)S(1)}, bf16[64,128]{1,0:T(8,128)(2,1)S(1)}, u32[]{:S(2)}, u32[]{:S(2)}) collective-permute-start(bf16[64,128]{1,0:T(8,128)(2,1)S(1)} %get-tuple-element.113), channel_id=1, source_target_pairs={{0,1},{1,0},{2,3},{3,2},{4,5},{5,4},{6,7},{7,6},{8,9},{9,8},{10,11... | collective-permute-start | bytes 49160 | tf_op jit(solution)/shard_map/ppermute | solution.py:14
  155.2 5.5 %collective-permute-start.49 = (bf16[64,128]{1,0:T(8,128)(2,1)S(1)}, bf16[64,128]{1,0:T(8,128)(2,1)S(1)}, u32[]{:S(2)}, u32[]{:S(2)}) collective-permute-start(bf16[64,128]{1,0:T(8,128)(2,1)S(1)} %get-tuple-element.114), channel_id=1, source_target_pairs={{0,2},{1,3},{2,0},{3,1},{4,6},{5,7},{6,4},{7,5},{8,10},{9,11},{10,... | collective-permute-start | bytes 49160 | tf_op jit(solution)/shard_map/ppermute | solution.py:14
  159.0 5.5 %collective-permute-start.50 = (bf16[64,128]{1,0:T(8,128)(2,1)S(1)}, bf16[64,128]{1,0:T(8,128)(2,1)S(1)}, u32[]{:S(2)}, u32[]{:S(2)}) collective-permute-start(bf16[64,128]{1,0:T(8,128)(2,1)S(1)} %get-tuple-element.115), channel_id=1, source_target_pairs={{0,3},{1,2},{2,1},{3,0},{4,7},{5,6},{6,5},{7,4},{8,11},{9,10},{10,... | collective-permute-start | bytes 49160 | tf_op jit(solution)/shard_map/ppermute | solution.py:14
  165.1 4.5 %collective-permute-start.51 = (f32[64,128]{1,0:T(8,128)S(1)}, f32[64,128]{1,0:T(8,128)S(1)}, u32[]{:S(2)}, u32[]{:S(2)}) collective-permute-start(f32[64,128]{1,0:T(8,128)S(1)} %shard_map.97), channel_id=1, source_target_pairs={{0,1},{1,0},{2,3},{3,2},{4,5},{5,4},{6,7},{7,6},{8,9},{9,8},{10,11... | collective-permute-start | bytes 98312 | tf_op jit(solution)/shard_map/ppermute | solution.py:14
  165.2 4.9 %collective-permute-start.52 = (f32[64,128]{1,0:T(8,128)S(1)}, f32[64,128]{1,0:T(8,128)S(1)}, u32[]{:S(2)}, u32[]{:S(2)}) collective-permute-start(f32[64,128]{1,0:T(8,128)S(1)} %shard_map.97), channel_id=1, source_target_pairs={{0,2},{1,3},{2,0},{3,1},{4,6},{5,7},{6,4},{7,5},{8,10},{9,11},{10,... | collective-permute-start | bytes 98312 | tf_op jit(solution)/shard_map/ppermute | solution.py:14
  166.0 5.8 %collective-permute-start.53 = (f32[64,128]{1,0:T(8,128)S(1)}, f32[64,128]{1,0:T(8,128)S(1)}, u32[]{:S(2)}, u32[]{:S(2)}) collective-permute-start(f32[64,128]{1,0:T(8,128)S(1)} %shard_map.97), channel_id=1, source_target_pairs={{0,3},{1,2},{2,1},{3,0},{4,7},{5,6},{6,5},{7,4},{8,11},{9,10},{10,... | collective-permute-start | bytes 98312 | tf_op jit(solution)/shard_map/ppermute | solution.py:14

commit v5 on v4

--- a/solution.py
+++ b/solution.py
@@ -123,40 +123,39 @@
         refs = list(refs)
         sc = refs.pop(0)
         idx = refs.pop(0)
-        if kind != "last":
-            whole = refs.pop(0)
-            diag = refs.pop(0)
+        whole = refs.pop(0)
+        diag = refs.pop(0)
         level_ref = refs.pop(0)
         pivot_ref = refs.pop(0)
         res_ref = refs.pop(0)
         sol_ref = refs.pop(0) if len(state) > 1 else None
         got = [refs.pop(0) for _ in received]
         if kind == "last":
-            out_sol = refs.pop(0)
+            share, share_sent = refs.pop(0), refs.pop(0)
         else:
             sends = [refs.pop(0) for _ in range(cols)]
             out_state = refs.pop(0)
-            xs, acc = refs
+        xs, acc = refs
         lv = level_ref[...]
         res = res_ref[...]
         if got:
             total = got[0][...]
             for ref in got[1:]:
                 total = total + ref[...].astype(jnp.float32)
-        if kind in ("solved", "last"):
+        if kind == "solved":
             rounded = res.astype(jnp.bfloat16).astype(jnp.float32)
             y = jnp.where(lv == step, total + pivot_ref[...] * rounded, 0.0)
             sol = y if sol_ref is None else sol_ref[...] + y
-            if kind == "last":
-                out_sol[...] = sol
-                return
             out_state[...] = sol
             source = y
-        elif kind == "updated":
+        elif kind in ("updated", "last"):
             back = total.astype(jnp.bfloat16).astype(jnp.float32)
             res = jnp.where(lv > step, res - back, res)
-            out_state[...] = res
             source = jnp.where(lv == step + 1, res, 0.0)
+            if kind == "updated":
+                out_state[...] = res
+            else:
+                done = sol_ref[...] + pivot_ref[...] * source.astype(jnp.bfloat16).astype(jnp.float32)
         else:
             out_state[...] = res
             source = jnp.where(lv == 0, res, 0.0)
@@ -175,7 +174,7 @@
             xs[m, locals_here] = jnp.zeros((lanes, block), jnp.float32)
         acc[...] = jnp.zeros(acc.shape, jnp.float32)
         col = sc[1]
-        which = 3 + 4 * (step + (1 if kind == "updated" else 0)) + (2 if kind == "solved" else 0)
+        which = 3 + 4 * (step + (1 if kind in ("updated", "last") else 0)) + (2 if kind == "solved" else 0)
 
         def contract(x, w):
             return lax.dot_general(
@@ -198,28 +197,37 @@
             return carry
 
         lax.fori_loop(sc[which], sc[which + 1], group, 0)
+        if kind == "last":
+            acc[col] += done.reshape(tile)
+            for cc in range(cols):
+                rows_of = acc[cc].reshape(flat)
+                share[cc] = rows_of
+                share_sent[cc] = rows_of.astype(share_sent.dtype)
+            return
         for d in range(cols):
             sends[d][...] = acc[col ^ d].reshape(flat).astype(sends[d].dtype)
 
     vmem = pl.BlockSpec(memory_space=pltpu.VMEM)
     smem = pl.BlockSpec(memory_space=pltpu.SMEM)
     budget = vmem_budget(operator)
-    args = [scalars, table] + ([] if kind == "last" else list(operator)) + [level, pivot, *state, *received]
+    args = [scalars, table] + list(operator) + [level, pivot, *state, *received]
     if kind == "last":
-        out_shape = jax.ShapeDtypeStruct(flat, jnp.float32)
-        out_specs = vmem
-        scratch = []
+        whole_shape = (cols, *flat)
+        out_shape = [
+            jax.ShapeDtypeStruct(whole_shape, jnp.float32),
+            jax.ShapeDtypeStruct(whole_shape, jnp.bfloat16),
+        ]
     else:
         out_shape = (
             [jax.ShapeDtypeStruct(flat, jnp.float32)]
             + [jax.ShapeDtypeStruct(flat, jnp.bfloat16)] * (cols - 1)
             + [jax.ShapeDtypeStruct(flat, jnp.float32)]
         )
-        out_specs = [vmem] * (cols + 1)
-        scratch = [
-            pltpu.VMEM((groups, locals_here + 1, lanes, block), jnp.float32),
-            pltpu.VMEM((cols, per_row, lanes, block), jnp.float32),
-        ]
+    out_specs = [vmem] * len(out_shape)
+    scratch = [
+        pltpu.VMEM((groups, locals_here + 1, lanes, block), jnp.float32),
+        pltpu.VMEM((cols, per_row, lanes, block), jnp.float32),
+    ]
     return pl.pallas_call(
         body,
         out_shape=out_shape,
@@ -330,11 +338,14 @@
     *sends, res = run("first", 0, state=(res,), received=[])
     for step in range(steps - 1):
         *sends, sol = run("solved", step, state=(res, sol) if step else (res,), received=exchange(sends))
-        *sends, res = run("updated", step, state=(res,), received=exchange(sends))
-    sol = run("last", steps - 1, state=(res, sol), received=exchange(sends))
-
-    whole = jnp.stack(exchange([sol] * cols))
-    whole = flip_order(whole, c)
+        if step + 2 < steps:
+            *sends, res = run("updated", step, state=(res,), received=exchange(sends))
+    share, share_sent = run("last", steps - 2, state=(res, sol), received=exchange(sends))
+
+    mine, *others = exchange([share] + [share_sent] * (cols - 1))
+    whole = mine
+    for other in others:
+        whole = whole + other.astype(jnp.float32)
     whole = whole.reshape(cols, per_row, groups, kept, block).transpose(2, 0, 1, 3, 4)
     whole = whole.reshape(rows, per_row * kept, block)
     got = lax.all_to_all(whole, "row", 0, 0).reshape(rows // 2, 2, per_row, kept, block)

time: 182 us -> 177 us (0.973)
  starting transfers between devices: 65.8 us -> 60.8 us
    ppermute x54 -> x51, starting transfers between devices: 65.8 us -> 60.8 us  [xor_permute(): return lax.ppermute(value, axis, [(i, i ^ distance) for i in range(size)])]
    ppermute x54 -> x51, waiting for transfers between devices: 71.3 us -> 71.9 us  [xor_permute(): return lax.ppermute(value, axis, [(i, i ^ distance) for i in range(size)])]
    pallas_call x12 -> x11, Pallas kernels: 17.4 us -> 16.8 us  [step_kernel(): pl.pallas_call(body, out_shape=out_shape, in_specs=[smem, smem] + [vmem]...]
  transfers between devices with their start and end apart: 54 -> 51, of which waited for: 28 -> 29; matrix products, arithmetic and copies ran while one was open for 4% -> 4% of each run, Pallas kernels for 3% -> 3%
where the time goes in v5:
time: 177 us; the launch traced here: 176 us
  waiting for transfers between devices  71.9 us (41%)
  starting transfers between devices  60.8 us (34%)
  Pallas kernels  24.2 us (14%)
  blocking collectives  8.09 us (5%)
  other arithmetic  6.8 us (4%)
  local copies, waits for them, and re-layouts  3.47 us (2%)
    ppermute x51, waiting for transfers between devices, xor_permute(): return lax.ppermute(value, axis, [(i, i ^ distance) for i in range(size)])  71.9 us
    ppermute x51, starting transfers between devices, xor_permute(): return lax.ppermute(value, axis, [(i, i ^ distance) for i in range(size)])  60.8 us
    pallas_call x11, Pallas kernels, step_kernel(): pl.pallas_call(body, out_shape=out_shape, in_specs=[smem, smem] + [vmem]...  16.8 us
    all_to_all x1, blocking collectives, shards(): lax.all_to_all(whole, 'row', 0, 0)  8.09 us
    pallas_call x2, Pallas kernels, load_blocks(): pl.pallas_call(body, out_shape=shapes, in_specs=[smem] * 2 + [vmem] * len...  7.38 us
  transfers between devices with their start and end apart: 51, of which 29 were waited for; matrix products, arithmetic and copies ran while one was open for 4% of the time, Pallas kernels for 3%

profile of v5, /device:TPU:0, one launch (start us, length us, event | category | flops | bytes accessed | tf_op | source)
XLA Modules:
  0.0 176.3 jit_solution(10823200294298493079)
XLA Ops:
  2.1 3.0 %collective-permute-start.1 = (f32[8,256]{1,0:T(8,128)S(1)}, f32[8,256]{1,0:T(8,128)S(1)}, u32[]{:S(2)}, u32[]{:S(2)}) collective-permute-start(f32[8,256]{1,0:T(8,128)S(1)} %get-tuple-element.123), channel_id=1, source_target_pairs={{0,16},{4,20},{8,24},{12,28},{16,0},{20,4},{24,8},{28,12},{1,17},{... | collective-permute-start | bytes 24584 | tf_op jit(solution)/shard_map/ppermute | solution.py:14
  5.1 1.5 collective-permute-start
  6.6 1.3 fusion.10
  7.9 2.0 %collective-permute-start.12 = (bf16[4,4,128,128]{3,2,1,0:T(8,128)(2,1)S(1)}, bf16[4,4,128,128]{3,2,1,0:T(8,128)(2,1)S(1)}, u32[]{:S(2)}, u32[]{:S(2)}) collective-permute-start(bf16[4,4,128,128]{3,2,1,0:T(8,128)(2,1)S(1)} %get-tuple-element.116.refs_3_), channel_id=1, source_target_pairs={{0,8},{4,12},{8,0},{12,4},{16,24},{20,28},{24,16},{28,20},{1,9},{5... | collective-permute-start | bytes 1572872 | tf_op jit(solution)/shard_map/ppermute | solution.py:14
  9.9 0.8 select_reduce_fusion.6
  11.3 1.1 select_reduce_fusion.3
  12.4 0.8 dynamic-slice_select_fusion
  13.4 1.5 collective-permute-start.6
  15.7 1.1 collective-permute-done.3
  16.9 5.8 %collective-permute-done.12.refs_7_ = bf16[4,4,128,128]{3,2,1,0:T(8,128)(2,1)S(1)} collective-permute-done((bf16[4,4,128,128]{3,2,1,0:T(8,128)(2,1)S(1)}, bf16[4,4,128,128]{3,2,1,0:T(8,128)(2,1)S(1)}, u32[]{:S(2)}, u32[]{:S(2)}) %collective-permute-start.12) | collective-permute-done | bytes 524320 | tf_op jit(solution)/shard_map/ppermute | solution.py:14
  23.2 5.0 %collective-permute-done.6.refs_11_ = bf16[4,4,128,128]{3,2,1,0:T(8,128)(2,1)S(1)} collective-permute-done((bf16[4,4,128,128]{3,2,1,0:T(8,128)(2,1)S(1)}, bf16[4,4,128,128]{3,2,1,0:T(8,128)(2,1)S(1)}, u32[]{:S(2)}, u32[]{:S(2)}) %collective-permute-start.6) | collective-permute-done | bytes 524320 | tf_op jit(solution)/shard_map/ppermute | solution.py:14
  28.3 5.7 %collective-permute-done.4.refs_6_ = bf16[4,4,128,128]{3,2,1,0:T(8,128)(2,1)} collective-permute-done((bf16[4,4,128,128]{3,2,1,0:T(8,128)(2,1)S(1)}, bf16[4,4,128,128]{3,2,1,0:T(8,128)(2,1)}, u32[]{:S(2)}, u32[]{:S(2)}) %collective-permute-start.4) | collective-permute-done | bytes 524320 | tf_op jit(solution)/shard_map/ppermute | solution.py:14
  34.1 1.9 %collective-permute-start.5 = (bf16[4,4,128,128]{3,2,1,0:T(8,128)(2,1)}, bf16[4,4,128,128]{3,2,1,0:T(8,128)(2,1)}, u32[]{:S(2)}, u32[]{:S(2)}) collective-permute-start(bf16[4,4,128,128]{3,2,1,0:T(8,128)(2,1)} %collective-permute-done.4.refs_6_), channel_id=1, source_target_pairs={{0,16},{4,20},{8,24},{12,28},{16,0},{20,4},{24,8},{28,12},{1,17},{... | collective-permute-start | bytes 1572872 | tf_op jit(solution)/shard_map/ppermute | solution.py:14
  36.3 3.2 %collective-permute-done.15.refs_10_ = bf16[4,4,128,128]{3,2,1,0:T(8,128)(2,1)S(1)} collective-permute-done((bf16[4,4,128,128]{3,2,1,0:T(8,128)(2,1)S(1)}, bf16[4,4,128,128]{3,2,1,0:T(8,128)(2,1)S(1)}, u32[]{:S(2)}, u32[]{:S(2)}) %collective-permute-start.15) | collective-permute-done | bytes 524320 | tf_op jit(solution)/shard_map/ppermute | solution.py:14
  40.1 3.6 %collective-permute-done.7.refs_3_ = bf16[4,4,128,128]{3,2,1,0:T(8,128)(2,1)} collective-permute-done((bf16[4,4,128,128]{3,2,1,0:T(8,128)(2,1)S(1)}, bf16[4,4,128,128]{3,2,1,0:T(8,128)(2,1)}, u32[]{:S(2)}, u32[]{:S(2)}) %collective-permute-start.7) | collective-permute-done | bytes 524320 | tf_op jit(solution)/shard_map/ppermute | solution.py:14
  43.7 6.6 %collective-permute-done.5.refs_2_ = bf16[4,4,128,128]{3,2,1,0:T(8,128)(2,1)} collective-permute-done((bf16[4,4,128,128]{3,2,1,0:T(8,128)(2,1)}, bf16[4,4,128,128]{3,2,1,0:T(8,128)(2,1)}, u32[]{:S(2)}, u32[]{:S(2)}) %collective-permute-start.5) | collective-permute-done | bytes 524320 | tf_op jit(solution)/shard_map/ppermute | solution.py:14
  50.4 1.9 %select_reduce_fusion.1 = (s32[8,8,4]{1,2,0:T(4,128)S(1)}, s32[8,8,4]{1,2,0:T(4,128)S(1)}) fusion(s32[64]{0:T(128)} %param.11, s32[8,8,4]{1,2,0:T(4,128)S(1)} %bitcast.102, s32[64]{0:T(128)S(1)} %broadcast_select_fusion), kind=kLoop, calls=%fused_computation.2 | loop fusion | flops 81408 | bytes 3584 | tf_op jit(solution)/shard_map/reduce_sum | solution.py:270
  52.7 4.8 %load_blocks.2.refs_6_ = bf16[8,8,4,128,128]{4,3,2,1,0:T(8,128)(2,1)S(1)} custom-call(s32[27]{0:T(128)S(1)} %pad_add_fusion.1.refs_0_, s32[16]{0:T(128)S(1)} %reshape.339.refs_1_, bf16[4,4,128,128]{3,2,1,0:T(8,128)(2,1)S(1)} %get-tuple-element.117.refs_2_, bf16[4,4,128,128]{3,2,1,0:T(8,128)(2,1)S(1)} %get-tuple-element.116.refs_3_, ...), custom_call_target="tpu_custom_call" | custom-call | tf_op jit(solution)/shard_map/load_blocks/pallas_call | solution.py:91
  57.5 2.6 %load_blocks.3 = (bf16[8,8,4,128,128]{4,3,2,1,0:T(8,128)(2,1)S(1)}, bf16[2,8,128,128]{3,2,1,0:T(8,128)(2,1)S(1)}) custom-call(s32[27]{0:T(128)S(1)} %pad_add_fusion.1.refs_0_, s32[16]{0:T(128)S(1)} %reshape.339.refs_1_, bf16[4,4,128,128]{3,2,1,0:T(8,128)(2,1)} %collective-permute-done.5.refs_2_, ...), custom_call_target="tpu_custom_call", output_to_operand_aliasing={{0}: (6, {})} | custom-call | tf_op jit(solution)/shard_map/load_blocks/pallas_call | solution.py:91
  60.1 0.9 shard_map.86
  61.0 1.6 collective-permute-start.18
  62.6 2.6 %collective-permute-start.19 = (bf16[64,128]{1,0:T(8,128)(2,1)S(1)}, bf16[64,128]{1,0:T(8,128)(2,1)S(1)}, u32[]{:S(2)}, u32[]{:S(2)}) collective-permute-start(bf16[64,128]{1,0:T(8,128)(2,1)S(1)} %get-tuple-element.61), channel_id=1, source_target_pairs={{0,2},{1,3},{2,0},{3,1},{4,6},{5,7},{6,4},{7,5},{8,10},{9,11},{10,... | collective-permute-start | bytes 49160 | tf_op jit(solution)/shard_map/ppermute | solution.py:14
  65.4 1.9 %collective-permute-done.19.refs_9_ = bf16[64,128]{1,0:T(8,128)(2,1)S(1)} collective-permute-done((bf16[64,128]{1,0:T(8,128)(2,1)S(1)}, bf16[64,128]{1,0:T(8,128)(2,1)S(1)}, u32[]{:S(2)}, u32[]{:S(2)}) %collective-permute-start.19) | collective-permute-done | bytes 16416 | tf_op jit(solution)/shard_map/ppermute | solution.py:14
  67.3 3.4 %collective-permute-done.20.refs_10_ = bf16[64,128]{1,0:T(8,128)(2,1)S(1)} collective-permute-done((bf16[64,128]{1,0:T(8,128)(2,1)S(1)}, bf16[64,128]{1,0:T(8,128)(2,1)S(1)}, u32[]{:S(2)}, u32[]{:S(2)}) %collective-permute-start.20) | collective-permute-done | bytes 16416 | tf_op jit(solution)/shard_map/ppermute | solution.py:14
  70.7 2.8 %shard_map.87 = (f32[64,128]{1,0:T(8,128)S(1)}, bf16[64,128]{1,0:T(8,128)(2,1)S(1)}, bf16[64,128]{1,0:T(8,128)(2,1)S(1)}, bf16[64,128]{1,0:T(8,128)(2,1)S(1)}, f32[64,128]{1,0:T(8,128)S(1)}) custom-call(s32[27]{0:T(128)S(1)} %pad_add_fusion.1.refs_0_, s32[256]{0:T(256)S(1)} %reshape.338.refs_14_.refs_1_, ...), custom_call_target="tpu_custom_call" | custom-call | tf_op jit(solution)/shard_map/pallas_call | solution.py:231
  73.6 0.8 collective-permute-start.22
  74.4 3.6 %collective-permute-start.23 = (bf16[64,128]{1,0:T(8,128)(2,1)S(1)}, bf16[64,128]{1,0:T(8,128)(2,1)S(1)}, u32[]{:S(2)}, u32[]{:S(2)}) collective-permute-start(bf16[64,128]{1,0:T(8,128)(2,1)S(1)} %get-tuple-element.66), channel_id=1, source_target_pairs={{0,3},{1,2},{2,1},{3,0},{4,7},{5,6},{6,5},{7,4},{8,11},{9,10},{10,... | collective-permute-start | bytes 49160 | tf_op jit(solution)/shard_map/ppermute | solution.py:14
  78.3 1.6 collective-permute-done.23.refs_10_
  79.9 1.1 shard_map.88
  81.5 3.8 %collective-permute-start.25 = (bf16[64,128]{1,0:T(8,128)(2,1)S(1)}, bf16[64,128]{1,0:T(8,128)(2,1)S(1)}, u32[]{:S(2)}, u32[]{:S(2)}) collective-permute-start(bf16[64,128]{1,0:T(8,128)(2,1)S(1)} %get-tuple-element.71), channel_id=1, source_target_pairs={{0,2},{1,3},{2,0},{3,1},{4,6},{5,7},{6,4},{7,5},{8,10},{9,11},{10,... | collective-permute-start | bytes 49160 | tf_op jit(solution)/shard_map/ppermute | solution.py:14
  85.5 1.5 collective-permute-done.25.refs_10_
  87.0 3.8 %collective-permute-done.26.refs_11_ = bf16[64,128]{1,0:T(8,128)(2,1)S(1)} collective-permute-done((bf16[64,128]{1,0:T(8,128)(2,1)S(1)}, bf16[64,128]{1,0:T(8,128)(2,1)S(1)}, u32[]{:S(2)}, u32[]{:S(2)}) %collective-permute-start.26) | collective-permute-done | bytes 16416 | tf_op jit(solution)/shard_map/ppermute | solution.py:14
  90.8 2.5 %shard_map.89 = (f32[64,128]{1,0:T(8,128)S(1)}, bf16[64,128]{1,0:T(8,128)(2,1)S(1)}, bf16[64,128]{1,0:T(8,128)(2,1)S(1)}, bf16[64,128]{1,0:T(8,128)(2,1)S(1)}, f32[64,128]{1,0:T(8,128)S(1)}) custom-call(s32[27]{0:T(128)S(1)} %pad_add_fusion.1.refs_0_, s32[256]{0:T(256)S(1)} %reshape.338.refs_14_.refs_1_, ...), custom_call_target="tpu_custom_call" | custom-call | tf_op jit(solution)/shard_map/pallas_call | solution.py:231
  94.2 3.6 %collective-permute-start.29 = (bf16[64,128]{1,0:T(8,128)(2,1)S(1)}, bf16[64,128]{1,0:T(8,128)(2,1)S(1)}, u32[]{:S(2)}, u32[]{:S(2)}) collective-permute-start(bf16[64,128]{1,0:T(8,128)(2,1)S(1)} %get-tuple-element.76), channel_id=1, source_target_pairs={{0,3},{1,2},{2,1},{3,0},{4,7},{5,6},{6,5},{7,4},{8,11},{9,10},{10,... | collective-permute-start | bytes 49160 | tf_op jit(solution)/shard_map/ppermute | solution.py:14
  98.1 1.7 collective-permute-done.29.refs_10_
  99.9 1.1 shard_map.90
  101.3 3.8 %collective-permute-start.31 = (bf16[64,128]{1,0:T(8,128)(2,1)S(1)}, bf16[64,128]{1,0:T(8,128)(2,1)S(1)}, u32[]{:S(2)}, u32[]{:S(2)}) collective-permute-start(bf16[64,128]{1,0:T(8,128)(2,1)S(1)} %get-tuple-element.81), channel_id=1, source_target_pairs={{0,2},{1,3},{2,0},{3,1},{4,6},{5,7},{6,4},{7,5},{8,10},{9,11},{10,... | collective-permute-start | bytes 49160 | tf_op jit(solution)/shard_map/ppermute | solution.py:14
  105.5 1.4 collective-permute-done.31.refs_10_
  106.8 3.8 %collective-permute-done.32.refs_11_ = bf16[64,128]{1,0:T(8,128)(2,1)S(1)} collective-permute-done((bf16[64,128]{1,0:T(8,128)(2,1)S(1)}, bf16[64,128]{1,0:T(8,128)(2,1)S(1)}, u32[]{:S(2)}, u32[]{:S(2)}) %collective-permute-start.32) | collective-permute-done | bytes 16416 | tf_op jit(solution)/shard_map/ppermute | solution.py:14
  110.6 2.2 %shard_map.91 = (f32[64,128]{1,0:T(8,128)S(1)}, bf16[64,128]{1,0:T(8,128)(2,1)S(1)}, bf16[64,128]{1,0:T(8,128)(2,1)S(1)}, bf16[64,128]{1,0:T(8,128)(2,1)S(1)}, f32[64,128]{1,0:T(8,128)S(1)}) custom-call(s32[27]{0:T(128)S(1)} %pad_add_fusion.1.refs_0_, s32[256]{0:T(256)S(1)} %reshape.338.refs_14_.refs_1_, ...), custom_call_target="tpu_custom_call" | custom-call | tf_op jit(solution)/shard_map/pallas_call | solution.py:231
  113.0 0.9 collective-permute-start.34
  113.9 3.5 %collective-permute-start.35 = (bf16[64,128]{1,0:T(8,128)(2,1)S(1)}, bf16[64,128]{1,0:T(8,128)(2,1)S(1)}, u32[]{:S(2)}, u32[]{:S(2)}) collective-permute-start(bf16[64,128]{1,0:T(8,128)(2,1)S(1)} %get-tuple-element.86), channel_id=1, source_target_pairs={{0,3},{1,2},{2,1},{3,0},{4,7},{5,6},{6,5},{7,4},{8,11},{9,10},{10,... | collective-permute-start | bytes 49160 | tf_op jit(solution)/shard_map/ppermute | solution.py:14
  117.7 1.7 collective-permute-done.35.refs_10_
  119.4 1.7 shard_map.92
  121.4 3.8 %collective-permute-start.37 = (bf16[64,128]{1,0:T(8,128)(2,1)S(1)}, bf16[64,128]{1,0:T(8,128)(2,1)S(1)}, u32[]{:S(2)}, u32[]{:S(2)}) collective-permute-start(bf16[64,128]{1,0:T(8,128)(2,1)S(1)} %get-tuple-element.91), channel_id=1, source_target_pairs={{0,2},{1,3},{2,0},{3,1},{4,6},{5,7},{6,4},{7,5},{8,10},{9,11},{10,... | collective-permute-start | bytes 49160 | tf_op jit(solution)/shard_map/ppermute | solution.py:14
  125.5 1.4 collective-permute-done.37.refs_10_
  126.9 4.0 %collective-permute-done.38.refs_11_ = bf16[64,128]{1,0:T(8,128)(2,1)S(1)} collective-permute-done((bf16[64,128]{1,0:T(8,128)(2,1)S(1)}, bf16[64,128]{1,0:T(8,128)(2,1)S(1)}, u32[]{:S(2)}, u32[]{:S(2)}) %collective-permute-start.38) | collective-permute-done | bytes 16416 | tf_op jit(solution)/shard_map/ppermute | solution.py:14
  130.9 1.4 shard_map.93
  133.1 3.6 %collective-permute-start.41 = (bf16[64,128]{1,0:T(8,128)(2,1)S(1)}, bf16[64,128]{1,0:T(8,128)(2,1)S(1)}, u32[]{:S(2)}, u32[]{:S(2)}) collective-permute-start(bf16[64,128]{1,0:T(8,128)(2,1)S(1)} %get-tuple-element.96), channel_id=1, source_target_pairs={{0,3},{1,2},{2,1},{3,0},{4,7},{5,6},{6,5},{7,4},{8,11},{9,10},{10,... | collective-permute-start | bytes 49160 | tf_op jit(solution)/shard_map/ppermute | solution.py:14
  137.1 1.6 collective-permute-done.41.refs_10_
  138.7 1.4 shard_map.94
  140.5 3.8 %collective-permute-start.43 = (bf16[64,128]{1,0:T(8,128)(2,1)S(1)}, bf16[64,128]{1,0:T(8,128)(2,1)S(1)}, u32[]{:S(2)}, u32[]{:S(2)}) collective-permute-start(bf16[64,128]{1,0:T(8,128)(2,1)S(1)} %get-tuple-element.101), channel_id=1, source_target_pairs={{0,2},{1,3},{2,0},{3,1},{4,6},{5,7},{6,4},{7,5},{8,10},{9,11},{10,... | collective-permute-start | bytes 49160 | tf_op jit(solution)/shard_map/ppermute | solution.py:14
  144.5 2.2 %collective-permute-done.43.refs_10_ = bf16[64,128]{1,0:T(8,128)(2,1)S(1)} collective-permute-done((bf16[64,128]{1,0:T(8,128)(2,1)S(1)}, bf16[64,128]{1,0:T(8,128)(2,1)S(1)}, u32[]{:S(2)}, u32[]{:S(2)}) %collective-permute-start.43) | collective-permute-done | bytes 16416 | tf_op jit(solution)/shard_map/ppermute | solution.py:14
  146.7 3.1 %collective-permute-done.44.refs_11_ = bf16[64,128]{1,0:T(8,128)(2,1)S(1)} collective-permute-done((bf16[64,128]{1,0:T(8,128)(2,1)S(1)}, bf16[64,128]{1,0:T(8,128)(2,1)S(1)}, u32[]{:S(2)}, u32[]{:S(2)}) %collective-permute-start.44) | collective-permute-done | bytes 16416 | tf_op jit(solution)/shard_map/ppermute | solution.py:14
  149.9 0.9 shard_map.95
  150.8 1.1 collective-permute-start.46
  151.9 3.3 %collective-permute-start.47 = (bf16[64,128]{1,0:T(8,128)(2,1)S(1)}, bf16[64,128]{1,0:T(8,128)(2,1)S(1)}, u32[]{:S(2)}, u32[]{:S(2)}) collective-permute-start(bf16[64,128]{1,0:T(8,128)(2,1)S(1)} %get-tuple-element.107), channel_id=1, source_target_pairs={{0,3},{1,2},{2,1},{3,0},{4,7},{5,6},{6,5},{7,4},{8,11},{9,10},{10,... | collective-permute-start | bytes 49160 | tf_op jit(solution)/shard_map/ppermute | solution.py:14
  155.5 1.9 %collective-permute-done.47.refs_11_ = bf16[64,128]{1,0:T(8,128)(2,1)S(1)} collective-permute-done((bf16[64,128]{1,0:T(8,128)(2,1)S(1)}, bf16[64,128]{1,0:T(8,128)(2,1)S(1)}, u32[]{:S(2)}, u32[]{:S(2)}) %collective-permute-start.47) | collective-permute-done | bytes 16416 | tf_op jit(solution)/shard_map/ppermute | solution.py:14
  157.4 0.9 shard_map.96
  158.3 3.4 %collective-permute-start.50 = (bf16[4,64,128]{2,1,0:T(8,128)(2,1)S(1)}, bf16[4,64,128]{2,1,0:T(8,128)(2,1)S(1)}, u32[]{:S(2)}, u32[]{:S(2)}) collective-permute-start(bf16[4,64,128]{2,1,0:T(8,128)(2,1)S(1)} %get-tuple-element.109), channel_id=1, source_target_pairs={{0,3},{1,2},{2,1},{3,0},{4,7},{5,6},{6,5},{7,4},{8,11},{9,10},{10,... | collective-permute-start | bytes 196616 | tf_op jit(solution)/shard_map/ppermute | solution.py:14
  161.7 1.1 collective-permute-start.48
  162.8 1.7 collective-permute-done.50
  164.4 2.4 %collective-permute-done.49 = bf16[4,64,128]{2,1,0:T(8,128)(2,1)S(1)} collective-permute-done((bf16[4,64,128]{2,1,0:T(8,128)(2,1)S(1)}, bf16[4,64,128]{2,1,0:T(8,128)(2,1)S(1)}, u32[]{:S(2)}, u32[]{:S(2)}) %collective-permute-start.49) | collective-permute-done | bytes 65568 | tf_op jit(solution)/shard_map/ppermute | solution.py:14
  166.9 8.1 %all_to_all.5 = f32[8,32,128]{2,1,0:T(8,128)S(1)} all-to-all(f32[8,32,128]{2,1,0:T(8,128)S(1)} %bitcast.98), channel_id=1, replica_groups=mesh['row'=8,'col'=4] {'row'}, dimensions={0} | all-to-all | bytes 262144 | tf_op jit(solution)/shard_map/all_to_all | solution.py:351
  (97 shorter events, 12.7 us)
Async XLA Ops:
  2.1 11.3 %collective-permute-start.1 = (f32[8,256]{1,0:T(8,128)S(1)}, f32[8,256]{1,0:T(8,128)S(1)}, u32[]{:S(2)}, u32[]{:S(2)}) collective-permute-start(f32[8,256]{1,0:T(8,128)S(1)} %get-tuple-element.123), channel_id=1, source_target_pairs={{0,16},{4,20},{8,24},{12,28},{16,0},{20,4},{24,8},{28,12},{1,17},{... | collective-permute-start | bytes 24584 | tf_op jit(solution)/shard_map/ppermute | solution.py:14
  5.1 9.9 %collective-permute-start = (f32[8,256]{1,0:T(8,128)S(1)}, f32[8,256]{1,0:T(8,128)S(1)}, u32[]{:S(2)}, u32[]{:S(2)}) collective-permute-start(f32[8,256]{1,0:T(8,128)S(1)} %get-tuple-element.123), channel_id=1, source_target_pairs={{0,8},{4,12},{8,0},{12,4},{16,24},{20,28},{24,16},{28,20},{1,9},{5... | collective-permute-start | bytes 24584 | tf_op jit(solution)/shard_map/ppermute | solution.py:14
  6.6 8.9 %collective-permute-start.2 = (f32[8,256]{1,0:T(8,128)S(1)}, f32[8,256]{1,0:T(8,128)S(1)}, u32[]{:S(2)}, u32[]{:S(2)}) collective-permute-start(f32[8,256]{1,0:T(8,128)S(1)} %get-tuple-element.123), channel_id=1, source_target_pairs={{0,24},{4,28},{8,16},{12,20},{16,8},{20,12},{24,0},{28,4},{1,25},{... | collective-permute-start | bytes 24584 | tf_op jit(solution)/shard_map/ppermute | solution.py:14
  7.9 14.9 %collective-permute-start.12 = (bf16[4,4,128,128]{3,2,1,0:T(8,128)(2,1)S(1)}, bf16[4,4,128,128]{3,2,1,0:T(8,128)(2,1)S(1)}, u32[]{:S(2)}, u32[]{:S(2)}) collective-permute-start(bf16[4,4,128,128]{3,2,1,0:T(8,128)(2,1)S(1)} %get-tuple-element.116.refs_3_), channel_id=1, source_target_pairs={{0,8},{4,12},{8,0},{12,4},{16,24},{20,28},{24,16},{28,20},{1,9},{5... | collective-permute-start | bytes 1572872 | tf_op jit(solution)/shard_map/ppermute | solution.py:14
  9.9 12.8 %collective-permute-start.11 = (bf16[4,4,128,128]{3,2,1,0:T(8,128)(2,1)S(1)}, bf16[4,4,128,128]{3,2,1,0:T(8,128)(2,1)S(1)}, u32[]{:S(2)}, u32[]{:S(2)}) collective-permute-start(bf16[4,4,128,128]{3,2,1,0:T(8,128)(2,1)S(1)} %get-tuple-element.116.refs_3_), channel_id=1, source_target_pairs={{0,4},{4,0},{8,12},{12,8},{16,20},{20,16},{24,28},{28,24},{1,5},{5... | collective-permute-start | bytes 1572872 | tf_op jit(solution)/shard_map/ppermute | solution.py:14
  13.4 14.8 %collective-permute-start.6 = (bf16[4,4,128,128]{3,2,1,0:T(8,128)(2,1)S(1)}, bf16[4,4,128,128]{3,2,1,0:T(8,128)(2,1)S(1)}, u32[]{:S(2)}, u32[]{:S(2)}) collective-permute-start(bf16[4,4,128,128]{3,2,1,0:T(8,128)(2,1)S(1)} %get-tuple-element.116.refs_3_), channel_id=1, source_target_pairs={{0,16},{4,20},{8,24},{12,28},{16,0},{20,4},{24,8},{28,12},{1,17},{... | collective-permute-start | bytes 1572872 | tf_op jit(solution)/shard_map/ppermute | solution.py:14
  15.0 24.5 %collective-permute-start.15 = (bf16[4,4,128,128]{3,2,1,0:T(8,128)(2,1)S(1)}, bf16[4,4,128,128]{3,2,1,0:T(8,128)(2,1)S(1)}, u32[]{:S(2)}, u32[]{:S(2)}) collective-permute-start(bf16[4,4,128,128]{3,2,1,0:T(8,128)(2,1)S(1)} %get-tuple-element.117.refs_2_), channel_id=1, source_target_pairs={{0,16},{4,20},{8,24},{12,28},{16,0},{20,4},{24,8},{28,12},{1,17},{... | collective-permute-start | bytes 1572872 | tf_op jit(solution)/shard_map/ppermute | solution.py:14
  15.5 1.3 collective-permute-start.3
  16.7 17.3 %collective-permute-start.4 = (bf16[4,4,128,128]{3,2,1,0:T(8,128)(2,1)S(1)}, bf16[4,4,128,128]{3,2,1,0:T(8,128)(2,1)}, u32[]{:S(2)}, u32[]{:S(2)}) collective-permute-start(bf16[4,4,128,128]{3,2,1,0:T(8,128)(2,1)S(1)} %get-tuple-element.117.refs_2_), channel_id=1, source_target_pairs={{0,8},{4,12},{8,0},{12,4},{16,24},{20,28},{24,16},{28,20},{1,9},{5... | collective-permute-start | bytes 1572872 | tf_op jit(solution)/shard_map/ppermute | solution.py:14
  22.7 16.8 %collective-permute-start.10 = (bf16[4,4,128,128]{3,2,1,0:T(8,128)(2,1)S(1)}, bf16[4,4,128,128]{3,2,1,0:T(8,128)(2,1)}, u32[]{:S(2)}, u32[]{:S(2)}) collective-permute-start(bf16[4,4,128,128]{3,2,1,0:T(8,128)(2,1)S(1)} %get-tuple-element.117.refs_2_), channel_id=1, source_target_pairs={{0,4},{4,0},{8,12},{12,8},{16,20},{20,16},{24,28},{28,24},{1,5},{5... | collective-permute-start | bytes 1572872 | tf_op jit(solution)/shard_map/ppermute | solution.py:14
  22.7 17.3 %collective-permute-start.14 = (bf16[4,4,128,128]{3,2,1,0:T(8,128)(2,1)S(1)}, bf16[4,4,128,128]{3,2,1,0:T(8,128)(2,1)}, u32[]{:S(2)}, u32[]{:S(2)}) collective-permute-start(bf16[4,4,128,128]{3,2,1,0:T(8,128)(2,1)S(1)} %collective-permute-done.12.refs_7_), channel_id=1, source_target_pairs={{0,4},{4,0},{8,12},{12,8},{16,20},{20,16},{24,28},{28,24},{1,5},{5... | collective-permute-start | bytes 1572872 | tf_op jit(solution)/shard_map/ppermute | solution.py:14
  28.2 15.5 %collective-permute-start.7 = (bf16[4,4,128,128]{3,2,1,0:T(8,128)(2,1)S(1)}, bf16[4,4,128,128]{3,2,1,0:T(8,128)(2,1)}, u32[]{:S(2)}, u32[]{:S(2)}) collective-permute-start(bf16[4,4,128,128]{3,2,1,0:T(8,128)(2,1)S(1)} %collective-permute-done.6.refs_11_), channel_id=1, source_target_pairs={{0,8},{4,12},{8,0},{12,4},{16,24},{20,28},{24,16},{28,20},{1,9},{5... | collective-permute-start | bytes 1572872 | tf_op jit(solution)/shard_map/ppermute | solution.py:14
  34.1 16.3 %collective-permute-start.5 = (bf16[4,4,128,128]{3,2,1,0:T(8,128)(2,1)}, bf16[4,4,128,128]{3,2,1,0:T(8,128)(2,1)}, u32[]{:S(2)}, u32[]{:S(2)}) collective-permute-start(bf16[4,4,128,128]{3,2,1,0:T(8,128)(2,1)} %collective-permute-done.4.refs_6_), channel_id=1, source_target_pairs={{0,16},{4,20},{8,24},{12,28},{16,0},{20,4},{24,8},{28,12},{1,17},{... | collective-permute-start | bytes 1572872 | tf_op jit(solution)/shard_map/ppermute | solution.py:14
  39.5 13.2 %collective-permute-start.17 = (bf16[4,4,128,128]{3,2,1,0:T(8,128)(2,1)S(1)}, bf16[4,4,128,128]{3,2,1,0:T(8,128)(2,1)}, u32[]{:S(2)}, u32[]{:S(2)}) collective-permute-start(bf16[4,4,128,128]{3,2,1,0:T(8,128)(2,1)S(1)} %collective-permute-done.6.refs_11_), channel_id=1, source_target_pairs={{0,4},{4,0},{8,12},{12,8},{16,20},{20,16},{24,28},{28,24},{1,5},{5... | collective-permute-start | bytes 1572872 | tf_op jit(solution)/shard_map/ppermute | solution.py:14
  39.5 13.2 %collective-permute-start.13 = (bf16[4,4,128,128]{3,2,1,0:T(8,128)(2,1)}, bf16[4,4,128,128]{3,2,1,0:T(8,128)(2,1)}, u32[]{:S(2)}, u32[]{:S(2)}) collective-permute-start(bf16[4,4,128,128]{3,2,1,0:T(8,128)(2,1)} %collective-permute-done.4.refs_6_), channel_id=1, source_target_pairs={{0,4},{4,0},{8,12},{12,8},{16,20},{20,16},{24,28},{28,24},{1,5},{5... | collective-permute-start | bytes 1572872 | tf_op jit(solution)/shard_map/ppermute | solution.py:14
  40.0 12.7 %collective-permute-start.16 = (bf16[4,4,128,128]{3,2,1,0:T(8,128)(2,1)S(1)}, bf16[4,4,128,128]{3,2,1,0:T(8,128)(2,1)}, u32[]{:S(2)}, u32[]{:S(2)}) collective-permute-start(bf16[4,4,128,128]{3,2,1,0:T(8,128)(2,1)S(1)} %collective-permute-done.15.refs_10_), channel_id=1, source_target_pairs={{0,4},{4,0},{8,12},{12,8},{16,20},{20,16},{24,28},{28,24},{1,5},{5... | collective-permute-start | bytes 1572872 | tf_op jit(solution)/shard_map/ppermute | solution.py:14
  43.7 13.8 %collective-permute-start.9 = (bf16[4,4,128,128]{3,2,1,0:T(8,128)(2,1)}, bf16[4,4,128,128]{3,2,1,0:T(8,128)(2,1)}, u32[]{:S(2)}, u32[]{:S(2)}) collective-permute-start(bf16[4,4,128,128]{3,2,1,0:T(8,128)(2,1)} %collective-permute-done.7.refs_3_), channel_id=1, source_target_pairs={{0,4},{4,0},{8,12},{12,8},{16,20},{20,16},{24,28},{28,24},{1,5},{5... | collective-permute-start | bytes 1572872 | tf_op jit(solution)/shard_map/ppermute | solution.py:14
  50.3 7.2 %collective-permute-start.8 = (bf16[4,4,128,128]{3,2,1,0:T(8,128)(2,1)}, bf16[4,4,128,128]{3,2,1,0:T(8,128)(2,1)}, u32[]{:S(2)}, u32[]{:S(2)}) collective-permute-start(bf16[4,4,128,128]{3,2,1,0:T(8,128)(2,1)} %collective-permute-done.5.refs_2_), channel_id=1, source_target_pairs={{0,4},{4,0},{8,12},{12,8},{16,20},{20,16},{24,28},{28,24},{1,5},{5... | collective-permute-start | bytes 1572872 | tf_op jit(solution)/shard_map/ppermute | solution.py:14
  61.0 4.5 %collective-permute-start.18 = (bf16[64,128]{1,0:T(8,128)(2,1)S(1)}, bf16[64,128]{1,0:T(8,128)(2,1)S(1)}, u32[]{:S(2)}, u32[]{:S(2)}) collective-permute-start(bf16[64,128]{1,0:T(8,128)(2,1)S(1)} %get-tuple-element.60), channel_id=1, source_target_pairs={{0,1},{1,0},{2,3},{3,2},{4,5},{5,4},{6,7},{7,6},{8,9},{9,8},{10,11... | collective-permute-start | bytes 49160 | tf_op jit(solution)/shard_map/ppermute | solution.py:14
  62.6 4.7 %collective-permute-start.19 = (bf16[64,128]{1,0:T(8,128)(2,1)S(1)}, bf16[64,128]{1,0:T(8,128)(2,1)S(1)}, u32[]{:S(2)}, u32[]{:S(2)}) collective-permute-start(bf16[64,128]{1,0:T(8,128)(2,1)S(1)} %get-tuple-element.61), channel_id=1, source_target_pairs={{0,2},{1,3},{2,0},{3,1},{4,6},{5,7},{6,4},{7,5},{8,10},{9,11},{10,... | collective-permute-start | bytes 49160 | tf_op jit(solution)/shard_map/ppermute | solution.py:14
  65.2 5.5 %collective-permute-start.20 = (bf16[64,128]{1,0:T(8,128)(2,1)S(1)}, bf16[64,128]{1,0:T(8,128)(2,1)S(1)}, u32[]{:S(2)}, u32[]{:S(2)}) collective-permute-start(bf16[64,128]{1,0:T(8,128)(2,1)S(1)} %get-tuple-element.62), channel_id=1, source_target_pairs={{0,3},{1,2},{2,1},{3,0},{4,7},{5,6},{6,5},{7,4},{8,11},{9,10},{10,... | collective-permute-start | bytes 49160 | tf_op jit(solution)/shard_map/ppermute | solution.py:14
  73.5 4.5 %collective-permute-start.21 = (bf16[64,128]{1,0:T(8,128)(2,1)S(1)}, bf16[64,128]{1,0:T(8,128)(2,1)S(1)}, u32[]{:S(2)}, u32[]{:S(2)}) collective-permute-start(bf16[64,128]{1,0:T(8,128)(2,1)S(1)} %get-tuple-element.64), channel_id=1, source_target_pairs={{0,1},{1,0},{2,3},{3,2},{4,5},{5,4},{6,7},{7,6},{8,9},{9,8},{10,11... | collective-permute-start | bytes 49160 | tf_op jit(solution)/shard_map/ppermute | solution.py:14
  73.6 4.7 %collective-permute-start.22 = (bf16[64,128]{1,0:T(8,128)(2,1)S(1)}, bf16[64,128]{1,0:T(8,128)(2,1)S(1)}, u32[]{:S(2)}, u32[]{:S(2)}) collective-permute-start(bf16[64,128]{1,0:T(8,128)(2,1)S(1)} %get-tuple-element.65), channel_id=1, source_target_pairs={{0,2},{1,3},{2,0},{3,1},{4,6},{5,7},{6,4},{7,5},{8,10},{9,11},{10,... | collective-permute-start | bytes 49160 | tf_op jit(solution)/shard_map/ppermute | solution.py:14
  74.4 5.5 %collective-permute-start.23 = (bf16[64,128]{1,0:T(8,128)(2,1)S(1)}, bf16[64,128]{1,0:T(8,128)(2,1)S(1)}, u32[]{:S(2)}, u32[]{:S(2)}) collective-permute-start(bf16[64,128]{1,0:T(8,128)(2,1)S(1)} %get-tuple-element.66), channel_id=1, source_target_pairs={{0,3},{1,2},{2,1},{3,0},{4,7},{5,6},{6,5},{7,4},{8,11},{9,10},{10,... | collective-permute-start | bytes 49160 | tf_op jit(solution)/shard_map/ppermute | solution.py:14
  81.0 4.5 %collective-permute-start.24 = (bf16[64,128]{1,0:T(8,128)(2,1)S(1)}, bf16[64,128]{1,0:T(8,128)(2,1)S(1)}, u32[]{:S(2)}, u32[]{:S(2)}) collective-permute-start(bf16[64,128]{1,0:T(8,128)(2,1)S(1)} %get-tuple-element.70), channel_id=1, source_target_pairs={{0,1},{1,0},{2,3},{3,2},{4,5},{5,4},{6,7},{7,6},{8,9},{9,8},{10,11... | collective-permute-start | bytes 49160 | tf_op jit(solution)/shard_map/ppermute | solution.py:14
  81.5 5.6 %collective-permute-start.25 = (bf16[64,128]{1,0:T(8,128)(2,1)S(1)}, bf16[64,128]{1,0:T(8,128)(2,1)S(1)}, u32[]{:S(2)}, u32[]{:S(2)}) collective-permute-start(bf16[64,128]{1,0:T(8,128)(2,1)S(1)} %get-tuple-element.71), channel_id=1, source_target_pairs={{0,2},{1,3},{2,0},{3,1},{4,6},{5,7},{6,4},{7,5},{8,10},{9,11},{10,... | collective-permute-start | bytes 49160 | tf_op jit(solution)/shard_map/ppermute | solution.py:14
  85.3 5.5 %collective-permute-start.26 = (bf16[64,128]{1,0:T(8,128)(2,1)S(1)}, bf16[64,128]{1,0:T(8,128)(2,1)S(1)}, u32[]{:S(2)}, u32[]{:S(2)}) collective-permute-start(bf16[64,128]{1,0:T(8,128)(2,1)S(1)} %get-tuple-element.72), channel_id=1, source_target_pairs={{0,3},{1,2},{2,1},{3,0},{4,7},{5,6},{6,5},{7,4},{8,11},{9,10},{10,... | collective-permute-start | bytes 49160 | tf_op jit(solution)/shard_map/ppermute | solution.py:14
  93.3 4.5 %collective-permute-start.27 = (bf16[64,128]{1,0:T(8,128)(2,1)S(1)}, bf16[64,128]{1,0:T(8,128)(2,1)S(1)}, u32[]{:S(2)}, u32[]{:S(2)}) collective-permute-start(bf16[64,128]{1,0:T(8,128)(2,1)S(1)} %get-tuple-element.74), channel_id=1, source_target_pairs={{0,1},{1,0},{2,3},{3,2},{4,5},{5,4},{6,7},{7,6},{8,9},{9,8},{10,11... | collective-permute-start | bytes 49160 | tf_op jit(solution)/shard_map/ppermute | solution.py:14
  93.4 4.7 %collective-permute-start.28 = (bf16[64,128]{1,0:T(8,128)(2,1)S(1)}, bf16[64,128]{1,0:T(8,128)(2,1)S(1)}, u32[]{:S(2)}, u32[]{:S(2)}) collective-permute-start(bf16[64,128]{1,0:T(8,128)(2,1)S(1)} %get-tuple-element.75), channel_id=1, source_target_pairs={{0,2},{1,3},{2,0},{3,1},{4,6},{5,7},{6,4},{7,5},{8,10},{9,11},{10,... | collective-permute-start | bytes 49160 | tf_op jit(solution)/shard_map/ppermute | solution.py:14
  94.2 5.7 %collective-permute-start.29 = (bf16[64,128]{1,0:T(8,128)(2,1)S(1)}, bf16[64,128]{1,0:T(8,128)(2,1)S(1)}, u32[]{:S(2)}, u32[]{:S(2)}) collective-permute-start(bf16[64,128]{1,0:T(8,128)(2,1)S(1)} %get-tuple-element.76), channel_id=1, source_target_pairs={{0,3},{1,2},{2,1},{3,0},{4,7},{5,6},{6,5},{7,4},{8,11},{9,10},{10,... | collective-permute-start | bytes 49160 | tf_op jit(solution)/shard_map/ppermute | solution.py:14
  101.0 4.5 %collective-permute-start.30 = (bf16[64,128]{1,0:T(8,128)(2,1)S(1)}, bf16[64,128]{1,0:T(8,128)(2,1)S(1)}, u32[]{:S(2)}, u32[]{:S(2)}) collective-permute-start(bf16[64,128]{1,0:T(8,128)(2,1)S(1)} %get-tuple-element.80), channel_id=1, source_target_pairs={{0,1},{1,0},{2,3},{3,2},{4,5},{5,4},{6,7},{7,6},{8,9},{9,8},{10,11... | collective-permute-start | bytes 49160 | tf_op jit(solution)/shard_map/ppermute | solution.py:14
  101.3 5.5 %collective-permute-start.31 = (bf16[64,128]{1,0:T(8,128)(2,1)S(1)}, bf16[64,128]{1,0:T(8,128)(2,1)S(1)}, u32[]{:S(2)}, u32[]{:S(2)}) collective-permute-start(bf16[64,128]{1,0:T(8,128)(2,1)S(1)} %get-tuple-element.81), channel_id=1, source_target_pairs={{0,2},{1,3},{2,0},{3,1},{4,6},{5,7},{6,4},{7,5},{8,10},{9,11},{10,... | collective-permute-start | bytes 49160 | tf_op jit(solution)/shard_map/ppermute | solution.py:14
  105.1 5.5 %collective-permute-start.32 = (bf16[64,128]{1,0:T(8,128)(2,1)S(1)}, bf16[64,128]{1,0:T(8,128)(2,1)S(1)}, u32[]{:S(2)}, u32[]{:S(2)}) collective-permute-start(bf16[64,128]{1,0:T(8,128)(2,1)S(1)} %get-tuple-element.82), channel_id=1, source_target_pairs={{0,3},{1,2},{2,1},{3,0},{4,7},{5,6},{6,5},{7,4},{8,11},{9,10},{10,... | collective-permute-start | bytes 49160 | tf_op jit(solution)/shard_map/ppermute | solution.py:14
  112.9 4.5 %collective-permute-start.33 = (bf16[64,128]{1,0:T(8,128)(2,1)S(1)}, bf16[64,128]{1,0:T(8,128)(2,1)S(1)}, u32[]{:S(2)}, u32[]{:S(2)}) collective-permute-start(bf16[64,128]{1,0:T(8,128)(2,1)S(1)} %get-tuple-element.84), channel_id=1, source_target_pairs={{0,1},{1,0},{2,3},{3,2},{4,5},{5,4},{6,7},{7,6},{8,9},{9,8},{10,11... | collective-permute-start | bytes 49160 | tf_op jit(solution)/shard_map/ppermute | solution.py:14
  113.0 4.7 %collective-permute-start.34 = (bf16[64,128]{1,0:T(8,128)(2,1)S(1)}, bf16[64,128]{1,0:T(8,128)(2,1)S(1)}, u32[]{:S(2)}, u32[]{:S(2)}) collective-permute-start(bf16[64,128]{1,0:T(8,128)(2,1)S(1)} %get-tuple-element.85), channel_id=1, source_target_pairs={{0,2},{1,3},{2,0},{3,1},{4,6},{5,7},{6,4},{7,5},{8,10},{9,11},{10,... | collective-permute-start | bytes 49160 | tf_op jit(solution)/shard_map/ppermute | solution.py:14
  113.9 5.5 %collective-permute-start.35 = (bf16[64,128]{1,0:T(8,128)(2,1)S(1)}, bf16[64,128]{1,0:T(8,128)(2,1)S(1)}, u32[]{:S(2)}, u32[]{:S(2)}) collective-permute-start(bf16[64,128]{1,0:T(8,128)(2,1)S(1)} %get-tuple-element.86), channel_id=1, source_target_pairs={{0,3},{1,2},{2,1},{3,0},{4,7},{5,6},{6,5},{7,4},{8,11},{9,10},{10,... | collective-permute-start | bytes 49160 | tf_op jit(solution)/shard_map/ppermute | solution.py:14
  121.1 4.5 %collective-permute-start.36 = (bf16[64,128]{1,0:T(8,128)(2,1)S(1)}, bf16[64,128]{1,0:T(8,128)(2,1)S(1)}, u32[]{:S(2)}, u32[]{:S(2)}) collective-permute-start(bf16[64,128]{1,0:T(8,128)(2,1)S(1)} %get-tuple-element.90), channel_id=1, source_target_pairs={{0,1},{1,0},{2,3},{3,2},{4,5},{5,4},{6,7},{7,6},{8,9},{9,8},{10,11... | collective-permute-start | bytes 49160 | tf_op jit(solution)/shard_map/ppermute | solution.py:14
  121.4 5.5 %collective-permute-start.37 = (bf16[64,128]{1,0:T(8,128)(2,1)S(1)}, bf16[64,128]{1,0:T(8,128)(2,1)S(1)}, u32[]{:S(2)}, u32[]{:S(2)}) collective-permute-start(bf16[64,128]{1,0:T(8,128)(2,1)S(1)} %get-tuple-element.91), channel_id=1, source_target_pairs={{0,2},{1,3},{2,0},{3,1},{4,6},{5,7},{6,4},{7,5},{8,10},{9,11},{10,... | collective-permute-start | bytes 49160 | tf_op jit(solution)/shard_map/ppermute | solution.py:14
  125.2 5.7 %collective-permute-start.38 = (bf16[64,128]{1,0:T(8,128)(2,1)S(1)}, bf16[64,128]{1,0:T(8,128)(2,1)S(1)}, u32[]{:S(2)}, u32[]{:S(2)}) collective-permute-start(bf16[64,128]{1,0:T(8,128)(2,1)S(1)} %get-tuple-element.92), channel_id=1, source_target_pairs={{0,3},{1,2},{2,1},{3,0},{4,7},{5,6},{6,5},{7,4},{8,11},{9,10},{10,... | collective-permute-start | bytes 49160 | tf_op jit(solution)/shard_map/ppermute | solution.py:14
  132.3 4.5 %collective-permute-start.39 = (bf16[64,128]{1,0:T(8,128)(2,1)S(1)}, bf16[64,128]{1,0:T(8,128)(2,1)S(1)}, u32[]{:S(2)}, u32[]{:S(2)}) collective-permute-start(bf16[64,128]{1,0:T(8,128)(2,1)S(1)} %get-tuple-element.94), channel_id=1, source_target_pairs={{0,1},{1,0},{2,3},{3,2},{4,5},{5,4},{6,7},{7,6},{8,9},{9,8},{10,11... | collective-permute-start | bytes 49160 | tf_op jit(solution)/shard_map/ppermute | solution.py:14
  132.4 4.7 %collective-permute-start.40 = (bf16[64,128]{1,0:T(8,128)(2,1)S(1)}, bf16[64,128]{1,0:T(8,128)(2,1)S(1)}, u32[]{:S(2)}, u32[]{:S(2)}) collective-permute-start(bf16[64,128]{1,0:T(8,128)(2,1)S(1)} %get-tuple-element.95), channel_id=1, source_target_pairs={{0,2},{1,3},{2,0},{3,1},{4,6},{5,7},{6,4},{7,5},{8,10},{9,11},{10,... | collective-permute-start | bytes 49160 | tf_op jit(solution)/shard_map/ppermute | solution.py:14
  133.1 5.6 %collective-permute-start.41 = (bf16[64,128]{1,0:T(8,128)(2,1)S(1)}, bf16[64,128]{1,0:T(8,128)(2,1)S(1)}, u32[]{:S(2)}, u32[]{:S(2)}) collective-permute-start(bf16[64,128]{1,0:T(8,128)(2,1)S(1)} %get-tuple-element.96), channel_id=1, source_target_pairs={{0,3},{1,2},{2,1},{3,0},{4,7},{5,6},{6,5},{7,4},{8,11},{9,10},{10,... | collective-permute-start | bytes 49160 | tf_op jit(solution)/shard_map/ppermute | solution.py:14
  140.1 4.5 %collective-permute-start.42 = (bf16[64,128]{1,0:T(8,128)(2,1)S(1)}, bf16[64,128]{1,0:T(8,128)(2,1)S(1)}, u32[]{:S(2)}, u32[]{:S(2)}) collective-permute-start(bf16[64,128]{1,0:T(8,128)(2,1)S(1)} %get-tuple-element.100), channel_id=1, source_target_pairs={{0,1},{1,0},{2,3},{3,2},{4,5},{5,4},{6,7},{7,6},{8,9},{9,8},{10,11... | collective-permute-start | bytes 49160 | tf_op jit(solution)/shard_map/ppermute | solution.py:14
  140.5 6.2 %collective-permute-start.43 = (bf16[64,128]{1,0:T(8,128)(2,1)S(1)}, bf16[64,128]{1,0:T(8,128)(2,1)S(1)}, u32[]{:S(2)}, u32[]{:S(2)}) collective-permute-start(bf16[64,128]{1,0:T(8,128)(2,1)S(1)} %get-tuple-element.101), channel_id=1, source_target_pairs={{0,2},{1,3},{2,0},{3,1},{4,6},{5,7},{6,4},{7,5},{8,10},{9,11},{10,... | collective-permute-start | bytes 49160 | tf_op jit(solution)/shard_map/ppermute | solution.py:14
  144.3 5.5 %collective-permute-start.44 = (bf16[64,128]{1,0:T(8,128)(2,1)S(1)}, bf16[64,128]{1,0:T(8,128)(2,1)S(1)}, u32[]{:S(2)}, u32[]{:S(2)}) collective-permute-start(bf16[64,128]{1,0:T(8,128)(2,1)S(1)} %get-tuple-element.102), channel_id=1, source_target_pairs={{0,3},{1,2},{2,1},{3,0},{4,7},{5,6},{6,5},{7,4},{8,11},{9,10},{10,... | collective-permute-start | bytes 49160 | tf_op jit(solution)/shard_map/ppermute | solution.py:14
  150.7 4.5 %collective-permute-start.45 = (bf16[64,128]{1,0:T(8,128)(2,1)S(1)}, bf16[64,128]{1,0:T(8,128)(2,1)S(1)}, u32[]{:S(2)}, u32[]{:S(2)}) collective-permute-start(bf16[64,128]{1,0:T(8,128)(2,1)S(1)} %get-tuple-element.105), channel_id=1, source_target_pairs={{0,1},{1,0},{2,3},{3,2},{4,5},{5,4},{6,7},{7,6},{8,9},{9,8},{10,11... | collective-permute-start | bytes 49160 | tf_op jit(solution)/shard_map/ppermute | solution.py:14
  150.8 4.7 %collective-permute-start.46 = (bf16[64,128]{1,0:T(8,128)(2,1)S(1)}, bf16[64,128]{1,0:T(8,128)(2,1)S(1)}, u32[]{:S(2)}, u32[]{:S(2)}) collective-permute-start(bf16[64,128]{1,0:T(8,128)(2,1)S(1)} %get-tuple-element.106), channel_id=1, source_target_pairs={{0,2},{1,3},{2,0},{3,1},{4,6},{5,7},{6,4},{7,5},{8,10},{9,11},{10,... | collective-permute-start | bytes 49160 | tf_op jit(solution)/shard_map/ppermute | solution.py:14
  151.9 5.5 %collective-permute-start.47 = (bf16[64,128]{1,0:T(8,128)(2,1)S(1)}, bf16[64,128]{1,0:T(8,128)(2,1)S(1)}, u32[]{:S(2)}, u32[]{:S(2)}) collective-permute-start(bf16[64,128]{1,0:T(8,128)(2,1)S(1)} %get-tuple-element.107), channel_id=1, source_target_pairs={{0,3},{1,2},{2,1},{3,0},{4,7},{5,6},{6,5},{7,4},{8,11},{9,10},{10,... | collective-permute-start | bytes 49160 | tf_op jit(solution)/shard_map/ppermute | solution.py:14
  158.3 6.1 %collective-permute-start.50 = (bf16[4,64,128]{2,1,0:T(8,128)(2,1)S(1)}, bf16[4,64,128]{2,1,0:T(8,128)(2,1)S(1)}, u32[]{:S(2)}, u32[]{:S(2)}) collective-permute-start(bf16[4,64,128]{2,1,0:T(8,128)(2,1)S(1)} %get-tuple-element.109), channel_id=1, source_target_pairs={{0,3},{1,2},{2,1},{3,0},{4,7},{5,6},{6,5},{7,4},{8,11},{9,10},{10,... | collective-permute-start | bytes 196616 | tf_op jit(solution)/shard_map/ppermute | solution.py:14
  161.7 5.2 %collective-permute-start.49 = (bf16[4,64,128]{2,1,0:T(8,128)(2,1)S(1)}, bf16[4,64,128]{2,1,0:T(8,128)(2,1)S(1)}, u32[]{:S(2)}, u32[]{:S(2)}) collective-permute-start(bf16[4,64,128]{2,1,0:T(8,128)(2,1)S(1)} %get-tuple-element.109), channel_id=1, source_target_pairs={{0,2},{1,3},{2,0},{3,1},{4,6},{5,7},{6,4},{7,5},{8,10},{9,11},{10,... | collective-permute-start | bytes 196616 | tf_op jit(solution)/shard_map/ppermute | solution.py:14
  161.7 5.2 %collective-permute-start.48 = (bf16[4,64,128]{2,1,0:T(8,128)(2,1)S(1)}, bf16[4,64,128]{2,1,0:T(8,128)(2,1)S(1)}, u32[]{:S(2)}, u32[]{:S(2)}) collective-permute-start(bf16[4,64,128]{2,1,0:T(8,128)(2,1)S(1)} %get-tuple-element.109), channel_id=1, source_target_pairs={{0,1},{1,0},{2,3},{3,2},{4,5},{5,4},{6,7},{7,6},{8,9},{9,8},{10,11... | collective-permute-start | bytes 196616 | tf_op jit(solution)/shard_map/ppermute | solution.py:14
